TPU v7x, 512 devices: a whole 4x8x8 slice. The times are simulated.
512 devices in a mesh: blk: 16 (over y, z_lo), wide: 32 (over x, z_hi, core).
Axes of the slice: x: 4, y: 8, z: 8 (z_hi: 4, z_lo: 2; z = z_hi * 2 + z_lo), core: 2. Of those that a mesh axis runs over, the one named last changes fastest.
Arguments:
- tokens: bfloat16 [24576, 128], P(('blk', 'wide')), may hold values from -11 to 11
- centroids: bfloat16 [131072, 128], P('blk'), may hold values from -7 to 7
- row_ids: int32 [512, 16, 32], P(('blk', 'wide')), may hold values from 0 to 47
- alt_ids: int32 [512, 16, 32], P(('blk', 'wide')), may hold values from 0 to 8191
- counts: int32 [512, 16], P(('blk', 'wide')), may hold values from 1 to 32, as said below
Outputs:
- row_duals: float32 [24576], P(('blk', 'wide'))
- col_duals: float32 [131072], P('blk')
- residuals: float32 [512, 16, 32, 128], P(('blk', 'wide'))
Inputs may be any that keep to these rules, and one draw needn't show every extreme that they name: `row_ids`: slot (d, b, c) names row d * 48 + value. `alt_ids`: slot (d, b, c) names centroid b * 8192 + value. The first counts[d, b] slots of device d toward owner b are live; one owner, the same on every device, gets 32 live slots from every device.
All inputs are finite; a program needn't handle non-finite values.
Results may differ from a plain program's by a relative error of at most 0.0003.
Values may be sent and summed in bfloat16 or wider, within the bound.
No kernel may reach another device: no remote copies, remote signals or barrier semaphores. Data moves between devices by JAX's collectives and lax.ppermute only.
A program may use at most 64 MiB of HBM per device.

v0:
```python
import math

import jax
import jax.numpy as jnp
from jax import lax
from jax.sharding import PartitionSpec as P

score_gain = 3.0


def local(tokens, centroids, row_ids, alt_ids, counts):
    scaling = score_gain / math.sqrt(tokens.shape[1])
    blk_count = lax.axis_size("blk")
    wide_count = lax.axis_size("wide")
    position = lax.axis_index("blk")
    tok_dev = tokens.shape[0]
    slab = centroids.shape[0]
    all_cols = slab * blk_count
    all_rows = tok_dev * blk_count * wide_count
    gathered = lax.all_gather(tokens, "blk", axis=0, tiled=True)
    group_rows = gathered.shape[0]
    block_cols = math.gcd(slab, 1024)
    col_blocks = centroids.reshape(slab // block_cols, block_cols, centroids.shape[1])

    def block_scores(centre_block):
        return (
            jnp.einsum("rd,kd->rk", gathered, centre_block, preferred_element_type=jnp.float32)
            * scaling
        )

    def online_step(carry, centre_block):
        running_peak, running_total = carry
        scores = block_scores(centre_block)
        new_peak = jnp.maximum(running_peak, jnp.max(scores, axis=1))
        new_total = running_total * jnp.exp(running_peak - new_peak) + jnp.sum(
            jnp.exp(scores - new_peak[:, None]), axis=1
        )
        return ((new_peak, new_total), None)

    initial = (
        jnp.full((group_rows,), -jnp.inf, jnp.float32),
        jnp.zeros((group_rows,), jnp.float32),
    )
    (local_peak, local_total), unused = lax.scan(online_step, initial, col_blocks)
    peak_score = lax.pmax(local_peak, "blk")
    totals = lax.psum(local_total * jnp.exp(local_peak - peak_score), "blk")
    row_group = math.log(all_cols) - (peak_score + jnp.log(totals))

    def block_mass(centre_block):
        scores = block_scores(centre_block)
        return jnp.sum(jnp.exp(scores + row_group[:, None]), axis=0)

    partial_mass = lax.map(block_mass, col_blocks).reshape(slab)
    col_duals = math.log(all_rows) - jnp.log(lax.psum(partial_mass, "wide"))
    row_duals = lax.dynamic_slice_in_dim(row_group, position * tok_dev, tok_dev)
    request_rows = row_ids[0]
    request_cols = alt_ids[0]
    capacity = request_rows.shape[1]
    live = (jnp.arange(capacity, dtype=jnp.int32)[None, :] < counts[0][:, None]).astype(jnp.int32)
    source_base = jnp.arange(blk_count, dtype=jnp.int32)[:, None] * tok_dev
    asked_rows = lax.all_to_all(request_rows, "blk", split_axis=0, concat_axis=0, tiled=True)
    asked_cols = lax.all_to_all(request_cols, "blk", split_axis=0, concat_axis=0, tiled=True)
    asked_live = lax.all_to_all(live, "blk", split_axis=0, concat_axis=0, tiled=True)
    rows_index = source_base + asked_rows
    picked = gathered[rows_index].astype(jnp.float32)
    centres = centroids[asked_cols].astype(jnp.float32)
    pair_scores = jnp.sum(picked * centres, axis=-1) * scaling
    picked, centres, weights = (
        picked,
        centres,
        jnp.exp(pair_scores + row_group[rows_index] + col_duals[asked_cols]),
    )
    weights = weights * asked_live.astype(jnp.float32)
    result = weights[..., None] * (picked - centres)
    residuals = lax.all_to_all(result, "blk", split_axis=0, concat_axis=0, tiled=True)
    return (row_duals, col_duals, residuals[None])


def solution(mesh):
    in_specs = (
        P(("blk", "wide"), None),
        P("blk", None),
        P(("blk", "wide"), None, None),
        P(("blk", "wide"), None, None),
        P(("blk", "wide"), None),
    )
    out_specs = (P(("blk", "wide")), P("blk"), P(("blk", "wide"), None, None, None))
    return jax.shard_map(local, mesh=mesh, in_specs=in_specs, out_specs=out_specs, check_vma=False)
```

profile of v0, /device:TPU:8, one launch (start us, length us, event | category | flops | bytes accessed | tf_op | source)
XLA Modules:
  0.0 324.0 jit_solution(13096027828668826560)
XLA Ops:
  0.6 9.4 %all-to-all-start = ((s32[16,1,32]{2,1,0:T(1,128)}), s32[16,1,32]{2,1,0:T(1,128)S(1)}, u32[]{:S(2)}, u32[]{:S(2)}) async-start(s32[16,1,32]{2,1,0:T(1,128)} %bitcast.48), calls=%async_computation | async-start | bytes 16384 | tf_op jit(solution)/shard_map/all_to_all | solution.py:61
  10.0 32.4 %all_gather.3 = bf16[768,128]{1,0:T(8,128)(2,1)S(1)} all-gather(bf16[48,128]{1,0:T(8,128)(2,1)} %param.9), channel_id=1, replica_groups=mesh['blk'=16,'wide'=32] {'blk'}, dimensions={0}, use_global_device_ids=true | all-gather | bytes 208896 | tf_op jit(solution)/shard_map/all_gather | solution.py:20
  42.4 17.3 %while.24 = (s32[]{:T(128)}, f32[768]{0:T(1024)S(1)}, f32[768]{0:T(1024)S(1)}, bf16[8,1024,128]{2,1,0:T(8,128)(2,1)}, bf16[768,128]{1,0:T(8,128)(2,1)S(1)}, /*index=5*/s32[]{:T(128)}, s32[]{:T(128)}) while((s32[]{:T(128)}, f32[768]{0:T(1024)S(1)}, f32[768]{0:T(1024)S(1)}, bf16[8,1024,128]{2,1,0:T(8,128)(2,1)}, ...), condition=%wide.region_3.4_spmd.clone, body=%wide.region_0.3_spmd.clone.sunk | while | flops 205262592 | bytes 6790244 | solution.py:44
  42.4 1.5 multiply_reduce_fusion.2
  44.6 1.5 multiply_reduce_fusion.2
  46.7 1.5 multiply_reduce_fusion.2
  48.9 1.5 multiply_reduce_fusion.2
  51.0 1.5 multiply_reduce_fusion.2
  53.2 1.5 multiply_reduce_fusion.2
  55.4 1.5 multiply_reduce_fusion.2
  57.5 1.5 multiply_reduce_fusion.2
  59.7 30.6 %pmax.7 = f32[768]{0:T(1024)S(1)} all-reduce(f32[768]{0:T(1024)S(1)} %get-tuple-element.58), channel_id=1, replica_groups=mesh['blk'=16,'wide'=32] {'blk'}, use_global_device_ids=true, to_apply=%region_4.5 | all-reduce | flops 768 | bytes 6144 | tf_op jit(solution)/shard_map/pmax | solution.py:45
  90.3 32.6 %psum.14 = f32[768]{0:T(1024)S(1)} all-reduce(f32[768]{0:T(1024)S(1)} %exponential_multiply_fusion), channel_id=1, replica_groups=mesh['blk'=16,'wide'=32] {'blk'}, use_global_device_ids=true, to_apply=%region_5.6 | all-reduce | flops 768 | bytes 6144 | tf_op jit(solution)/shard_map/psum | solution.py:46
  123.0 14.5 %while.23 = (s32[]{:T(128)}, f32[8,1024]{1,0:T(8,128)S(1)}, bf16[8,1024,128]{2,1,0:T(8,128)(2,1)}, bf16[768,128]{1,0:T(8,128)(2,1)S(1)}, f32[768]{0:T(1024)S(1)}, /*index=5*/s32[]{:T(128)}, s32[]{:T(128)}) while((s32[]{:T(128)}, f32[8,1024]{1,0:T(8,128)S(1)}, bf16[8,1024,128]{2,1,0:T(8,128)(2,1)}, bf16[768,128]{1,0:T(8,128)(2,1)S(1)}, ...), condition=%wide.region_8.9_spmd, body=%wide.region_6.8_spmd.sunk | while | flops 203684864 | bytes 474205 | solution.py:53
  123.0 1.7 exponential_reduce_fusion.4
  124.8 1.7 exponential_reduce_fusion.4
  126.6 1.7 exponential_reduce_fusion.4
  128.4 1.7 exponential_reduce_fusion.4
  130.2 1.7 exponential_reduce_fusion.4
  132.0 1.7 exponential_reduce_fusion.4
  133.8 1.7 exponential_reduce_fusion.4
  135.6 1.7 exponential_reduce_fusion.4
  137.5 142.6 %psum.15 = f32[8192]{0:T(1024)S(1)} all-reduce(f32[8192]{0:T(1024)S(1)} %bitcast.42), channel_id=1, replica_groups=mesh['blk'=16,'wide'=32] {'wide'}, use_global_device_ids=true, to_apply=%region_9.10 | all-reduce | flops 8192 | bytes 65536 | tf_op jit(solution)/shard_map/psum | solution.py:54
  280.8 7.3 %all-to-all-start.1 = ((s32[16,1,32]{2,1,0:T(1,128)}), s32[16,1,32]{2,1,0:T(1,128)S(1)}, u32[]{:S(2)}, u32[]{:S(2)}) async-start(s32[16,1,32]{2,1,0:T(1,128)} %bitcast.5), calls=%async_computation.1 | async-start | bytes 16384 | tf_op jit(solution)/shard_map/all_to_all | solution.py:62
  289.6 2.3 gather_fusion.2
  291.9 3.3 %all-to-all-done.1 = s32[16,1,32]{2,1,0:T(1,128)S(1)} async-done(((s32[16,1,32]{2,1,0:T(1,128)}), s32[16,1,32]{2,1,0:T(1,128)S(1)}, u32[]{:S(2)}, u32[]{:S(2)}) %all-to-all-start.1) | async-done | bytes 2080 | tf_op jit(solution)/shard_map/all_to_all | solution.py:62
  295.2 4.9 %all-to-all-start.2 = ((s32[16,1,32]{2,1,0:T(1,128)}), s32[16,1,32]{2,1,0:T(1,128)S(1)}, u32[]{:S(2)}, u32[]{:S(2)}) async-start(s32[16,1,32]{2,1,0:T(1,128)} %compare_convert_fusion), calls=%async_computation.2 | async-start | bytes 16384 | tf_op jit(solution)/shard_map/all_to_all | solution.py:63
  300.2 1.3 gather_fusion.1
  301.5 3.1 gather_fusion.3
  304.9 2.2 all-to-all-done.2
  308.0 5.9 %all-to-all-start.3 = ((f32[16,32,128]{2,1,0:T(8,128)}), f32[16,32,128]{2,1,0:T(8,128)S(1)}, u32[]{:S(2)}, u32[]{:S(2)}) async-start(f32[16,32,128]{2,1,0:T(8,128)} %broadcast_multiply_fusion), calls=%async_computation.3 | async-start | bytes 524288 | tf_op jit(solution)/shard_map/all_to_all | solution.py:75
  314.5 8.8 %all-to-all-done.3 = f32[16,32,128]{2,1,0:T(8,128)S(1)} async-done(((f32[16,32,128]{2,1,0:T(8,128)}), f32[16,32,128]{2,1,0:T(8,128)S(1)}, u32[]{:S(2)}, u32[]{:S(2)}) %all-to-all-start.3) | async-done | bytes 262176 | tf_op jit(solution)/shard_map/all_to_all | solution.py:75
  (71 shorter events, 10.2 us)
Async XLA Ops:
  0.6 280.2 %all-to-all-start = ((s32[16,1,32]{2,1,0:T(1,128)}), s32[16,1,32]{2,1,0:T(1,128)S(1)}, u32[]{:S(2)}, u32[]{:S(2)}) async-start(s32[16,1,32]{2,1,0:T(1,128)} %bitcast.48), calls=%async_computation | async-start | bytes 16384 | tf_op jit(solution)/shard_map/all_to_all | solution.py:61
  123.0 157.2 %copy-start.2 = (s32[1,16]{1,0:T(1,128)S(1)}, s32[1,16]{1,0:T(1,128)}, u32[]{:S(2)}) copy-start(s32[1,16]{1,0:T(1,128)} %param.13) | copy-start | bytes 196
  280.1 21.4 %copy-start = (f32[8192]{0:T(1024)}, f32[8192]{0:T(1024)S(1)}, u32[]{:S(2)}) copy-start(f32[8192]{0:T(1024)S(1)} %log_subtract_fusion) | copy-start | bytes 98308
  280.8 14.4 %all-to-all-start.1 = ((s32[16,1,32]{2,1,0:T(1,128)}), s32[16,1,32]{2,1,0:T(1,128)S(1)}, u32[]{:S(2)}, u32[]{:S(2)}) async-start(s32[16,1,32]{2,1,0:T(1,128)} %bitcast.5), calls=%async_computation.1 | async-start | bytes 16384 | tf_op jit(solution)/shard_map/all_to_all | solution.py:62
  289.6 10.6 %copy-start.1 = (bf16[8,1024,128]{2,1,0:T(8,128)(2,1)S(1)}, bf16[8,1024,128]{2,1,0:T(8,128)(2,1)}, u32[]{:S(2)}) copy-start(bf16[8,1024,128]{2,1,0:T(8,128)(2,1)} %get-tuple-element.221) | copy-start | bytes 6291460
  295.2 12.0 %all-to-all-start.2 = ((s32[16,1,32]{2,1,0:T(1,128)}), s32[16,1,32]{2,1,0:T(1,128)S(1)}, u32[]{:S(2)}, u32[]{:S(2)}) async-start(s32[16,1,32]{2,1,0:T(1,128)} %compare_convert_fusion), calls=%async_computation.2 | async-start | bytes 16384 | tf_op jit(solution)/shard_map/all_to_all | solution.py:63
  308.0 15.3 %all-to-all-start.3 = ((f32[16,32,128]{2,1,0:T(8,128)}), f32[16,32,128]{2,1,0:T(8,128)S(1)}, u32[]{:S(2)}, u32[]{:S(2)}) async-start(f32[16,32,128]{2,1,0:T(8,128)} %broadcast_multiply_fusion), calls=%async_computation.3 | async-start | bytes 524288 | tf_op jit(solution)/shard_map/all_to_all | solution.py:75
where the time goes:
time: 325 us; the launch traced here: 324 us
  blocking collectives  238 us (73%)
  starting transfers between devices  27.5 us (8%)
  matrix products  25.6 us (8%)
  waiting for transfers between devices  14.3 us (4%)
  local copies, waits for them, and re-layouts  10.5 us (3%)
  other arithmetic  6.47 us (2%)
    psum x1, blocking collectives, local(): col_duals = math.log(all_rows) - jnp.log(lax.psum(partial_mass, 'wide'))  143 us
    psum x1, blocking collectives, local(): totals = lax.psum(local_total * jnp.exp(local_peak - peak_score), 'blk')  32.6 us
    all_gather x1, blocking collectives, local(): gathered = lax.all_gather(tokens, 'blk', axis=0, tiled=True)  32.4 us
    pmax x1, blocking collectives, local(): peak_score = lax.pmax(local_peak, 'blk')  30.6 us
    dot_general x16, matrix products, block_scores(): jnp.einsum('rd,kd->rk', gathered, centre_block, preferred_element_type=jn...  25.6 us
    all_to_all x1, starting transfers between devices, local(): lax.all_to_all(request_rows, 'blk', split_axis=0, concat_axis=0, tiled=True)  9.38 us
    all_to_all x1, waiting for transfers between devices, local(): lax.all_to_all(result, 'blk', split_axis=0, concat_axis=0, tiled=True)  8.82 us
    all_to_all x1, starting transfers between devices, local(): lax.all_to_all(request_cols, 'blk', split_axis=0, concat_axis=0, tiled=True)  7.3 us
  transfers between devices with their start and end apart: 4, of which 3 were waited for; matrix products, arithmetic and copies ran while one was open for 13% of the time, Pallas kernels for 0%

commit v1 on v0

v1 whole, which is shorter than its diff:
```python
import math

import jax
import jax.numpy as jnp
from jax import lax
from jax.experimental import pallas as pl
from jax.experimental.pallas import tpu as pltpu
from jax.sharding import PartitionSpec as P

score_gain = 3.0
log2e = 1.4426950408889634
dead = -1.0e30


def vmem(n):
    return [pl.BlockSpec(memory_space=pltpu.VMEM)] * n


def load_rows(x_ref, t_ref, n_blk, tok):
    for i in range(n_blk):
        t_ref[i * tok : (i + 1) * tok, :] = x_ref[i, :tok, :]


def exchange(x, axis):
    return lax.all_to_all(x, axis, split_axis=0, concat_axis=0, tiled=True)


def row_pass(x, centroids, tok, scaling):
    n_blk = x.shape[0]
    rows = n_blk * tok
    slab, width = centroids.shape
    block = 256
    steps = slab // block
    factor = scaling * log2e

    def kernel(x_ref, c_ref, out_ref, t_ref, s_ref, m_ref, a_ref):
        load_rows(x_ref, t_ref, n_blk, tok)

        def scores(j):
            return lax.dot_general(
                c_ref[pl.ds(pl.multiple_of(j * block, block), block), :],
                t_ref[...],
                (((1,), (1,)), ((), ())),
                preferred_element_type=jnp.float32,
            )

        m_ref[...] = jnp.full_like(m_ref, dead)
        a_ref[...] = jnp.zeros_like(a_ref)
        s_ref[0] = scores(0)

        def step(j, carry):
            now = lax.rem(j, 2)
            s_ref[1 - now] = scores(jnp.minimum(j + 1, steps - 1))
            for g in range(rows // 128):
                lanes = slice(g * 128, (g + 1) * 128)
                s = s_ref[now, :, lanes].reshape(block // 8, 8, 128)
                old = m_ref[:, lanes]
                new = jnp.maximum(old, jnp.max(s, axis=0))
                m_ref[:, lanes] = new
                part = jnp.sum(jnp.exp2((s - new[None]) * factor), axis=0)
                a_ref[:, lanes] = a_ref[:, lanes] * jnp.exp2((old - new) * factor) + part
            return carry

        lax.fori_loop(0, steps, step, 0)
        m = m_ref[...]
        top = jnp.max(m, axis=0, keepdims=True)
        total = jnp.sum(a_ref[...] * jnp.exp2((m - top) * factor), axis=0, keepdims=True)
        lse = top * scaling + jnp.log(total)
        for i in range(n_blk):
            out_ref[i] = lse

    return pl.pallas_call(
        kernel,
        out_shape=jax.ShapeDtypeStruct((n_blk, 1, rows), jnp.float32),
        in_specs=vmem(2),
        out_specs=pl.BlockSpec(memory_space=pltpu.VMEM),
        scratch_shapes=[
            pltpu.VMEM((rows, width), jnp.bfloat16),
            pltpu.VMEM((2, block, rows), jnp.float32),
            pltpu.VMEM((8, rows), jnp.float32),
            pltpu.VMEM((8, rows), jnp.float32),
        ],
        compiler_params=pltpu.CompilerParams(vmem_limit_bytes=24 << 20),
        name="row_pass",
    )(x, centroids)


def column_pass(x, centroids, parts, tok, scaling, all_cols, chunks):
    n_blk = x.shape[0]
    rows = n_blk * tok
    slab, width = centroids.shape
    block = slab // chunks
    factor = scaling * log2e

    def kernel(x_ref, c_ref, l_ref, dual_ref, mass_ref, t_ref, d_ref, s_ref):
        load_rows(x_ref, t_ref, n_blk, tok)
        lse = l_ref[:, 0, :]
        top = jnp.max(lse, axis=0, keepdims=True)
        total = jnp.sum(jnp.exp(lse - top), axis=0, keepdims=True)
        dual = math.log(all_cols) - (top + jnp.log(total))
        dual_ref[...] = dual
        d_ref[...] = jnp.transpose(jnp.broadcast_to(dual * log2e, (128, rows)))

        def scores(j):
            return lax.dot_general(
                t_ref[...],
                c_ref[pl.ds(pl.multiple_of(j * block, block), block), :],
                (((1,), (1,)), ((), ())),
                preferred_element_type=jnp.float32,
            )

        s_ref[0] = scores(0)

        def step(j, carry):
            now = lax.rem(j, 2)
            s_ref[1 - now] = scores(jnp.minimum(j + 1, chunks - 1))
            for g in range(block // 128):
                lanes = slice(g * 128, (g + 1) * 128)
                acc = jnp.zeros((8, 128), jnp.float32)
                for r in range(0, rows, 128):
                    s = s_ref[now, r : r + 128, lanes]
                    e = jnp.exp2(s * factor + d_ref[r : r + 128, :])
                    acc = acc + jnp.sum(e.reshape(16, 8, 128), axis=0)
                mass_ref[j, :, lanes] = jnp.sum(acc, axis=0, keepdims=True)
            return carry

        lax.fori_loop(0, chunks, step, 0)

    return pl.pallas_call(
        kernel,
        out_shape=(
            jax.ShapeDtypeStruct((1, rows), jnp.float32),
            jax.ShapeDtypeStruct((chunks, 1, block), jnp.float32),
        ),
        in_specs=vmem(3),
        out_specs=tuple(vmem(2)),
        scratch_shapes=[
            pltpu.VMEM((rows, width), jnp.bfloat16),
            pltpu.VMEM((rows, 128), jnp.float32),
            pltpu.VMEM((2, rows, block), jnp.float32),
        ],
        compiler_params=pltpu.CompilerParams(vmem_limit_bytes=24 << 20),
        name="column_pass",
    )(x, centroids, parts)


def sum_and_copy(parts):
    def kernel(p_ref, out_ref):
        total = jnp.sum(p_ref[:, 0, :], axis=0, keepdims=True)
        for j in range(parts.shape[0]):
            out_ref[j] = total

    return pl.pallas_call(
        kernel,
        out_shape=jax.ShapeDtypeStruct(parts.shape, jnp.float32),
        in_specs=vmem(1),
        out_specs=pl.BlockSpec(memory_space=pltpu.VMEM),
        name="sum_and_copy",
    )(parts)


def look_up(masses, high, low, all_rows, n_blk, capacity):
    chunks, _, block = masses.shape
    lines = chunks * block // 128
    slots = high.shape[1]

    def kernel(m_ref, h_ref, l_ref, dual_ref, out_ref):
        for j in range(chunks):
            for g in range(block // 128):
                k = j * (block // 128) + g
                dual_ref[k : k + 1, :] = m_ref[j, :, g * 128 : (g + 1) * 128]
        dual = math.log(all_rows) - jnp.log(dual_ref[...])
        dual_ref[...] = dual
        line = lax.broadcasted_iota(jnp.int32, (lines, slots), 0)
        pick = jnp.where(line == h_ref[...], 1.0, 0.0).astype(jnp.bfloat16)
        rest = dual
        found = jnp.zeros((128, slots), jnp.float32)
        for _ in range(3):
            piece = rest.astype(jnp.bfloat16)
            rest = rest - piece.astype(jnp.float32)
            found = found + lax.dot_general(
                piece, pick, (((0,), (0,)), ((), ())), preferred_element_type=jnp.float32
            )
        lane = lax.broadcasted_iota(jnp.int32, (128, slots), 0)
        value = jnp.sum(jnp.where(lane == l_ref[...], found, 0.0), axis=0, keepdims=True)
        out_ref[...] = jnp.zeros_like(out_ref)
        for i in range(n_blk):
            out_ref[i, :, :capacity] = value[:, i * capacity : (i + 1) * capacity]

    return pl.pallas_call(
        kernel,
        out_shape=(
            jax.ShapeDtypeStruct((lines, 128), jnp.float32),
            jax.ShapeDtypeStruct((n_blk, 1, 128), jnp.float32),
        ),
        in_specs=vmem(3),
        out_specs=tuple(vmem(2)),
        name="look_up",
    )(masses, high, low)


def prepare(tokens, centres, rows, live, duals, scaling):
    slots, width = rows.shape[0], tokens.shape[1]
    tok = tokens.shape[0]

    def kernel(t_ref, c_ref, r_ref, v_ref, d_ref, diff_ref, exp_ref):
        row = lax.broadcasted_iota(jnp.int32, (slots, tok), 1)
        hit = row == r_ref[...]
        picked = jnp.dot(
            jnp.where(hit, 1.0, 0.0).astype(jnp.bfloat16), t_ref[...], preferred_element_type=jnp.float32
        )
        centre = c_ref[...].astype(jnp.float32)
        diff_ref[...] = picked - centre
        score = jnp.sum(picked * centre, axis=1, keepdims=True) * scaling
        dual = jnp.sum(jnp.where(hit, d_ref[...], 0.0), axis=1, keepdims=True)
        exponent = jnp.where(v_ref[...] > 0, score + dual, dead)
        exp_ref[...] = jnp.broadcast_to(exponent, (slots, width))

    shape = jax.ShapeDtypeStruct((slots, width), jnp.float32)
    return pl.pallas_call(
        kernel,
        out_shape=(shape, shape),
        in_specs=vmem(5),
        out_specs=tuple(vmem(2)),
        name="prepare",
    )(tokens, centres, rows, live, duals)


def finish(duals, diff, exponents, n_blk, capacity):
    width = diff.shape[1]

    def kernel(g_ref, d_ref, e_ref, out_ref):
        turned = jnp.transpose(g_ref[:, 0, :])
        for i in range(n_blk):
            part = slice(i * capacity, (i + 1) * capacity)
            dual = jnp.broadcast_to(turned[:capacity, i : i + 1], (capacity, width))
            e = e_ref[part, :]
            weight = jnp.where(e > 0.1 * dead, jnp.exp(e + dual), 0.0)
            out_ref[0, i] = weight * d_ref[part, :]

    return pl.pallas_call(
        kernel,
        out_shape=jax.ShapeDtypeStruct((1, n_blk, capacity, width), jnp.float32),
        in_specs=vmem(3),
        out_specs=pl.BlockSpec(memory_space=pltpu.VMEM),
        name="finish",
    )(duals, diff, exponents)


def local(tokens, centroids, row_ids, alt_ids, counts):
    tok, width = tokens.shape
    slab = centroids.shape[0]
    n_blk = lax.axis_size("blk")
    n_wide = lax.axis_size("wide")
    position = lax.axis_index("blk")
    scaling = score_gain / math.sqrt(width)
    capacity = alt_ids.shape[2]
    slots = n_blk * capacity

    ids = alt_ids[0]
    line = jnp.concatenate([ids >> 7, ids & 127], axis=1).astype(jnp.bfloat16)
    line = jnp.pad(line, ((0, 0), (0, width - 2 * capacity)))[:, None, :]
    outgoing = jnp.concatenate([jnp.broadcast_to(tokens[None], (n_blk, tok, width)), line], axis=1)
    gathered = exchange(outgoing, "blk")

    parts = exchange(row_pass(gathered, centroids, tok, scaling), "blk")

    asked = gathered[:, tok, :].astype(jnp.int32)
    high = asked[:, :capacity].reshape(1, slots)
    low = asked[:, capacity : 2 * capacity].reshape(1, slots)
    wanted = (high * 128 + low).reshape(slots)
    centres = exchange(centroids[wanted].reshape(n_blk, capacity, width), "blk")
    centres = centres.reshape(slots, width)

    duals, partial_mass = column_pass(gathered, centroids, parts, tok, scaling, slab * n_blk, n_wide)
    own_duals = lax.dynamic_slice_in_dim(duals[0], position * tok, tok)

    chunk = sum_and_copy(exchange(partial_mass, "wide"))
    masses = exchange(chunk, "wide")
    col_duals, found = look_up(masses, high, low, tok * n_blk * n_wide, n_blk, capacity)
    found = exchange(found, "blk")

    live = (jnp.arange(capacity, dtype=jnp.int32)[None, :] < counts[0][:, None]).astype(jnp.int32)
    diff, exponents = prepare(
        tokens, centres, row_ids.reshape(slots, 1), live.reshape(slots, 1), own_duals[None, :], scaling
    )
    residuals = finish(found, diff, exponents, n_blk, capacity)
    return (own_duals, col_duals.reshape(slab), residuals)


def solution(mesh):
    in_specs = (
        P(("blk", "wide"), None),
        P("blk", None),
        P(("blk", "wide"), None, None),
        P(("blk", "wide"), None, None),
        P(("blk", "wide"), None),
    )
    out_specs = (P(("blk", "wide")), P("blk"), P(("blk", "wide"), None, None, None))
    return jax.shard_map(local, mesh=mesh, in_specs=in_specs, out_specs=out_specs, check_vma=False)
```

time: 325 us -> 133 us (0.41)
  the two profiles are of different devices: /device:TPU:8 before, /device:TPU:1 now
where the time goes in v1:
time: 133 us
  waiting for transfers between devices  42.3 us (32%)
  starting transfers between devices  40.9 us (31%)
  Pallas kernels  36.9 us (28%)
  local copies, waits for them, and re-layouts  10 us (8%)
  other arithmetic  1.66 us (1%)
    all_to_all x6, waiting for transfers between devices, exchange(): return lax.all_to_all(x, axis, split_axis=0, concat_axis=0, tiled=True)  42.3 us
    all_to_all x6, starting transfers between devices, exchange(): return lax.all_to_all(x, axis, split_axis=0, concat_axis=0, tiled=True)  40.9 us
    pallas_call x1, Pallas kernels, column_pass(): pl.pallas_call(kernel, out_shape=(jax.ShapeDtypeStruct((1, rows), jnp.flo...  15 us
    pallas_call x1, Pallas kernels, row_pass(): pl.pallas_call(kernel, out_shape=jax.ShapeDtypeStruct((n_blk, 1, rows), j...  14.4 us
    unnamed x16, local copies, waits for them, and re-layouts  2.81 us
  transfers between devices with their start and end apart: 6, of which 6 were waited for; matrix products, arithmetic and copies ran while one was open for 5% of the time, Pallas kernels for 3%

profile of v1, /device:TPU:1, one launch (start us, length us, event | category | flops | bytes accessed | tf_op | source)
XLA Modules:
  0.0 132.5 jit_solution(5194711303882895595)
XLA Ops:
  0.6 0.7 fusion.3
  1.4 0.7 broadcast_in_dim.4
  2.2 0.7 pad_maximum_fusion
  2.9 9.6 %all-to-all-start = ((bf16[16,49,128]{2,1,0:T(8,128)(2,1)}), bf16[16,49,128]{2,1,0:T(8,128)(2,1)S(1)}, u32[]{:S(2)}, u32[]{:S(2)}) async-start(bf16[16,49,128]{2,1,0:T(8,128)(2,1)} %pad_maximum_fusion), calls=%async_computation | async-start | bytes 458752 | tf_op jit(solution)/shard_map/all_to_all | solution.py:25
  12.5 9.7 %all-to-all-done.x_ref = bf16[16,49,128]{2,1,0:T(8,128)(2,1)S(1)} async-done(((bf16[16,49,128]{2,1,0:T(8,128)(2,1)}), bf16[16,49,128]{2,1,0:T(8,128)(2,1)S(1)}, u32[]{:S(2)}, u32[]{:S(2)}) %all-to-all-start) | async-done | bytes 200736 | tf_op jit(solution)/shard_map/all_to_all | solution.py:25
  22.2 1.6 %copy-done = bf16[8192,128]{1,0:T(8,128)(2,1)S(1)} copy-done((bf16[8192,128]{1,0:T(8,128)(2,1)S(1)}, bf16[8192,128]{1,0:T(8,128)(2,1)}, u32[]{:S(2)}) %copy-start) | copy-done | bytes 2097176
  23.8 14.4 %row_pass.1 = f32[16,1,768]{2,1,0:T(1,128)} custom-call(bf16[16,49,128]{2,1,0:T(8,128)(2,1)S(1)} %all-to-all-done.x_ref, bf16[8192,128]{1,0:T(8,128)(2,1)S(1)} %copy-done), custom_call_target="tpu_custom_call" | custom-call | tf_op jit(solution)/shard_map/row_pass/pallas_call | solution.py:72
  38.2 3.6 %all-to-all-start.1 = ((f32[16,1,768]{2,1,0:T(1,128)}), f32[16,1,768]{2,1,0:T(1,128)S(1)}, u32[]{:S(2)}, u32[]{:S(2)}) async-start(f32[16,1,768]{2,1,0:T(1,128)} %row_pass.1), calls=%async_computation.1 | async-start | bytes 98304 | tf_op jit(solution)/shard_map/all_to_all | solution.py:25
  41.9 0.1 add.36
  42.0 7.5 %all-to-all-done.1.l_ref = f32[16,1,768]{2,1,0:T(1,128)S(1)} async-done(((f32[16,1,768]{2,1,0:T(1,128)}), f32[16,1,768]{2,1,0:T(1,128)S(1)}, u32[]{:S(2)}, u32[]{:S(2)}) %all-to-all-start.1) | async-done | bytes 49184 | tf_op jit(solution)/shard_map/all_to_all | solution.py:25
  49.5 15.0 %column_pass.1 = (f32[1,768]{1,0:T(1,128)S(1)}, f32[32,1,256]{2,1,0:T(1,128)}) custom-call(bf16[16,49,128]{2,1,0:T(8,128)(2,1)S(1)} %all-to-all-done.x_ref, bf16[8192,128]{1,0:T(8,128)(2,1)S(1)} %copy-done.1, f32[16,1,768]{2,1,0:T(1,128)S(1)} %all-to-all-done.1.l_ref), custom_call_target="tpu_custom_call" | custom-call | tf_op jit(solution)/shard_map/column_pass/pallas_call | solution.py:129
  64.5 16.0 %all-to-all-start.2 = ((f32[32,1,256]{2,1,0:T(1,128)}), f32[32,1,256]{2,1,0:T(1,128)S(1)}, u32[]{:S(2)}, u32[]{:S(2)}) async-start(f32[32,1,256]{2,1,0:T(1,128)} %get-tuple-element.10), calls=%async_computation.2 | async-start | bytes 65536 | tf_op jit(solution)/shard_map/all_to_all | solution.py:25
  80.5 9.7 %all-to-all-done.2.p_ref = f32[32,1,256]{2,1,0:T(1,128)S(1)} async-done(((f32[32,1,256]{2,1,0:T(1,128)}), f32[32,1,256]{2,1,0:T(1,128)S(1)}, u32[]{:S(2)}, u32[]{:S(2)}) %all-to-all-start.2) | async-done | bytes 32800 | tf_op jit(solution)/shard_map/all_to_all | solution.py:25
  90.2 0.6 copy-done.4
  90.8 1.4 %sum_and_copy.1 = f32[32,1,256]{2,1,0:T(1,128)} custom-call(f32[32,1,256]{2,1,0:T(1,128)} %copy-done.4), custom_call_target="tpu_custom_call" | custom-call | tf_op jit(solution)/shard_map/sum_and_copy/pallas_call | solution.py:153
  92.2 3.9 %all-to-all-start.3 = ((f32[32,1,256]{2,1,0:T(1,128)}), f32[32,1,256]{2,1,0:T(1,128)S(1)}, u32[]{:S(2)}, u32[]{:S(2)}) async-start(f32[32,1,256]{2,1,0:T(1,128)} %sum_and_copy.1), calls=%async_computation.3 | async-start | bytes 65536 | tf_op jit(solution)/shard_map/all_to_all | solution.py:25
  96.1 1.9 %gather_fusion = bf16[512,128]{1,0:T(8,128)(2,1)} fusion(bf16[8192,128]{1,0:T(8,128)(2,1)S(1)} %copy-done.1, s32[1024]{0:T(1024)S(1)} %pad_clamp_fusion), kind=kCustom, calls=%fused_computation | custom fusion | bytes 264192 | tf_op jit(solution)/shard_map/gather | solution.py:272
  98.0 7.8 %all-to-all-done.3.m_ref = f32[32,1,256]{2,1,0:T(1,128)S(1)} async-done(((f32[32,1,256]{2,1,0:T(1,128)}), f32[32,1,256]{2,1,0:T(1,128)S(1)}, u32[]{:S(2)}, u32[]{:S(2)}) %all-to-all-start.3) | async-done | bytes 32800 | tf_op jit(solution)/shard_map/all_to_all | solution.py:25
  105.9 3.5 %all-to-all-start.5 = ((bf16[16,32,128]{2,1,0:T(8,128)(2,1)}), bf16[16,32,128]{2,1,0:T(8,128)(2,1)S(1)}, u32[]{:S(2)}, u32[]{:S(2)}) async-start(bf16[16,32,128]{2,1,0:T(8,128)(2,1)} %bitcast.7), calls=%async_computation.5 | async-start | bytes 262144 | tf_op jit(solution)/shard_map/all_to_all | solution.py:25
  109.5 1.0 reshape.122.v_ref
  110.5 1.0 reshape.121.r_ref
  111.4 0.7 reshape.106.l_ref
  112.1 0.7 reshape.105.h_ref
  112.7 0.6 fusion.7
  113.3 1.8 %look_up.1 = (f32[64,128]{1,0:T(8,128)}, f32[16,1,128]{2,1,0:T(1,128)}) custom-call(f32[32,1,256]{2,1,0:T(1,128)} %copy-done.3, s32[1,512]{1,0:T(1,128)} %reshape.105.h_ref, s32[1,512]{1,0:T(1,128)} %reshape.106.l_ref), custom_call_target="tpu_custom_call" | custom-call | tf_op jit(solution)/shard_map/look_up/pallas_call | solution.py:190
  115.1 3.1 %all-to-all-done.5 = bf16[16,32,128]{2,1,0:T(8,128)(2,1)S(1)} async-done(((bf16[16,32,128]{2,1,0:T(8,128)(2,1)}), bf16[16,32,128]{2,1,0:T(8,128)(2,1)S(1)}, u32[]{:S(2)}, u32[]{:S(2)}) %all-to-all-start.5) | async-done | bytes 131104 | tf_op jit(solution)/shard_map/all_to_all | solution.py:25
  118.2 4.3 %all-to-all-start.4 = ((f32[16,1,128]{2,1,0:T(1,128)}), f32[16,1,128]{2,1,0:T(1,128)S(1)}, u32[]{:S(2)}, u32[]{:S(2)}) async-start(f32[16,1,128]{2,1,0:T(1,128)} %get-tuple-element.12), calls=%async_computation.4 | async-start | bytes 16384 | tf_op jit(solution)/shard_map/all_to_all | solution.py:25
  122.6 0.7 constant_dynamic-slice_fusion.d_ref
  123.2 2.3 %prepare.1 = (f32[512,128]{1,0:T(8,128)}, f32[512,128]{1,0:T(8,128)}) custom-call(bf16[48,128]{1,0:T(8,128)(2,1)} %t_ref.1, bf16[512,128]{1,0:T(8,128)(2,1)} %bitcast.14, s32[512,1]{1,0:T(8,128)} %reshape.121.r_ref, s32[512,1]{1,0:T(8,128)} %reshape.122.v_ref, f32[1,48]{1,0:T(1,128)} %constant_dynamic-slice_fusion.d_ref), custom_call_target="tpu_custom_call" | custom-call | tf_op jit(solution)/shard_map/prepare/pallas_call | solution.py:220
  125.5 4.4 %all-to-all-done.4.g_ref = f32[16,1,128]{2,1,0:T(1,128)S(1)} async-done(((f32[16,1,128]{2,1,0:T(1,128)}), f32[16,1,128]{2,1,0:T(1,128)S(1)}, u32[]{:S(2)}, u32[]{:S(2)}) %all-to-all-start.4) | async-done | bytes 8224 | tf_op jit(solution)/shard_map/all_to_all | solution.py:25
  129.9 0.6 copy-done.5
  130.5 2.0 %finish.1 = f32[1,16,32,128]{3,2,1,0:T(8,128)} custom-call(f32[16,1,128]{2,1,0:T(1,128)} %copy-done.5, f32[512,128]{1,0:T(8,128)} %get-tuple-element.13.d_ref, f32[512,128]{1,0:T(8,128)} %get-tuple-element.14.e_ref), custom_call_target="tpu_custom_call" | custom-call | tf_op jit(solution)/shard_map/finish/pallas_call | solution.py:241
  (20 shorter events, 0.3 us)
Async XLA Ops:
  2.9 19.3 %all-to-all-start = ((bf16[16,49,128]{2,1,0:T(8,128)(2,1)}), bf16[16,49,128]{2,1,0:T(8,128)(2,1)S(1)}, u32[]{:S(2)}, u32[]{:S(2)}) async-start(bf16[16,49,128]{2,1,0:T(8,128)(2,1)} %pad_maximum_fusion), calls=%async_computation | async-start | bytes 458752 | tf_op jit(solution)/shard_map/all_to_all | solution.py:25
  22.2 1.6 %copy-start = (bf16[8192,128]{1,0:T(8,128)(2,1)S(1)}, bf16[8192,128]{1,0:T(8,128)(2,1)}, u32[]{:S(2)}) copy-start(bf16[8192,128]{1,0:T(8,128)(2,1)} %c_ref.3) | copy-start | bytes 6291460
  23.8 25.7 %copy-start.1 = (bf16[8192,128]{1,0:T(8,128)(2,1)S(1)}, bf16[8192,128]{1,0:T(8,128)(2,1)}, u32[]{:S(2)}) copy-start(bf16[8192,128]{1,0:T(8,128)(2,1)} %c_ref.3) | copy-start | bytes 6291460
  38.2 71.2 %copy-start.7 = (s32[1,16]{1,0:T(1,128)S(1)}, s32[1,16]{1,0:T(1,128)}, u32[]{:S(2)}) copy-start(s32[1,16]{1,0:T(1,128)} %param.9) | copy-start | bytes 196
  38.2 11.3 %all-to-all-start.1 = ((f32[16,1,768]{2,1,0:T(1,128)}), f32[16,1,768]{2,1,0:T(1,128)S(1)}, u32[]{:S(2)}, u32[]{:S(2)}) async-start(f32[16,1,768]{2,1,0:T(1,128)} %row_pass.1), calls=%async_computation.1 | async-start | bytes 98304 | tf_op jit(solution)/shard_map/all_to_all | solution.py:25
  42.0 68.5 %copy-start.6 = (s32[1,16,32]{2,1,0:T(8,128)S(1)}, s32[1,16,32]{2,1,0:T(8,128)}, u32[]{:S(2)}) copy-start(s32[1,16,32]{2,1,0:T(8,128)} %param.7) | copy-start | bytes 6148
  64.5 25.6 %all-to-all-start.2 = ((f32[32,1,256]{2,1,0:T(1,128)}), f32[32,1,256]{2,1,0:T(1,128)S(1)}, u32[]{:S(2)}, u32[]{:S(2)}) async-start(f32[32,1,256]{2,1,0:T(1,128)} %get-tuple-element.10), calls=%async_computation.2 | async-start | bytes 65536 | tf_op jit(solution)/shard_map/all_to_all | solution.py:25
  90.2 0.6 copy-start.4
  92.2 13.7 %all-to-all-start.3 = ((f32[32,1,256]{2,1,0:T(1,128)}), f32[32,1,256]{2,1,0:T(1,128)S(1)}, u32[]{:S(2)}, u32[]{:S(2)}) async-start(f32[32,1,256]{2,1,0:T(1,128)} %sum_and_copy.1), calls=%async_computation.3 | async-start | bytes 65536 | tf_op jit(solution)/shard_map/all_to_all | solution.py:25
  105.9 7.4 %copy-start.3 = (f32[32,1,256]{2,1,0:T(1,128)}, f32[32,1,256]{2,1,0:T(1,128)S(1)}, u32[]{:S(2)}) copy-start(f32[32,1,256]{2,1,0:T(1,128)S(1)} %all-to-all-done.3.m_ref) | copy-start | bytes 98308
  105.9 12.3 %all-to-all-start.5 = ((bf16[16,32,128]{2,1,0:T(8,128)(2,1)}), bf16[16,32,128]{2,1,0:T(8,128)(2,1)S(1)}, u32[]{:S(2)}, u32[]{:S(2)}) async-start(bf16[16,32,128]{2,1,0:T(8,128)(2,1)} %bitcast.7), calls=%async_computation.5 | async-start | bytes 262144 | tf_op jit(solution)/shard_map/all_to_all | solution.py:25
  118.2 5.0 %copy-start.2 = (bf16[16,32,128]{2,1,0:T(8,128)(2,1)}, bf16[16,32,128]{2,1,0:T(8,128)(2,1)S(1)}, u32[]{:S(2)}) copy-start(bf16[16,32,128]{2,1,0:T(8,128)(2,1)S(1)} %all-to-all-done.5) | copy-start | bytes 393220
  118.2 11.7 %all-to-all-start.4 = ((f32[16,1,128]{2,1,0:T(1,128)}), f32[16,1,128]{2,1,0:T(1,128)S(1)}, u32[]{:S(2)}, u32[]{:S(2)}) async-start(f32[16,1,128]{2,1,0:T(1,128)} %get-tuple-element.12), calls=%async_computation.4 | async-start | bytes 16384 | tf_op jit(solution)/shard_map/all_to_all | solution.py:25
  129.9 0.6 copy-start.5

commit v2 on v1

v2 whole, which is shorter than its diff:
```python
import math

import jax
import jax.numpy as jnp
from jax import lax
from jax.experimental import pallas as pl
from jax.experimental.pallas import tpu as pltpu
from jax.sharding import PartitionSpec as P

score_gain = 3.0
log2e = 1.4426950408889634
dead = -1.0e30


def vmem(n):
    return [pl.BlockSpec(memory_space=pltpu.VMEM)] * n


def load_rows(x_ref, t_ref, n_blk, tok):
    for i in range(n_blk):
        t_ref[i * tok : (i + 1) * tok, :] = x_ref[i, :tok, :]


def exchange(x, axis):
    return lax.all_to_all(x, axis, split_axis=0, concat_axis=0, tiled=True)


def params(mib):
    return pltpu.CompilerParams(vmem_limit_bytes=mib << 20)


def pack(tokens, alt_ids):
    tok, width = tokens.shape
    n_blk, capacity = alt_ids.shape

    def kernel(t_ref, a_ref, out_ref):
        ids = a_ref[...]
        line = jnp.concatenate(
            [ids >> 7, ids & 127, jnp.zeros((n_blk, width - 2 * capacity), jnp.int32)], axis=1
        ).astype(jnp.float32)
        rows = t_ref[...]
        for i in range(n_blk):
            out_ref[i, :tok, :] = rows
            out_ref[i, tok:, :] = line[i : i + 1, :].astype(jnp.bfloat16)

    return pl.pallas_call(
        kernel,
        out_shape=jax.ShapeDtypeStruct((n_blk, tok + 1, width), jnp.bfloat16),
        in_specs=vmem(2),
        out_specs=pl.BlockSpec(memory_space=pltpu.VMEM),
        compiler_params=params(4),
        name="pack",
    )(tokens, alt_ids)


def row_pass(x, centroids, tok, capacity, scaling):
    n_blk = x.shape[0]
    rows = n_blk * tok
    slots = n_blk * capacity
    slab, width = centroids.shape
    factor = scaling * log2e
    block = math.gcd(slab, 2048)
    small = math.gcd(slab, 256)

    def kernel(x_ref, c_ref, out_ref, ids_ref, t_ref, m_ref, a_ref):
        load_rows(x_ref, t_ref, n_blk, tok)
        for i in range(n_blk):
            line = x_ref[i, tok:, :].astype(jnp.float32).astype(jnp.int32)
            part = slice(i * capacity, (i + 1) * capacity)
            ids_ref[0:1, part] = line[:, :capacity]
            ids_ref[1:2, part] = line[:, capacity : 2 * capacity]
            ids_ref[2:3, part] = line[:, :capacity] * 128 + line[:, capacity : 2 * capacity]

        def scores(start, size, lanes):
            return lax.dot_general(
                c_ref[pl.ds(start, size), :],
                t_ref[lanes, :],
                (((1,), (1,)), ((), ())),
                preferred_element_type=jnp.float32,
            ).reshape(size // 8, 8, 256)

        def rescale_free():
            for g in range(rows // 256):
                lanes = slice(g * 256, (g + 1) * 256)
                first = jnp.max(scores(0, small, lanes), axis=(0, 1)).reshape(1, 256)
                m_ref[:, lanes] = jnp.broadcast_to(first, (8, 256))
            a_ref[...] = jnp.zeros_like(a_ref)

            def step(j, carry):
                start = pl.multiple_of(j * block, block)
                for g in range(rows // 256):
                    lanes = slice(g * 256, (g + 1) * 256)
                    e = jnp.exp2((scores(start, block, lanes) - m_ref[:, lanes][None]) * factor)
                    a_ref[:, lanes] = a_ref[:, lanes] + jnp.sum(e, axis=0)
                return carry

            lax.fori_loop(0, slab // block, step, 0)

        def rescaled():
            m_ref[...] = jnp.full_like(m_ref, dead)
            a_ref[...] = jnp.zeros_like(a_ref)

            def step(j, carry):
                start = pl.multiple_of(j * small, small)
                for g in range(rows // 256):
                    lanes = slice(g * 256, (g + 1) * 256)
                    s = scores(start, small, lanes)
                    old = m_ref[:, lanes]
                    new = jnp.maximum(old, jnp.max(s, axis=0))
                    m_ref[:, lanes] = new
                    part = jnp.sum(jnp.exp2((s - new[None]) * factor), axis=0)
                    a_ref[:, lanes] = a_ref[:, lanes] * jnp.exp2((old - new) * factor) + part
                return carry

            lax.fori_loop(0, slab // small, step, 0)

        rescale_free()

        @pl.when(jnp.logical_not(jnp.max(a_ref[...]) < 1.0e38))
        def _():
            rescaled()

        m = m_ref[...]
        top = jnp.max(m, axis=0, keepdims=True)
        total = jnp.sum(a_ref[...] * jnp.exp2((m - top) * factor), axis=0, keepdims=True)
        lse = top * scaling + jnp.log(total)
        for i in range(n_blk):
            out_ref[i] = lse

    return pl.pallas_call(
        kernel,
        out_shape=(
            jax.ShapeDtypeStruct((n_blk, 1, rows), jnp.float32),
            jax.ShapeDtypeStruct((3, slots), jnp.int32),
        ),
        in_specs=vmem(2),
        out_specs=tuple(vmem(2)),
        scratch_shapes=[
            pltpu.VMEM((rows, width), jnp.bfloat16),
            pltpu.VMEM((8, rows), jnp.float32),
            pltpu.VMEM((8, rows), jnp.float32),
        ],
        compiler_params=params(16),
        name="row_pass",
    )(x, centroids)


def column_pass(x, centroids, parts, tok, scaling, all_cols, chunks):
    n_blk = x.shape[0]
    rows = n_blk * tok
    slab, width = centroids.shape
    block = slab // chunks
    group = math.gcd(chunks, 8)
    factor = scaling * log2e

    def kernel(x_ref, c_ref, l_ref, own_ref, mass_ref, t_ref, d_ref):
        load_rows(x_ref, t_ref, n_blk, tok)
        lse = l_ref[:, 0, :]
        top = jnp.max(lse, axis=0, keepdims=True)
        total = jnp.sum(jnp.exp(lse - top), axis=0, keepdims=True)
        dual = math.log(all_cols) - (top + jnp.log(total))
        position = lax.axis_index("blk")
        own = jnp.zeros((1, tok), jnp.float32)
        for i in range(n_blk):
            own = own + jnp.where(position == i, dual[:, i * tok : (i + 1) * tok], 0.0)
        own_ref[...] = own
        d_ref[...] = jnp.transpose(jnp.broadcast_to(dual * log2e, (128, rows)))

        def step(j, carry):
            for g in range(group):
                k = j * group + g
                s = lax.dot_general(
                    t_ref[...],
                    c_ref[pl.ds(pl.multiple_of(k * block, block), block), :],
                    (((1,), (1,)), ((), ())),
                    preferred_element_type=jnp.float32,
                )
                d = d_ref[...]
                e = jnp.exp2(s * factor + jnp.concatenate([d] * (block // 128), axis=1))
                mass_ref[k] = jnp.sum(e, axis=0, keepdims=True)
            return carry

        lax.fori_loop(0, chunks // group, step, 0)

    return pl.pallas_call(
        kernel,
        out_shape=(
            jax.ShapeDtypeStruct((1, tok), jnp.float32),
            jax.ShapeDtypeStruct((chunks, 1, block), jnp.float32),
        ),
        in_specs=vmem(3),
        out_specs=tuple(vmem(2)),
        scratch_shapes=[
            pltpu.VMEM((rows, width), jnp.bfloat16),
            pltpu.VMEM((rows, 128), jnp.float32),
        ],
        compiler_params=params(16),
        name="column_pass",
    )(x, centroids, parts)


def sum_and_copy(parts):
    def kernel(p_ref, out_ref):
        total = jnp.sum(p_ref[:, 0, :], axis=0, keepdims=True)
        for j in range(parts.shape[0]):
            out_ref[j] = total

    return pl.pallas_call(
        kernel,
        out_shape=jax.ShapeDtypeStruct(parts.shape, jnp.float32),
        in_specs=vmem(1),
        out_specs=pl.BlockSpec(memory_space=pltpu.VMEM),
        compiler_params=params(4),
        name="sum_and_copy",
    )(parts)


def look_up(masses, ids, all_rows, n_blk, capacity):
    chunks, _, block = masses.shape
    lines = chunks * block // 128
    slots = n_blk * capacity

    def kernel(m_ref, i_ref, dual_ref, out_ref):
        for j in range(chunks):
            for g in range(block // 128):
                k = j * (block // 128) + g
                dual_ref[k : k + 1, :] = m_ref[j, :, g * 128 : (g + 1) * 128]
        dual = math.log(all_rows) - jnp.log(dual_ref[...])
        dual_ref[...] = dual
        line = lax.broadcasted_iota(jnp.int32, (lines, slots), 0)
        pick = jnp.where(line == i_ref[0:1, :], 1.0, 0.0).astype(jnp.bfloat16)
        rest = jnp.clip(dual, -3.0e38, 3.0e38)
        found = jnp.zeros((128, slots), jnp.float32)
        for _ in range(3):
            piece = rest.astype(jnp.bfloat16)
            rest = rest - piece.astype(jnp.float32)
            found = found + lax.dot_general(
                piece, pick, (((0,), (0,)), ((), ())), preferred_element_type=jnp.float32
            )
        lane = lax.broadcasted_iota(jnp.int32, (128, slots), 0)
        value = jnp.sum(jnp.where(lane == i_ref[1:2, :], found, 0.0), axis=0, keepdims=True)
        out_ref[...] = jnp.zeros_like(out_ref)
        for i in range(n_blk):
            out_ref[i, :, :capacity] = value[:, i * capacity : (i + 1) * capacity]

    return pl.pallas_call(
        kernel,
        out_shape=(
            jax.ShapeDtypeStruct((lines, 128), jnp.float32),
            jax.ShapeDtypeStruct((n_blk, 1, 128), jnp.float32),
        ),
        in_specs=vmem(2),
        out_specs=tuple(vmem(2)),
        compiler_params=params(4),
        name="look_up",
    )(masses, ids)


def prepare(tokens, centres, row_ids, counts, duals, scaling):
    n_blk, capacity = row_ids.shape
    slots = n_blk * capacity
    tok, width = tokens.shape

    def kernel(n_ref, t_ref, c_ref, r_ref, d_ref, diff_ref, exp_ref, w_ref):
        w_ref[...] = jnp.zeros_like(w_ref)
        w_ref[:, :capacity] = r_ref[...].astype(jnp.float32)
        turned = jnp.transpose(w_ref[...])
        row = lax.broadcasted_iota(jnp.int32, (capacity, tok), 1).astype(jnp.float32)
        place = lax.broadcasted_iota(jnp.int32, (capacity, 1), 0)
        rows = t_ref[...]
        for i in range(n_blk):
            part = slice(i * capacity, (i + 1) * capacity)
            hit = row == turned[:capacity, i : i + 1]
            picked = jnp.dot(
                jnp.where(hit, 1.0, 0.0).astype(jnp.bfloat16), rows, preferred_element_type=jnp.float32
            )
            centre = c_ref[i].astype(jnp.float32)
            diff_ref[part, :] = picked - centre
            score = jnp.sum(picked * centre, axis=1, keepdims=True) * scaling
            dual = jnp.sum(jnp.where(hit, d_ref[...], 0.0), axis=1, keepdims=True)
            exponent = jnp.where(place < n_ref[0, i], score + dual, dead)
            exp_ref[part, :] = jnp.broadcast_to(exponent, (capacity, width))

    shape = jax.ShapeDtypeStruct((slots, width), jnp.float32)
    return pl.pallas_call(
        kernel,
        out_shape=(shape, shape),
        in_specs=[pl.BlockSpec(memory_space=pltpu.SMEM)] + vmem(4),
        out_specs=tuple(vmem(2)),
        scratch_shapes=[pltpu.VMEM((n_blk, 128), jnp.float32)],
        compiler_params=params(4),
        name="prepare",
    )(counts, tokens, centres, row_ids, duals)


def finish(duals, diff, exponents, n_blk, capacity):
    width = diff.shape[1]

    def kernel(g_ref, d_ref, e_ref, out_ref):
        turned = jnp.transpose(g_ref[:, 0, :])
        for i in range(n_blk):
            part = slice(i * capacity, (i + 1) * capacity)
            dual = jnp.broadcast_to(turned[:capacity, i : i + 1], (capacity, width))
            e = e_ref[part, :]
            weight = jnp.where(e > 0.1 * dead, jnp.exp(e + dual), 0.0)
            out_ref[0, i] = weight * d_ref[part, :]

    return pl.pallas_call(
        kernel,
        out_shape=jax.ShapeDtypeStruct((1, n_blk, capacity, width), jnp.float32),
        in_specs=vmem(3),
        out_specs=pl.BlockSpec(memory_space=pltpu.VMEM),
        compiler_params=params(4),
        name="finish",
    )(duals, diff, exponents)


def local(tokens, centroids, row_ids, alt_ids, counts):
    tok, width = tokens.shape
    slab = centroids.shape[0]
    n_blk = lax.axis_size("blk")
    n_wide = lax.axis_size("wide")
    scaling = score_gain / math.sqrt(width)
    capacity = alt_ids.shape[2]
    slots = n_blk * capacity

    gathered = exchange(pack(tokens, alt_ids[0]), "blk")
    lse, ids = row_pass(gathered, centroids, tok, capacity, scaling)
    parts = exchange(lse, "blk")
    centres = exchange(centroids[ids[2]].reshape(n_blk, capacity, width), "blk")
    own_duals, partial_mass = column_pass(gathered, centroids, parts, tok, scaling, slab * n_blk, n_wide)
    partial_mass, centres = lax.optimization_barrier((partial_mass, centres))

    chunk = sum_and_copy(exchange(partial_mass, "wide"))
    diff, exponents = prepare(tokens, centres, row_ids[0], counts, own_duals, scaling)
    chunk, diff, exponents = lax.optimization_barrier((chunk, diff, exponents))
    masses = exchange(chunk, "wide")
    col_duals, found = look_up(masses, ids, tok * n_blk * n_wide, n_blk, capacity)
    residuals = finish(exchange(found, "blk"), diff, exponents, n_blk, capacity)
    return (own_duals.reshape(tok), col_duals.reshape(slab), residuals)


def solution(mesh):
    in_specs = (
        P(("blk", "wide"), None),
        P("blk", None),
        P(("blk", "wide"), None, None),
        P(("blk", "wide"), None, None),
        P(("blk", "wide"), None),
    )
    out_specs = (P(("blk", "wide")), P("blk"), P(("blk", "wide"), None, None, None))
    return jax.shard_map(local, mesh=mesh, in_specs=in_specs, out_specs=out_specs, check_vma=False)
```

time: 133 us -> 115 us (0.86)
  blocking collectives: 0 us -> 42.1 us
  waiting for transfers between devices: 42.3 us -> 16.2 us
  Pallas kernels: 36.9 us -> 14.1 us
  starting transfers between devices: 40.9 us -> 35.8 us
  local copies, waits for them, and re-layouts: 10 us -> 5.57 us
  other arithmetic: 1.66 us -> 0.01 us
    all_to_all x0 -> x3, blocking collectives: none -> 42.1 us  [exchange(): return lax.all_to_all(x, axis, split_axis=0, concat_axis=0, tiled=True)]
    all_to_all x6 -> x3, waiting for transfers between devices: 42.3 us -> 16.2 us  [exchange(): return lax.all_to_all(x, axis, split_axis=0, concat_axis=0, tiled=True)]
    pallas_call x3 -> x4, Pallas kernels: 31.7 us -> 12.5 us  [the longest x1 5.28 us: row_pass(): pl.pallas_call(kernel, out_shape=(jax.ShapeDtypeStruct((n_blk, 1, rows),...]
    all_to_all x6 -> x3, starting transfers between devices: 40.9 us -> 35.8 us  [exchange(): return lax.all_to_all(x, axis, split_axis=0, concat_axis=0, tiled=True)]
    reshape x3 -> x0, local copies, waits for them, and re-layouts: 2.27 us -> none  [the longest x1 0.96 us: local(): row_ids.reshape(slots, 1)]
    pallas_call x1, Pallas kernels: 1.4 us -> 0.04 us  [sum_and_copy(): pl.pallas_call(kernel, out_shape=jax.ShapeDtypeStruct(parts.shape, jnp.fl...]
  transfers between devices with their start and end apart: 6 -> 3, of which waited for: 6 -> 3; matrix products, arithmetic and copies ran while one was open for 5% -> 2% of each run, Pallas kernels for 3% -> 6%
where the time goes in v2:
time: 115 us; the launch traced here: 114 us
  blocking collectives  42.1 us (37%)
  starting transfers between devices  35.8 us (31%)
  waiting for transfers between devices  16.2 us (14%)
  Pallas kernels  14.1 us (12%)
  local copies, waits for them, and re-layouts  5.57 us (5%)
    all_to_all x3, blocking collectives, exchange(): return lax.all_to_all(x, axis, split_axis=0, concat_axis=0, tiled=True)  42.1 us
    all_to_all x3, starting transfers between devices, exchange(): return lax.all_to_all(x, axis, split_axis=0, concat_axis=0, tiled=True)  35.8 us
    all_to_all x3, waiting for transfers between devices, exchange(): return lax.all_to_all(x, axis, split_axis=0, concat_axis=0, tiled=True)  16.2 us
    pallas_call x1, Pallas kernels, row_pass(): pl.pallas_call(kernel, out_shape=(jax.ShapeDtypeStruct((n_blk, 1, rows),...  5.28 us
    pallas_call x1, Pallas kernels, column_pass(): pl.pallas_call(kernel, out_shape=(jax.ShapeDtypeStruct((1, tok), jnp.floa...  4.89 us
    unnamed x16, local copies, waits for them, and re-layouts  3.66 us
  transfers between devices with their start and end apart: 3, of which 3 were waited for; matrix products, arithmetic and copies ran while one was open for 2% of the time, Pallas kernels for 6%

profile of v2, /device:TPU:1, one launch (start us, length us, event | category | flops | bytes accessed | tf_op | source)
XLA Modules:
  0.0 114.4 jit_solution(15328596069995350493)
XLA Ops:
  0.6 0.0 copy-start.2
  0.6 0.7 copy-done.2
  1.3 0.0 copy-start.4
  1.3 0.7 copy-done.4
  2.0 0.1 pack.1
  2.1 19.1 %all_to_all.30.x_ref = bf16[16,49,128]{2,1,0:T(8,128)(2,1)S(1)} all-to-all(bf16[16,49,128]{2,1,0:T(8,128)(2,1)S(1)} %pack.1), channel_id=1, replica_groups=mesh['blk'=16,'wide'=32] {'blk'}, dimensions={0} | all-to-all | bytes 401408 | tf_op jit(solution)/shard_map/all_to_all | solution.py:25
  21.2 0.0 copy-start
  21.2 1.6 %copy-done = bf16[8192,128]{1,0:T(8,128)(2,1)S(1)} copy-done((bf16[8192,128]{1,0:T(8,128)(2,1)S(1)}, bf16[8192,128]{1,0:T(8,128)(2,1)}, u32[]{:S(2)}) %copy-start) | copy-done | bytes 2097176
  22.8 0.0 copy-start.1
  22.8 5.3 %row_pass.1 = (f32[16,1,768]{2,1,0:T(1,128)}, s32[3,512]{1,0:T(4,128)S(1)}) custom-call(bf16[16,49,128]{2,1,0:T(8,128)(2,1)S(1)} %all_to_all.30.x_ref, bf16[8192,128]{1,0:T(8,128)(2,1)S(1)} %copy-done), custom_call_target="tpu_custom_call" | custom-call | tf_op jit(solution)/shard_map/row_pass/pallas_call | solution.py:130
  28.1 0.0 copy-start.3
  28.1 0.0 copy-start.5
  28.1 0.0 copy-start.6
  28.1 15.2 %all-to-all-start.1 = ((f32[16,1,768]{2,1,0:T(1,128)}), f32[16,1,768]{2,1,0:T(1,128)S(1)}, u32[]{:S(2)}, u32[]{:S(2)}) async-start(f32[16,1,768]{2,1,0:T(1,128)} %get-tuple-element.16), calls=%async_computation.1 | async-start | bytes 98304 | tf_op jit(solution)/shard_map/all_to_all | solution.py:25
  43.3 0.0 copy-done.1
  43.3 1.9 %gather_fusion = bf16[512,128]{1,0:T(8,128)(2,1)} fusion(bf16[8192,128]{1,0:T(8,128)(2,1)S(1)} %copy-done.1, s32[1024]{0:T(1024)S(1)} %pad_clamp_fusion), kind=kCustom, calls=%fused_computation | custom fusion | bytes 264192 | tf_op jit(solution)/shard_map/gather | solution.py:330
  45.2 5.8 %all-to-all-done.1.l_ref = f32[16,1,768]{2,1,0:T(1,128)S(1)} async-done(((f32[16,1,768]{2,1,0:T(1,128)}), f32[16,1,768]{2,1,0:T(1,128)S(1)}, u32[]{:S(2)}, u32[]{:S(2)}) %all-to-all-start.1) | async-done | bytes 49184 | tf_op jit(solution)/shard_map/all_to_all | solution.py:25
  51.0 3.5 %all-to-all-start.2 = ((bf16[16,32,128]{2,1,0:T(8,128)(2,1)}), bf16[16,32,128]{2,1,0:T(8,128)(2,1)S(1)}, u32[]{:S(2)}, u32[]{:S(2)}) async-start(bf16[16,32,128]{2,1,0:T(8,128)(2,1)} %bitcast.4), calls=%async_computation.2 | async-start | bytes 262144 | tf_op jit(solution)/shard_map/all_to_all | solution.py:25
  54.5 4.9 %column_pass.1 = (f32[1,48]{1,0:T(1,128)}, f32[32,1,256]{2,1,0:T(1,128)}) custom-call(bf16[16,49,128]{2,1,0:T(8,128)(2,1)S(1)} %all_to_all.30.x_ref, bf16[8192,128]{1,0:T(8,128)(2,1)S(1)} %copy-done.1, f32[16,1,768]{2,1,0:T(1,128)S(1)} %all-to-all-done.1.l_ref), custom_call_target="tpu_custom_call" | custom-call | tf_op jit(solution)/shard_map/column_pass/pallas_call | solution.py:185
  59.4 3.6 %all-to-all-done.2.c_ref = bf16[16,32,128]{2,1,0:T(8,128)(2,1)S(1)} async-done(((bf16[16,32,128]{2,1,0:T(8,128)(2,1)}), bf16[16,32,128]{2,1,0:T(8,128)(2,1)S(1)}, u32[]{:S(2)}, u32[]{:S(2)}) %all-to-all-start.2) | async-done | bytes 131104 | tf_op jit(solution)/shard_map/all_to_all | solution.py:25
  63.1 17.1 %all-to-all-start.3 = ((f32[32,1,256]{2,1,0:T(1,128)}), f32[32,1,256]{2,1,0:T(1,128)S(1)}, u32[]{:S(2)}, u32[]{:S(2)}) async-start(f32[32,1,256]{2,1,0:T(1,128)} %get-tuple-element.20), calls=%async_computation.3 | async-start | bytes 65536 | tf_op jit(solution)/shard_map/all_to_all | solution.py:25
  80.2 0.0 copy-done.3
  80.2 0.0 copy-done.5
  80.2 0.0 copy-done.6
  80.2 0.0 copy-start.7
  80.2 0.6 copy-done.7
  80.9 2.2 %prepare.1 = (f32[512,128]{1,0:T(8,128)S(1)}, f32[512,128]{1,0:T(8,128)S(1)}) custom-call(s32[1,16]{1,0:T(1,128)S(1)} %copy-done.6, bf16[48,128]{1,0:T(8,128)(2,1)S(1)} %copy-done.3, bf16[16,32,128]{2,1,0:T(8,128)(2,1)S(1)} %all-to-all-done.2.c_ref, s32[16,32]{1,0:T(8,128)S(1)} %bitcast.9, f32[1,48]{1,0:T(1,128)S(1)} %copy-done.7), custom_call_target="tpu_custom_call" | custom-call | tf_op jit(solution)/shard_map/prepare/pallas_call | solution.py:285
  83.1 6.7 %all-to-all-done.3.p_ref = f32[32,1,256]{2,1,0:T(1,128)S(1)} async-done(((f32[32,1,256]{2,1,0:T(1,128)}), f32[32,1,256]{2,1,0:T(1,128)S(1)}, u32[]{:S(2)}, u32[]{:S(2)}) %all-to-all-start.3) | async-done | bytes 32800 | tf_op jit(solution)/shard_map/all_to_all | solution.py:25
  89.9 12.8 %all_to_all.31.m_ref = f32[32,1,256]{2,1,0:T(1,128)S(1)} all-to-all(f32[32,1,256]{2,1,0:T(1,128)S(1)} %sum_and_copy.1), channel_id=1, replica_groups=mesh['blk'=16,'wide'=32] {'wide'}, dimensions={0} | all-to-all | bytes 65536 | tf_op jit(solution)/shard_map/all_to_all | solution.py:25
  102.7 0.6 look_up.1
  103.3 10.2 %all_to_all.32.g_ref = f32[16,1,128]{2,1,0:T(1,128)S(1)} all-to-all(f32[16,1,128]{2,1,0:T(1,128)S(1)} %get-tuple-element.26), channel_id=1, replica_groups=mesh['blk'=16,'wide'=32] {'blk'}, dimensions={0} | all-to-all | bytes 16384 | tf_op jit(solution)/shard_map/all_to_all | solution.py:25
  113.5 1.0 finish.1
  (3 shorter events, 0.0 us)
Async XLA Ops:
  0.6 0.7 copy-start.2
  1.3 0.7 copy-start.4
  21.2 1.6 %copy-start = (bf16[8192,128]{1,0:T(8,128)(2,1)S(1)}, bf16[8192,128]{1,0:T(8,128)(2,1)}, u32[]{:S(2)}) copy-start(bf16[8192,128]{1,0:T(8,128)(2,1)} %c_ref.3) | copy-start | bytes 6291460
  22.8 20.5 %copy-start.1 = (bf16[8192,128]{1,0:T(8,128)(2,1)S(1)}, bf16[8192,128]{1,0:T(8,128)(2,1)}, u32[]{:S(2)}) copy-start(bf16[8192,128]{1,0:T(8,128)(2,1)} %c_ref.3) | copy-start | bytes 6291460
  28.1 52.1 %copy-start.3 = (bf16[48,128]{1,0:T(8,128)(2,1)S(1)}, bf16[48,128]{1,0:T(8,128)(2,1)}, u32[]{:S(2)}) copy-start(bf16[48,128]{1,0:T(8,128)(2,1)} %t_ref.3) | copy-start | bytes 36868
  28.1 52.1 %copy-start.5 = (s32[1,16,32]{2,1,0:T(8,128)S(1)}, s32[1,16,32]{2,1,0:T(8,128)}, u32[]{:S(2)}) copy-start(s32[1,16,32]{2,1,0:T(8,128)} %param.7) | copy-start | bytes 6148
  28.1 52.1 %copy-start.6 = (s32[1,16]{1,0:T(1,128)S(1)}, s32[1,16]{1,0:T(1,128)}, u32[]{:S(2)}) copy-start(s32[1,16]{1,0:T(1,128)} %n_ref.1) | copy-start | bytes 196
  28.1 22.9 %all-to-all-start.1 = ((f32[16,1,768]{2,1,0:T(1,128)}), f32[16,1,768]{2,1,0:T(1,128)S(1)}, u32[]{:S(2)}, u32[]{:S(2)}) async-start(f32[16,1,768]{2,1,0:T(1,128)} %get-tuple-element.16), calls=%async_computation.1 | async-start | bytes 98304 | tf_op jit(solution)/shard_map/all_to_all | solution.py:25
  51.0 12.0 %all-to-all-start.2 = ((bf16[16,32,128]{2,1,0:T(8,128)(2,1)}), bf16[16,32,128]{2,1,0:T(8,128)(2,1)S(1)}, u32[]{:S(2)}, u32[]{:S(2)}) async-start(bf16[16,32,128]{2,1,0:T(8,128)(2,1)} %bitcast.4), calls=%async_computation.2 | async-start | bytes 262144 | tf_op jit(solution)/shard_map/all_to_all | solution.py:25
  63.1 26.8 %all-to-all-start.3 = ((f32[32,1,256]{2,1,0:T(1,128)}), f32[32,1,256]{2,1,0:T(1,128)S(1)}, u32[]{:S(2)}, u32[]{:S(2)}) async-start(f32[32,1,256]{2,1,0:T(1,128)} %get-tuple-element.20), calls=%async_computation.3 | async-start | bytes 65536 | tf_op jit(solution)/shard_map/all_to_all | solution.py:25
  80.2 0.7 copy-start.7

commit v3 on v2

v3 whole, which is shorter than its diff:
```python
import math

import jax
import jax.numpy as jnp
from jax import lax
from jax.experimental import pallas as pl
from jax.experimental.pallas import tpu as pltpu
from jax.sharding import PartitionSpec as P

score_gain = 3.0
log2e = 1.4426950408889634
dead = -1.0e30


def vmem(n):
    return [pl.BlockSpec(memory_space=pltpu.VMEM)] * n


def load_rows(x_ref, t_ref, n_blk, tok):
    for i in range(n_blk):
        t_ref[i * tok : (i + 1) * tok, :] = x_ref[i, :tok, :]


def exchange(x, axis, groups=None):
    return lax.all_to_all(x, axis, split_axis=0, concat_axis=0, axis_index_groups=groups, tiled=True)


def params(mib):
    return pltpu.CompilerParams(vmem_limit_bytes=mib << 20)


def stage(x):
    def kernel(x_ref, out_ref, sem):
        copy = pltpu.make_async_copy(x_ref, out_ref, sem)
        copy.start()
        copy.wait()

    return pl.pallas_call(
        kernel,
        out_shape=jax.ShapeDtypeStruct(x.shape, x.dtype),
        in_specs=[pl.BlockSpec(memory_space=pl.ANY)],
        out_specs=pl.BlockSpec(memory_space=pltpu.VMEM),
        scratch_shapes=[pltpu.SemaphoreType.DMA],
        compiler_params=params(4),
        cost_estimate=pl.CostEstimate(flops=0, transcendentals=0, bytes_accessed=2 * x.size * x.dtype.itemsize),
        name="stage",
    )(x)


def row_pass(x, centroids, alt_ids, tok, scaling):
    n_blk = x.shape[0]
    rows = n_blk * tok
    capacity = alt_ids.shape[1]
    slab, width = centroids.shape
    factor = scaling * log2e
    block = math.gcd(slab, 2048)
    small = math.gcd(slab, 256)

    def kernel(x_ref, c_ref, i_ref, out_ref, t_ref, m_ref, a_ref):
        load_rows(x_ref, t_ref, n_blk, tok)

        def scores(start, size, lanes):
            return lax.dot_general(
                c_ref[pl.ds(start, size), :],
                t_ref[lanes, :],
                (((1,), (1,)), ((), ())),
                preferred_element_type=jnp.float32,
            ).reshape(size // 8, 8, 256)

        def rescale_free():
            for g in range(rows // 256):
                lanes = slice(g * 256, (g + 1) * 256)
                first = jnp.max(scores(0, small, lanes), axis=(0, 1)).reshape(1, 256)
                m_ref[:, lanes] = jnp.broadcast_to(first, (8, 256))
            a_ref[...] = jnp.zeros_like(a_ref)

            def step(j, carry):
                start = pl.multiple_of(j * block, block)
                for g in range(rows // 256):
                    lanes = slice(g * 256, (g + 1) * 256)
                    e = jnp.exp2((scores(start, block, lanes) - m_ref[:, lanes][None]) * factor)
                    a_ref[:, lanes] = a_ref[:, lanes] + jnp.sum(e, axis=0)
                return carry

            lax.fori_loop(0, slab // block, step, 0)

        def rescaled():
            m_ref[...] = jnp.full_like(m_ref, dead)
            a_ref[...] = jnp.zeros_like(a_ref)

            def step(j, carry):
                start = pl.multiple_of(j * small, small)
                for g in range(rows // 256):
                    lanes = slice(g * 256, (g + 1) * 256)
                    s = scores(start, small, lanes)
                    old = m_ref[:, lanes]
                    new = jnp.maximum(old, jnp.max(s, axis=0))
                    m_ref[:, lanes] = new
                    part = jnp.sum(jnp.exp2((s - new[None]) * factor), axis=0)
                    a_ref[:, lanes] = a_ref[:, lanes] * jnp.exp2((old - new) * factor) + part
                return carry

            lax.fori_loop(0, slab // small, step, 0)

        rescale_free()

        @pl.when(jnp.logical_not(jnp.max(a_ref[...]) < 1.0e38))
        def _():
            rescaled()

        m = m_ref[...]
        top = jnp.max(m, axis=0, keepdims=True)
        total = jnp.sum(a_ref[...] * jnp.exp2((m - top) * factor), axis=0, keepdims=True)
        lse = top * scaling + jnp.log(total)
        ids = i_ref[...]
        line = jnp.concatenate(
            [ids >> 7, ids & 127, jnp.zeros((n_blk, 128 - 2 * capacity), jnp.int32)], axis=1
        ).astype(jnp.float32)
        for i in range(n_blk):
            out_ref[i, :, :rows] = lse
            out_ref[i, :, rows:] = line[i : i + 1, :]

    return pl.pallas_call(
        kernel,
        out_shape=jax.ShapeDtypeStruct((n_blk, 1, rows + 128), jnp.float32),
        in_specs=vmem(3),
        out_specs=pl.BlockSpec(memory_space=pltpu.VMEM),
        scratch_shapes=[
            pltpu.VMEM((rows, width), jnp.bfloat16),
            pltpu.VMEM((8, rows), jnp.float32),
            pltpu.VMEM((8, rows), jnp.float32),
        ],
        compiler_params=params(16),
        name="row_pass",
    )(x, centroids, alt_ids)


def unpack(parts, rows, capacity):
    n_blk = parts.shape[0]

    def kernel(p_ref, ids_ref):
        for i in range(n_blk):
            line = p_ref[i, :, rows:].astype(jnp.int32)
            part = slice(i * capacity, (i + 1) * capacity)
            ids_ref[0:1, part] = line[:, :capacity]
            ids_ref[1:2, part] = line[:, capacity : 2 * capacity]
            ids_ref[2:3, part] = line[:, :capacity] * 128 + line[:, capacity : 2 * capacity]

    return pl.pallas_call(
        kernel,
        out_shape=jax.ShapeDtypeStruct((3, n_blk * capacity), jnp.int32),
        in_specs=vmem(1),
        out_specs=pl.BlockSpec(memory_space=pltpu.VMEM),
        compiler_params=params(4),
        name="unpack",
    )(parts)


def column_pass(x, centroids, parts, tok, scaling, all_cols):
    n_blk = x.shape[0]
    rows = n_blk * tok
    slab, width = centroids.shape
    block = 256
    group = math.gcd(slab // block, 8)
    factor = scaling * log2e

    def kernel(x_ref, c_ref, l_ref, own_ref, mass_ref, t_ref, d_ref):
        load_rows(x_ref, t_ref, n_blk, tok)
        lse = l_ref[:, 0, :rows]
        top = jnp.max(lse, axis=0, keepdims=True)
        total = jnp.sum(jnp.exp(lse - top), axis=0, keepdims=True)
        dual = math.log(all_cols) - (top + jnp.log(total))
        position = lax.axis_index("blk")
        own = jnp.zeros((1, tok), jnp.float32)
        for i in range(n_blk):
            own = own + jnp.where(position == i, dual[:, i * tok : (i + 1) * tok], 0.0)
        own_ref[...] = own
        d_ref[...] = jnp.transpose(jnp.broadcast_to(dual * log2e, (128, rows)))

        def step(j, carry):
            for g in range(group):
                k = j * group + g
                s = lax.dot_general(
                    t_ref[...],
                    c_ref[pl.ds(pl.multiple_of(k * block, block), block), :],
                    (((1,), (1,)), ((), ())),
                    preferred_element_type=jnp.float32,
                )
                d = d_ref[...]
                e = jnp.exp2(s * factor + jnp.concatenate([d] * (block // 128), axis=1))
                mass = jnp.sum(e, axis=0, keepdims=True)
                for h in range(block // 128):
                    mass_ref[pl.ds(k * (block // 128) + h, 1), :] = mass[:, h * 128 : (h + 1) * 128]
            return carry

        lax.fori_loop(0, slab // (block * group), step, 0)

    return pl.pallas_call(
        kernel,
        out_shape=(
            jax.ShapeDtypeStruct((1, tok), jnp.float32),
            jax.ShapeDtypeStruct((slab // 128, 128), jnp.float32),
        ),
        in_specs=vmem(3),
        out_specs=tuple(vmem(2)),
        scratch_shapes=[
            pltpu.VMEM((rows, width), jnp.bfloat16),
            pltpu.VMEM((rows, 128), jnp.float32),
        ],
        compiler_params=params(16),
        name="column_pass",
    )(x, centroids, parts)


def spread(pair_mass, copies):
    half = pair_mass.shape[0] // 2

    def kernel(p_ref, out_ref):
        core = lax.rem(lax.axis_index("wide"), 2)
        part = p_ref[pl.ds(pl.multiple_of(core * half, half), half), :]
        for j in range(copies):
            out_ref[j] = part

    return pl.pallas_call(
        kernel,
        out_shape=jax.ShapeDtypeStruct((copies, half, 128), jnp.float32),
        in_specs=vmem(1),
        out_specs=pl.BlockSpec(memory_space=pltpu.VMEM),
        compiler_params=params(4),
        name="spread",
    )(pair_mass)


def add_up(parts):
    def kernel(p_ref, out_ref):
        out_ref[...] = jnp.sum(p_ref[...], axis=0)

    return pl.pallas_call(
        kernel,
        out_shape=jax.ShapeDtypeStruct(parts.shape[1:], jnp.float32),
        in_specs=vmem(1),
        out_specs=pl.BlockSpec(memory_space=pltpu.VMEM),
        compiler_params=params(4),
        name="add_up",
    )(parts)


def pieces_of(value):
    rest, pieces = jnp.clip(value, -3.0e38, 3.0e38), []
    for _ in range(3):
        piece = rest.astype(jnp.bfloat16)
        pieces.append(piece)
        rest = rest - piece.astype(jnp.float32)
    return pieces


def look_up(masses, ids, centres, all_rows, n_blk, capacity):
    lines = masses.shape[0]
    slots = n_blk * capacity

    def kernel(m_ref, i_ref, c_ref, dual_ref, out_ref):
        dual = math.log(all_rows) - jnp.log(m_ref[...])
        dual_ref[...] = dual
        line = lax.broadcasted_iota(jnp.int32, (lines, slots), 0)
        pick = jnp.where(line == i_ref[0:1, :], 1.0, 0.0).astype(jnp.bfloat16)
        lane = lax.broadcasted_iota(jnp.int32, (128, slots), 0)
        here = lane == i_ref[1:2, :]
        found = []
        for piece in pieces_of(dual):
            column = lax.dot_general(
                piece, pick, (((0,), (0,)), ((), ())), preferred_element_type=jnp.float32
            )
            found.append(jnp.sum(jnp.where(here, column, 0.0), axis=0, keepdims=True))
        blank = jnp.zeros((1, 128 - 3 * capacity), jnp.float32)
        for i in range(n_blk):
            part = slice(i * capacity, (i + 1) * capacity)
            out_ref[i, :capacity, :] = c_ref[part, :]
            row = jnp.concatenate([f[:, part] for f in found] + [blank], axis=1)
            out_ref[i, capacity:, :] = row.astype(jnp.bfloat16)

    return pl.pallas_call(
        kernel,
        out_shape=(
            jax.ShapeDtypeStruct((lines, 128), jnp.float32),
            jax.ShapeDtypeStruct((n_blk, capacity + 1, 128), jnp.bfloat16),
        ),
        in_specs=vmem(3),
        out_specs=tuple(vmem(2)),
        compiler_params=params(4),
        name="look_up",
    )(masses, ids, centres)


def prepare(tokens, row_ids, counts, duals):
    n_blk, capacity = row_ids.shape
    slots = n_blk * capacity
    tok, width = tokens.shape

    def kernel(n_ref, t_ref, r_ref, d_ref, row_ref, dual_ref, w_ref):
        w_ref[...] = jnp.zeros_like(w_ref)
        w_ref[:, :capacity] = r_ref[...].astype(jnp.float32)
        turned = jnp.transpose(w_ref[...])
        row = lax.broadcasted_iota(jnp.int32, (capacity, tok), 1).astype(jnp.float32)
        place = lax.broadcasted_iota(jnp.int32, (capacity, 1), 0)
        rows = t_ref[...]
        for i in range(n_blk):
            part = slice(i * capacity, (i + 1) * capacity)
            hit = row == turned[:capacity, i : i + 1]
            row_ref[part, :] = jnp.dot(
                jnp.where(hit, 1.0, 0.0).astype(jnp.bfloat16), rows, preferred_element_type=jnp.float32
            )
            dual = jnp.sum(jnp.where(hit, d_ref[...], 0.0), axis=1, keepdims=True)
            dual = jnp.where(place < n_ref[0, i], dual, dead)
            dual_ref[part, :] = jnp.broadcast_to(dual, (capacity, width))

    shape = jax.ShapeDtypeStruct((slots, width), jnp.float32)
    return pl.pallas_call(
        kernel,
        out_shape=(shape, shape),
        in_specs=[pl.BlockSpec(memory_space=pltpu.SMEM)] + vmem(3),
        out_specs=tuple(vmem(2)),
        scratch_shapes=[pltpu.VMEM((n_blk, 128), jnp.float32)],
        compiler_params=params(4),
        name="prepare",
    )(counts, tokens, row_ids, duals)


def finish(answers, rows, row_duals, scaling):
    n_blk, _, width = answers.shape
    capacity = rows.shape[0] // n_blk

    def kernel(g_ref, t_ref, d_ref, out_ref, w_ref):
        for i in range(n_blk):
            w_ref[i : i + 1, :] = g_ref[i, capacity:, :].astype(jnp.float32)
        pieces = w_ref[...]
        col_duals = pieces[:, :capacity]
        for k in range(1, 3):
            col_duals = col_duals + pieces[:, k * capacity : (k + 1) * capacity]
        w_ref[:, :capacity] = col_duals
        turned = jnp.transpose(w_ref[...])
        for i in range(n_blk):
            part = slice(i * capacity, (i + 1) * capacity)
            row = t_ref[part, :]
            centre = g_ref[i, :capacity, :].astype(jnp.float32)
            score = jnp.sum(row * centre, axis=1, keepdims=True) * scaling
            dual = d_ref[part, :]
            weight = jnp.where(dual > 0.1 * dead, jnp.exp(dual + (score + turned[:capacity, i : i + 1])), 0.0)
            out_ref[0, i] = weight * (row - centre)

    return pl.pallas_call(
        kernel,
        out_shape=jax.ShapeDtypeStruct((1, n_blk, capacity, width), jnp.float32),
        in_specs=vmem(3),
        out_specs=pl.BlockSpec(memory_space=pltpu.VMEM),
        scratch_shapes=[pltpu.VMEM((n_blk, 128), jnp.float32)],
        compiler_params=params(4),
        name="finish",
    )(answers, rows, row_duals)


def local(tokens, centroids, row_ids, alt_ids, counts):
    tok, width = tokens.shape
    slab = centroids.shape[0]
    n_blk = lax.axis_size("blk")
    n_wide = lax.axis_size("wide")
    scaling = score_gain / math.sqrt(width)
    capacity = alt_ids.shape[2]
    pairs = [[k, k + 1] for k in range(0, n_wide, 2)]
    same_core = [list(range(core, n_wide, 2)) for core in range(2)]

    gathered = exchange(jnp.broadcast_to(tokens[None], (n_blk, tok, width)), "blk")
    near = stage(centroids)
    parts = exchange(row_pass(gathered, near, alt_ids[0], tok, scaling), "blk")
    own_duals, mass = column_pass(gathered, near, parts, tok, scaling, slab * n_blk)
    mass = spread(lax.psum(mass, "wide", axis_index_groups=pairs), n_wide // 2)
    mass = add_up(exchange(mass, "wide", same_core))
    ids = unpack(parts, n_blk * tok, capacity)
    centres = near[ids[2]]
    rows, slot_duals = prepare(tokens, row_ids[0], counts, own_duals)
    mass, centres, rows, slot_duals = lax.optimization_barrier((mass, centres, rows, slot_duals))
    mass = lax.all_gather(mass, "wide", axis=0, axis_index_groups=pairs, tiled=True)
    col_duals, answers = look_up(mass, ids, centres, tok * n_blk * n_wide, n_blk, capacity)
    residuals = finish(exchange(answers, "blk"), rows, slot_duals, scaling)
    return (own_duals.reshape(tok), col_duals.reshape(slab), residuals)


def solution(mesh):
    in_specs = (
        P(("blk", "wide"), None),
        P("blk", None),
        P(("blk", "wide"), None, None),
        P(("blk", "wide"), None, None),
        P(("blk", "wide"), None),
    )
    out_specs = (P(("blk", "wide")), P("blk"), P(("blk", "wide"), None, None, None))
    return jax.shard_map(local, mesh=mesh, in_specs=in_specs, out_specs=out_specs, check_vma=False)
```

time: 115 us -> 102 us (0.89)
  starting transfers between devices: 35.8 us -> 21.3 us
  blocking collectives: 42.1 us -> 44 us
  local copies, waits for them, and re-layouts: 5.57 us -> 4.36 us
    all_to_all x3 -> x2, starting transfers between devices: 35.8 us -> 21.3 us  [exchange(): lax.all_to_all(x, axis, split_axis=0, concat_axis=0, axis_index_groups=gr...]
    all_to_all x3 -> x2, blocking collectives: 42.1 us -> 34.4 us  [exchange(): lax.all_to_all(x, axis, split_axis=0, concat_axis=0, axis_index_groups=gr...]
    psum x0 -> x1, blocking collectives: none -> 6.54 us  [local(): mass = spread(lax.psum(mass, 'wide', axis_index_groups=pairs), n_wide // 2)]
    all_gather x0 -> x1, blocking collectives: none -> 3.04 us  [local(): lax.all_gather(mass, 'wide', axis=0, axis_index_groups=pairs, tiled=True)]
    unnamed x16 -> x12, local copies, waits for them, and re-layouts: 3.66 us -> 1.61 us
    broadcast_in_dim x0 -> x1, local copies, waits for them, and re-layouts: none -> 1.41 us  [local(): jnp.broadcast_to(tokens[None], (n_blk, tok, width))]
    all_to_all x3 -> x2, waiting for transfers between devices: 16.2 us -> 17.1 us  [exchange(): lax.all_to_all(x, axis, split_axis=0, concat_axis=0, axis_index_groups=gr...]
    pallas_call x3 -> x5, Pallas kernels: 5.4 us -> 5.76 us  [the longest x1 4.7 us: row_pass(): pl.pallas_call(kernel, out_shape=jax.ShapeDtypeStruct((n_blk, 1, rows + 1...]
  transfers between devices with their start and end apart: 3 -> 2, of which waited for: 3 -> 2; matrix products, arithmetic and copies ran while one was open for 2% -> 1% of each run, Pallas kernels for 6% -> 2%
where the time goes in v3:
time: 102 us
  blocking collectives  44 us (43%)
  starting transfers between devices  21.3 us (21%)
  waiting for transfers between devices  17.1 us (17%)
  Pallas kernels  14.2 us (14%)
  local copies, waits for them, and re-layouts  4.36 us (4%)
    all_to_all x2, blocking collectives, exchange(): lax.all_to_all(x, axis, split_axis=0, concat_axis=0, axis_index_groups=gr...  34.4 us
    all_to_all x2, starting transfers between devices, exchange(): lax.all_to_all(x, axis, split_axis=0, concat_axis=0, axis_index_groups=gr...  21.3 us
    all_to_all x2, waiting for transfers between devices, exchange(): lax.all_to_all(x, axis, split_axis=0, concat_axis=0, axis_index_groups=gr...  17.1 us
    psum x1, blocking collectives, local(): mass = spread(lax.psum(mass, 'wide', axis_index_groups=pairs), n_wide // 2)  6.54 us
    pallas_call x1, Pallas kernels, row_pass(): pl.pallas_call(kernel, out_shape=jax.ShapeDtypeStruct((n_blk, 1, rows + 1...  4.7 us
    pallas_call x1, Pallas kernels, column_pass(): pl.pallas_call(kernel, out_shape=(jax.ShapeDtypeStruct((1, tok), jnp.floa...  4.25 us
    all_gather x1, blocking collectives, local(): lax.all_gather(mass, 'wide', axis=0, axis_index_groups=pairs, tiled=True)  3.04 us
    pallas_call x1, Pallas kernels, finish(): pl.pallas_call(kernel, out_shape=jax.ShapeDtypeStruct((1, n_blk, capacity...  2.1 us
  transfers between devices with their start and end apart: 2, of which 2 were waited for; matrix products, arithmetic and copies ran while one was open for 1% of the time, Pallas kernels for 2%

profile of v3, /device:TPU:1, one launch (start us, length us, event | category | flops | bytes accessed | tf_op | source)
XLA Modules:
  0.0 101.6 jit_solution(5626435086985550884)
XLA Ops:
  0.6 1.4 %broadcast_in_dim.2 = bf16[16,48,128]{2,1,0:T(8,128)(2,1)} broadcast(bf16[48,128]{1,0:T(8,128)(2,1)} %t_ref.1), dimensions={1,2} | broadcast | bytes 208896 | tf_op jit(solution)/shard_map/broadcast_in_dim | solution.py:371
  2.0 9.6 %all-to-all-start = ((bf16[16,48,128]{2,1,0:T(8,128)(2,1)}), bf16[16,48,128]{2,1,0:T(8,128)(2,1)S(1)}, u32[]{:S(2)}, u32[]{:S(2)}) async-start(bf16[16,48,128]{2,1,0:T(8,128)(2,1)} %broadcast_in_dim.2), calls=%async_computation | async-start | bytes 393216 | tf_op jit(solution)/shard_map/all_to_all | solution.py:25
  11.6 0.0 copy-start
  11.6 1.6 %copy-done = bf16[8192,128]{1,0:T(8,128)(2,1)S(1)} copy-done((bf16[8192,128]{1,0:T(8,128)(2,1)S(1)}, bf16[8192,128]{1,0:T(8,128)(2,1)}, u32[]{:S(2)}) %copy-start) | copy-done | bytes 2097176
  13.2 0.0 copy-start.2
  13.2 0.1 stage.1.c_ref
  13.4 7.5 %all-to-all-done.x_ref = bf16[16,48,128]{2,1,0:T(8,128)(2,1)S(1)} async-done(((bf16[16,48,128]{2,1,0:T(8,128)(2,1)}), bf16[16,48,128]{2,1,0:T(8,128)(2,1)S(1)}, u32[]{:S(2)}, u32[]{:S(2)}) %all-to-all-start) | async-done | bytes 196640 | tf_op jit(solution)/shard_map/all_to_all | solution.py:25
  20.9 0.0 copy-done.2
  20.9 4.7 %row_pass.1 = f32[16,1,896]{2,1,0:T(1,128)S(1)} custom-call(bf16[16,48,128]{2,1,0:T(8,128)(2,1)S(1)} %all-to-all-done.x_ref, bf16[8192,128]{1,0:T(8,128)(2,1)S(1)} %stage.1.c_ref, s32[16,32]{1,0:T(8,128)S(1)} %bitcast.9), custom_call_target="tpu_custom_call" | custom-call | tf_op jit(solution)/shard_map/row_pass/pallas_call | solution.py:123
  25.6 22.4 %all_to_all.20.l_ref.p_ref = f32[16,1,896]{2,1,0:T(1,128)S(1)} all-to-all(f32[16,1,896]{2,1,0:T(1,128)S(1)} %row_pass.1), channel_id=1, replica_groups=mesh['blk'=16,'wide'=32] {'blk'}, dimensions={0} | all-to-all | bytes 114688 | tf_op jit(solution)/shard_map/all_to_all | solution.py:25
  48.0 0.0 copy-start.1
  48.0 0.0 copy-start.3
  48.0 0.0 copy-start.4
  48.0 4.3 %column_pass.1 = (f32[1,48]{1,0:T(1,128)}, f32[64,128]{1,0:T(8,128)S(1)}) custom-call(bf16[16,48,128]{2,1,0:T(8,128)(2,1)S(1)} %all-to-all-done.x_ref, bf16[8192,128]{1,0:T(8,128)(2,1)S(1)} %stage.1.c_ref, f32[16,1,896]{2,1,0:T(1,128)S(1)} %all_to_all.20.l_ref.p_ref), custom_call_target="tpu_custom_call" | custom-call | tf_op jit(solution)/shard_map/column_pass/pallas_call | solution.py:198
  52.3 0.0 copy-start.5
  52.3 6.5 %psum.7.p_ref = f32[64,128]{1,0:T(8,128)S(1)} all-reduce(f32[64,128]{1,0:T(8,128)S(1)} %get-tuple-element.14), channel_id=1, replica_groups={{0,1},{2,3},{4,5},{6,7},{8,9},{10,11},{12,13},{14,15},{16,17},{18,19},{..., use_global_device_ids=true, to_apply=%region_0.0 | all-reduce | flops 8192 | bytes 65536 | tf_op jit(solution)/shard_map/psum | solution.py:375
  58.8 0.7 spread.1
  59.6 11.7 %all-to-all-start.2 = ((f32[16,32,128]{2,1,0:T(8,128)}), f32[16,32,128]{2,1,0:T(8,128)S(1)}, u32[]{:S(2)}, u32[]{:S(2)}) async-start(f32[16,32,128]{2,1,0:T(8,128)} %spread.1), calls=%async_computation.2 | async-start | bytes 524288 | tf_op jit(solution)/shard_map/all_to_all | solution.py:25
  71.3 0.2 unpack.1.i_ref
  71.5 1.3 %gather_fusion = bf16[512,128]{1,0:T(8,128)(2,1)S(1)} fusion(bf16[8192,128]{1,0:T(8,128)(2,1)S(1)} %stage.1.c_ref, s32[1024]{0:T(1024)S(1)} %pad_clamp_fusion), kind=kCustom, calls=%fused_computation | custom fusion | bytes 264192 | tf_op jit(solution)/shard_map/gather | solution.py:378
  72.8 0.0 copy-done.1
  72.8 0.0 copy-done.3
  72.8 0.0 copy-done.4
  72.8 0.0 copy-done.5
  72.8 1.4 %prepare.1 = (f32[512,128]{1,0:T(8,128)S(1)}, f32[512,128]{1,0:T(8,128)S(1)}) custom-call(s32[1,16]{1,0:T(1,128)S(1)} %copy-done.4, bf16[48,128]{1,0:T(8,128)(2,1)S(1)} %copy-done.1, s32[16,32]{1,0:T(8,128)S(1)} %bitcast.10, f32[1,48]{1,0:T(1,128)S(1)} %copy-done.5), custom_call_target="tpu_custom_call" | custom-call | tf_op jit(solution)/shard_map/prepare/pallas_call | solution.py:317
  74.3 9.6 %all-to-all-done.2.p_ref = f32[16,32,128]{2,1,0:T(8,128)S(1)} async-done(((f32[16,32,128]{2,1,0:T(8,128)}), f32[16,32,128]{2,1,0:T(8,128)S(1)}, u32[]{:S(2)}, u32[]{:S(2)}) %all-to-all-start.2) | async-done | bytes 262176 | tf_op jit(solution)/shard_map/all_to_all | solution.py:25
  83.9 3.0 %all_gather.3.m_ref = f32[64,128]{1,0:T(8,128)S(1)} all-gather(f32[32,128]{1,0:T(8,128)S(1)} %add_up.1), channel_id=1, replica_groups={{0,1},{2,3},{4,5},{6,7},{8,9},{10,11},{12,13},{14,15},{16,17},{18,19},{..., dimensions={0}, use_global_device_ids=true | all-gather | bytes 49152 | tf_op jit(solution)/shard_map/all_gather | solution.py:381
  86.9 0.6 look_up.1
  87.6 12.0 %all_to_all.21.g_ref = bf16[16,33,128]{2,1,0:T(8,128)(2,1)S(1)} all-to-all(bf16[16,33,128]{2,1,0:T(8,128)(2,1)S(1)} %get-tuple-element.20), channel_id=1, replica_groups=mesh['blk'=16,'wide'=32] {'blk'}, dimensions={0} | all-to-all | bytes 270336 | tf_op jit(solution)/shard_map/all_to_all | solution.py:25
  99.5 2.1 %finish.1 = f32[1,16,32,128]{3,2,1,0:T(8,128)} custom-call(bf16[16,33,128]{2,1,0:T(8,128)(2,1)S(1)} %all_to_all.21.g_ref, f32[512,128]{1,0:T(8,128)S(1)} %get-tuple-element.21.t_ref, f32[512,128]{1,0:T(8,128)S(1)} %get-tuple-element.22.d_ref), custom_call_target="tpu_custom_call" | custom-call | tf_op jit(solution)/shard_map/finish/pallas_call | solution.py:350
  (3 shorter events, 0.0 us)
Async XLA Ops:
  2.0 18.8 %all-to-all-start = ((bf16[16,48,128]{2,1,0:T(8,128)(2,1)}), bf16[16,48,128]{2,1,0:T(8,128)(2,1)S(1)}, u32[]{:S(2)}, u32[]{:S(2)}) async-start(bf16[16,48,128]{2,1,0:T(8,128)(2,1)} %broadcast_in_dim.2), calls=%async_computation | async-start | bytes 393216 | tf_op jit(solution)/shard_map/all_to_all | solution.py:25
  11.6 1.6 %copy-start = (bf16[8192,128]{1,0:T(8,128)(2,1)S(1)}, bf16[8192,128]{1,0:T(8,128)(2,1)}, u32[]{:S(2)}) copy-start(bf16[8192,128]{1,0:T(8,128)(2,1)} %x_ref.1) | copy-start | bytes 6291460
  13.2 7.7 %copy-start.2 = (s32[1,16,32]{2,1,0:T(8,128)S(1)}, s32[1,16,32]{2,1,0:T(8,128)}, u32[]{:S(2)}) copy-start(s32[1,16,32]{2,1,0:T(8,128)} %param.8) | copy-start | bytes 6148
  48.0 24.8 %copy-start.1 = (bf16[48,128]{1,0:T(8,128)(2,1)S(1)}, bf16[48,128]{1,0:T(8,128)(2,1)}, u32[]{:S(2)}) copy-start(bf16[48,128]{1,0:T(8,128)(2,1)} %t_ref.1) | copy-start | bytes 36868
  48.0 24.8 %copy-start.3 = (s32[1,16,32]{2,1,0:T(8,128)S(1)}, s32[1,16,32]{2,1,0:T(8,128)}, u32[]{:S(2)}) copy-start(s32[1,16,32]{2,1,0:T(8,128)} %param.7) | copy-start | bytes 6148
  48.0 24.8 %copy-start.4 = (s32[1,16]{1,0:T(1,128)S(1)}, s32[1,16]{1,0:T(1,128)}, u32[]{:S(2)}) copy-start(s32[1,16]{1,0:T(1,128)} %n_ref.1) | copy-start | bytes 196
  52.3 20.6 %copy-start.5 = (f32[1,48]{1,0:T(1,128)S(1)}, f32[1,48]{1,0:T(1,128)}, u32[]{:S(2)}) copy-start(f32[1,48]{1,0:T(1,128)} %get-tuple-element.13.d_ref) | copy-start | bytes 580
  59.6 24.3 %all-to-all-start.2 = ((f32[16,32,128]{2,1,0:T(8,128)}), f32[16,32,128]{2,1,0:T(8,128)S(1)}, u32[]{:S(2)}, u32[]{:S(2)}) async-start(f32[16,32,128]{2,1,0:T(8,128)} %spread.1), calls=%async_computation.2 | async-start | bytes 524288 | tf_op jit(solution)/shard_map/all_to_all | solution.py:25

commit v4 on v3

--- a/solution.py
+++ b/solution.py
@@ -47,16 +47,16 @@
     )(x)
 
 
-def row_pass(x, centroids, alt_ids, tok, scaling):
+def row_pass(x, centroids, alt_ids, row_ids, tok, scaling):
     n_blk = x.shape[0]
     rows = n_blk * tok
     capacity = alt_ids.shape[1]
     slab, width = centroids.shape
     factor = scaling * log2e
-    block = math.gcd(slab, 2048)
+    block = math.gcd(slab, 8192)
     small = math.gcd(slab, 256)
 
-    def kernel(x_ref, c_ref, i_ref, out_ref, t_ref, m_ref, a_ref):
+    def kernel(x_ref, c_ref, i_ref, r_ref, out_ref, t_ref, m_ref, a_ref):
         load_rows(x_ref, t_ref, n_blk, tok)
 
         def scores(start, size, lanes):
@@ -114,7 +114,7 @@
         lse = top * scaling + jnp.log(total)
         ids = i_ref[...]
         line = jnp.concatenate(
-            [ids >> 7, ids & 127, jnp.zeros((n_blk, 128 - 2 * capacity), jnp.int32)], axis=1
+            [ids >> 7, ids & 127, r_ref[...], jnp.zeros((n_blk, 128 - 3 * capacity), jnp.int32)], axis=1
         ).astype(jnp.float32)
         for i in range(n_blk):
             out_ref[i, :, :rows] = lse
@@ -123,7 +123,7 @@
     return pl.pallas_call(
         kernel,
         out_shape=jax.ShapeDtypeStruct((n_blk, 1, rows + 128), jnp.float32),
-        in_specs=vmem(3),
+        in_specs=vmem(4),
         out_specs=pl.BlockSpec(memory_space=pltpu.VMEM),
         scratch_shapes=[
             pltpu.VMEM((rows, width), jnp.bfloat16),
@@ -132,7 +132,7 @@
         ],
         compiler_params=params(16),
         name="row_pass",
-    )(x, centroids, alt_ids)
+    )(x, centroids, alt_ids, row_ids)
 
 
 def unpack(parts, rows, capacity):
@@ -161,15 +161,16 @@
     rows = n_blk * tok
     slab, width = centroids.shape
     block = 256
-    group = math.gcd(slab // block, 8)
+    group = math.gcd(slab // block, 32)
     factor = scaling * log2e
 
-    def kernel(x_ref, c_ref, l_ref, own_ref, mass_ref, t_ref, d_ref):
+    def kernel(x_ref, c_ref, l_ref, own_ref, dual_ref, mass_ref, t_ref, d_ref):
         load_rows(x_ref, t_ref, n_blk, tok)
         lse = l_ref[:, 0, :rows]
         top = jnp.max(lse, axis=0, keepdims=True)
         total = jnp.sum(jnp.exp(lse - top), axis=0, keepdims=True)
         dual = math.log(all_cols) - (top + jnp.log(total))
+        dual_ref[...] = dual
         position = lax.axis_index("blk")
         own = jnp.zeros((1, tok), jnp.float32)
         for i in range(n_blk):
@@ -199,10 +200,11 @@
         kernel,
         out_shape=(
             jax.ShapeDtypeStruct((1, tok), jnp.float32),
+            jax.ShapeDtypeStruct((1, rows), jnp.float32),
             jax.ShapeDtypeStruct((slab // 128, 128), jnp.float32),
         ),
         in_specs=vmem(3),
-        out_specs=tuple(vmem(2)),
+        out_specs=tuple(vmem(3)),
         scratch_shapes=[
             pltpu.VMEM((rows, width), jnp.bfloat16),
             pltpu.VMEM((rows, 128), jnp.float32),
@@ -212,12 +214,14 @@
     )(x, centroids, parts)
 
 
-def spread(pair_mass, copies):
-    half = pair_mass.shape[0] // 2
+def spread(both, copies):
+    lines = both.shape[0] // 2
+    half = lines // 2
 
     def kernel(p_ref, out_ref):
         core = lax.rem(lax.axis_index("wide"), 2)
-        part = p_ref[pl.ds(pl.multiple_of(core * half, half), half), :]
+        start = pl.multiple_of(core * half, half)
+        part = p_ref[pl.ds(start, half), :] + p_ref[pl.ds(lines + start, half), :]
         for j in range(copies):
             out_ref[j] = part
 
@@ -228,7 +232,7 @@
         out_specs=pl.BlockSpec(memory_space=pltpu.VMEM),
         compiler_params=params(4),
         name="spread",
-    )(pair_mass)
+    )(both)
 
 
 def add_up(parts):
@@ -254,28 +258,66 @@
     return pieces
 
 
-def look_up(masses, ids, centres, all_rows, n_blk, capacity):
+def ask_scores(x, centres, parts, duals, scaling):
+    n_blk, tok, width = x.shape
+    rows = n_blk * tok
+    capacity = centres.shape[0] // n_blk
+
+    def kernel(x_ref, c_ref, p_ref, d_ref, out_ref, w_ref):
+        for i in range(n_blk):
+            w_ref[i : i + 1, :] = p_ref[i, :, rows:]
+        turned = jnp.transpose(w_ref[...])[2 * capacity : 3 * capacity, :]
+        row = lax.broadcasted_iota(jnp.int32, (capacity, tok), 1).astype(jnp.float32)
+        lane = lax.broadcasted_iota(jnp.int32, (capacity, 128), 1)
+        table = jnp.zeros((capacity, 128), jnp.float32)
+        for i in range(n_blk):
+            hit = row == turned[:, i : i + 1]
+            picked = jnp.dot(
+                jnp.where(hit, 1.0, 0.0).astype(jnp.bfloat16), x_ref[i], preferred_element_type=jnp.float32
+            )
+            centre = c_ref[i * capacity : (i + 1) * capacity, :].astype(jnp.float32)
+            score = jnp.sum(picked * centre, axis=1, keepdims=True) * scaling
+            dual = jnp.where(hit, d_ref[:, i * tok : (i + 1) * tok], 0.0)
+            dual = jnp.sum(dual, axis=1, keepdims=True)
+            table = jnp.where(lane == i, score + dual, table)
+        table = jnp.transpose(table)
+        for i in range(n_blk):
+            out_ref[:, i * capacity : (i + 1) * capacity] = table[i : i + 1, :]
+
+    return pl.pallas_call(
+        kernel,
+        out_shape=jax.ShapeDtypeStruct((1, n_blk * capacity), jnp.float32),
+        in_specs=vmem(4),
+        out_specs=pl.BlockSpec(memory_space=pltpu.VMEM),
+        scratch_shapes=[pltpu.VMEM((n_blk, 128), jnp.float32)],
+        compiler_params=params(4),
+        name="ask_scores",
+    )(x, centres, parts, duals)
+
+
+def look_up(masses, ids, centres, sums, all_rows, n_blk, capacity):
     lines = masses.shape[0]
     slots = n_blk * capacity
 
-    def kernel(m_ref, i_ref, c_ref, dual_ref, out_ref):
+    def kernel(m_ref, i_ref, c_ref, s_ref, dual_ref, out_ref):
         dual = math.log(all_rows) - jnp.log(m_ref[...])
         dual_ref[...] = dual
         line = lax.broadcasted_iota(jnp.int32, (lines, slots), 0)
         pick = jnp.where(line == i_ref[0:1, :], 1.0, 0.0).astype(jnp.bfloat16)
         lane = lax.broadcasted_iota(jnp.int32, (128, slots), 0)
         here = lane == i_ref[1:2, :]
-        found = []
+        total = jnp.zeros((128, slots), jnp.float32)
         for piece in pieces_of(dual):
-            column = lax.dot_general(
+            total = total + lax.dot_general(
                 piece, pick, (((0,), (0,)), ((), ())), preferred_element_type=jnp.float32
             )
-            found.append(jnp.sum(jnp.where(here, column, 0.0), axis=0, keepdims=True))
+        total = jnp.sum(jnp.where(here, total, 0.0), axis=0, keepdims=True) + s_ref[...]
+        pieces = [piece.astype(jnp.float32) for piece in pieces_of(total)]
         blank = jnp.zeros((1, 128 - 3 * capacity), jnp.float32)
         for i in range(n_blk):
             part = slice(i * capacity, (i + 1) * capacity)
             out_ref[i, :capacity, :] = c_ref[part, :]
-            row = jnp.concatenate([f[:, part] for f in found] + [blank], axis=1)
+            row = jnp.concatenate([piece[:, part] for piece in pieces] + [blank], axis=1)
             out_ref[i, capacity:, :] = row.astype(jnp.bfloat16)
 
     return pl.pallas_call(
@@ -284,24 +326,24 @@
             jax.ShapeDtypeStruct((lines, 128), jnp.float32),
             jax.ShapeDtypeStruct((n_blk, capacity + 1, 128), jnp.bfloat16),
         ),
-        in_specs=vmem(3),
+        in_specs=vmem(4),
         out_specs=tuple(vmem(2)),
         compiler_params=params(4),
         name="look_up",
-    )(masses, ids, centres)
-
-
-def prepare(tokens, row_ids, counts, duals):
+    )(masses, ids, centres, sums)
+
+
+def prepare(tokens, row_ids, counts):
     n_blk, capacity = row_ids.shape
     slots = n_blk * capacity
     tok, width = tokens.shape
 
-    def kernel(n_ref, t_ref, r_ref, d_ref, row_ref, dual_ref, w_ref):
+    def kernel(n_ref, t_ref, r_ref, row_ref, live_ref, w_ref):
         w_ref[...] = jnp.zeros_like(w_ref)
         w_ref[:, :capacity] = r_ref[...].astype(jnp.float32)
         turned = jnp.transpose(w_ref[...])
         row = lax.broadcasted_iota(jnp.int32, (capacity, tok), 1).astype(jnp.float32)
-        place = lax.broadcasted_iota(jnp.int32, (capacity, 1), 0)
+        place = lax.broadcasted_iota(jnp.int32, (1, 128), 1)
         rows = t_ref[...]
         for i in range(n_blk):
             part = slice(i * capacity, (i + 1) * capacity)
@@ -309,43 +351,39 @@
             row_ref[part, :] = jnp.dot(
                 jnp.where(hit, 1.0, 0.0).astype(jnp.bfloat16), rows, preferred_element_type=jnp.float32
             )
-            dual = jnp.sum(jnp.where(hit, d_ref[...], 0.0), axis=1, keepdims=True)
-            dual = jnp.where(place < n_ref[0, i], dual, dead)
-            dual_ref[part, :] = jnp.broadcast_to(dual, (capacity, width))
-
-    shape = jax.ShapeDtypeStruct((slots, width), jnp.float32)
-    return pl.pallas_call(
-        kernel,
-        out_shape=(shape, shape),
-        in_specs=[pl.BlockSpec(memory_space=pltpu.SMEM)] + vmem(3),
+            live_ref[i : i + 1, :] = jnp.where(place < n_ref[0, i], 1.0, 0.0)
+
+    return pl.pallas_call(
+        kernel,
+        out_shape=(
+            jax.ShapeDtypeStruct((slots, width), jnp.float32),
+            jax.ShapeDtypeStruct((n_blk, 128), jnp.float32),
+        ),
+        in_specs=[pl.BlockSpec(memory_space=pltpu.SMEM)] + vmem(2),
         out_specs=tuple(vmem(2)),
         scratch_shapes=[pltpu.VMEM((n_blk, 128), jnp.float32)],
         compiler_params=params(4),
         name="prepare",
-    )(counts, tokens, row_ids, duals)
-
-
-def finish(answers, rows, row_duals, scaling):
+    )(counts, tokens, row_ids)
+
+
+def finish(answers, rows, live):
     n_blk, _, width = answers.shape
     capacity = rows.shape[0] // n_blk
 
-    def kernel(g_ref, t_ref, d_ref, out_ref, w_ref):
+    def kernel(g_ref, t_ref, v_ref, out_ref, w_ref):
         for i in range(n_blk):
             w_ref[i : i + 1, :] = g_ref[i, capacity:, :].astype(jnp.float32)
         pieces = w_ref[...]
-        col_duals = pieces[:, :capacity]
+        exponent = pieces[:, :capacity]
         for k in range(1, 3):
-            col_duals = col_duals + pieces[:, k * capacity : (k + 1) * capacity]
-        w_ref[:, :capacity] = col_duals
+            exponent = exponent + pieces[:, k * capacity : (k + 1) * capacity]
+        w_ref[:, :capacity] = jnp.where(v_ref[:, :capacity] > 0.0, jnp.exp(exponent), 0.0)
         turned = jnp.transpose(w_ref[...])
         for i in range(n_blk):
             part = slice(i * capacity, (i + 1) * capacity)
-            row = t_ref[part, :]
             centre = g_ref[i, :capacity, :].astype(jnp.float32)
-            score = jnp.sum(row * centre, axis=1, keepdims=True) * scaling
-            dual = d_ref[part, :]
-            weight = jnp.where(dual > 0.1 * dead, jnp.exp(dual + (score + turned[:capacity, i : i + 1])), 0.0)
-            out_ref[0, i] = weight * (row - centre)
+            out_ref[0, i] = turned[:capacity, i : i + 1] * (t_ref[part, :] - centre)
 
     return pl.pallas_call(
         kernel,
@@ -355,7 +393,25 @@
         scratch_shapes=[pltpu.VMEM((n_blk, 128), jnp.float32)],
         compiler_params=params(4),
         name="finish",
-    )(answers, rows, row_duals)
+    )(answers, rows, live)
+
+
+def copies(x, count):
+    def kernel(x_ref, out_ref, sems):
+        moves = [pltpu.make_async_copy(x_ref, out_ref.at[i], sems.at[i]) for i in range(count)]
+        for move in moves:
+            move.start()
+        for move in moves:
+            move.wait()
+
+    return pl.pallas_call(
+        kernel,
+        out_shape=jax.ShapeDtypeStruct((count,) + x.shape, x.dtype),
+        in_specs=[pl.BlockSpec(memory_space=pl.ANY)],
+        out_specs=pl.BlockSpec(memory_space=pl.ANY),
+        scratch_shapes=[pltpu.SemaphoreType.DMA((count,))],
+        name="copies",
+    )(x)
 
 
 def local(tokens, centroids, row_ids, alt_ids, counts):
@@ -368,19 +424,20 @@
     pairs = [[k, k + 1] for k in range(0, n_wide, 2)]
     same_core = [list(range(core, n_wide, 2)) for core in range(2)]
 
-    gathered = exchange(jnp.broadcast_to(tokens[None], (n_blk, tok, width)), "blk")
+    gathered = exchange(copies(tokens, n_blk), "blk")
     near = stage(centroids)
-    parts = exchange(row_pass(gathered, near, alt_ids[0], tok, scaling), "blk")
-    own_duals, mass = column_pass(gathered, near, parts, tok, scaling, slab * n_blk)
-    mass = spread(lax.psum(mass, "wide", axis_index_groups=pairs), n_wide // 2)
-    mass = add_up(exchange(mass, "wide", same_core))
+    parts = exchange(row_pass(gathered, near, alt_ids[0], row_ids[0], tok, scaling), "blk")
+    own_duals, duals, mass = column_pass(gathered, near, parts, tok, scaling, slab * n_blk)
+    both = lax.all_gather(mass, "wide", axis=0, axis_index_groups=pairs, tiled=True)
+    mass = add_up(exchange(spread(both, n_wide // 2), "wide", same_core))
     ids = unpack(parts, n_blk * tok, capacity)
     centres = near[ids[2]]
-    rows, slot_duals = prepare(tokens, row_ids[0], counts, own_duals)
-    mass, centres, rows, slot_duals = lax.optimization_barrier((mass, centres, rows, slot_duals))
+    sums = ask_scores(gathered, centres, parts, duals, scaling)
+    rows, live = prepare(tokens, row_ids[0], counts)
+    mass, sums, rows, live = lax.optimization_barrier((mass, sums, rows, live))
     mass = lax.all_gather(mass, "wide", axis=0, axis_index_groups=pairs, tiled=True)
-    col_duals, answers = look_up(mass, ids, centres, tok * n_blk * n_wide, n_blk, capacity)
-    residuals = finish(exchange(answers, "blk"), rows, slot_duals, scaling)
+    col_duals, answers = look_up(mass, ids, centres, sums, tok * n_blk * n_wide, n_blk, capacity)
+    residuals = finish(exchange(answers, "blk"), rows, live)
     return (own_duals.reshape(tok), col_duals.reshape(slab), residuals)
 
 

time: 102 us -> 104 us (1.020)
  Pallas kernels: 14.2 us -> 21.7 us
  waiting for transfers between devices: 17.1 us -> 14.7 us
  blocking collectives: 44 us -> 42.3 us
  local copies, waits for them, and re-layouts: 4.36 us -> 2.95 us
    pallas_call x1 -> x3, Pallas kernels: 1.45 us -> 10.9 us  [the longest x1 7.21 us: copies(): pl.pallas_call(kernel, out_shape=jax.ShapeDtypeStruct((count,) + x.shape,...]
    psum x1 -> x0, blocking collectives: 6.54 us -> none  [local(): mass = spread(lax.psum(mass, 'wide', axis_index_groups=pairs), n_wide // 2)]
    all_gather x1 -> x2, blocking collectives: 3.04 us -> 7.91 us  [local(): lax.all_gather(mass, 'wide', axis=0, axis_index_groups=pairs, tiled=True)]
    all_to_all x2, waiting for transfers between devices: 17.1 us -> 14.7 us  [exchange(): lax.all_to_all(x, axis, split_axis=0, concat_axis=0, axis_index_groups=gr...]
    broadcast_in_dim x1 -> x0, local copies, waits for them, and re-layouts: 1.41 us -> none  [local(): jnp.broadcast_to(tokens[None], (n_blk, tok, width))]
    pallas_call x1, Pallas kernels: 2.1 us -> 1.03 us  [finish(): pl.pallas_call(kernel, out_shape=jax.ShapeDtypeStruct((1, n_blk, capacity...]
  transfers between devices with their start and end apart: 2 -> 2, of which waited for: 2 -> 2; matrix products, arithmetic and copies ran while one was open for 1% -> 1% of each run, Pallas kernels for 2% -> 4%
where the time goes in v4:
time: 104 us
  blocking collectives  42.3 us (41%)
  Pallas kernels  21.7 us (21%)
  starting transfers between devices  21.2 us (20%)
  waiting for transfers between devices  14.7 us (14%)
  local copies, waits for them, and re-layouts  2.95 us (3%)
    all_to_all x2, blocking collectives, exchange(): lax.all_to_all(x, axis, split_axis=0, concat_axis=0, axis_index_groups=gr...  34.4 us
    all_to_all x2, starting transfers between devices, exchange(): lax.all_to_all(x, axis, split_axis=0, concat_axis=0, axis_index_groups=gr...  21.2 us
    all_to_all x2, waiting for transfers between devices, exchange(): lax.all_to_all(x, axis, split_axis=0, concat_axis=0, axis_index_groups=gr...  14.7 us
    all_gather x2, blocking collectives, local(): lax.all_gather(mass, 'wide', axis=0, axis_index_groups=pairs, tiled=True)  7.91 us
    pallas_call x1, Pallas kernels, copies(): pl.pallas_call(kernel, out_shape=jax.ShapeDtypeStruct((count,) + x.shape,...  7.21 us
    pallas_call x1, Pallas kernels, column_pass(): pl.pallas_call(kernel, out_shape=(jax.ShapeDtypeStruct((1, tok), jnp.floa...  4.15 us
    pallas_call x1, Pallas kernels, row_pass(): pl.pallas_call(kernel, out_shape=jax.ShapeDtypeStruct((n_blk, 1, rows + 1...  3.97 us
    pallas_call x1, Pallas kernels, ask_scores(): pl.pallas_call(kernel, out_shape=jax.ShapeDtypeStruct((1, n_blk * capacit...  2.79 us
  transfers between devices with their start and end apart: 2, of which 2 were waited for; matrix products, arithmetic and copies ran while one was open for 1% of the time, Pallas kernels for 4%

profile of v4, /device:TPU:1, one launch (start us, length us, event | category | flops | bytes accessed | tf_op | source)
XLA Modules:
  0.0 103.7 jit_solution(5144905357767048883)
XLA Ops:
  0.6 7.2 %copies.1 = bf16[16,48,128]{2,1,0:T(8,128)(2,1)} custom-call(bf16[48,128]{1,0:T(8,128)(2,1)} %t_ref.1), custom_call_target="tpu_custom_call" | custom-call | tf_op jit(solution)/shard_map/copies/pallas_call | solution.py:407
  7.8 9.6 %all-to-all-start = ((bf16[16,48,128]{2,1,0:T(8,128)(2,1)}), bf16[16,48,128]{2,1,0:T(8,128)(2,1)S(1)}, u32[]{:S(2)}, u32[]{:S(2)}) async-start(bf16[16,48,128]{2,1,0:T(8,128)(2,1)} %copies.1), calls=%async_computation | async-start | bytes 393216 | tf_op jit(solution)/shard_map/all_to_all | solution.py:25
  17.4 0.0 copy-start
  17.4 1.6 %copy-done = bf16[8192,128]{1,0:T(8,128)(2,1)S(1)} copy-done((bf16[8192,128]{1,0:T(8,128)(2,1)S(1)}, bf16[8192,128]{1,0:T(8,128)(2,1)}, u32[]{:S(2)}) %copy-start) | copy-done | bytes 2097176
  19.0 0.0 copy-start.2
  19.0 0.0 copy-start.3
  19.0 0.1 stage.1.c_ref
  19.2 7.5 %all-to-all-done.x_ref = bf16[16,48,128]{2,1,0:T(8,128)(2,1)S(1)} async-done(((bf16[16,48,128]{2,1,0:T(8,128)(2,1)}), bf16[16,48,128]{2,1,0:T(8,128)(2,1)S(1)}, u32[]{:S(2)}, u32[]{:S(2)}) %all-to-all-start) | async-done | bytes 196640 | tf_op jit(solution)/shard_map/all_to_all | solution.py:25
  26.7 0.0 copy-done.2
  26.7 0.0 copy-done.3
  26.7 4.0 %row_pass.1 = f32[16,1,896]{2,1,0:T(1,128)S(1)} custom-call(bf16[16,48,128]{2,1,0:T(8,128)(2,1)S(1)} %all-to-all-done.x_ref, bf16[8192,128]{1,0:T(8,128)(2,1)S(1)} %stage.1.c_ref, s32[16,32]{1,0:T(8,128)S(1)} %bitcast.11, s32[16,32]{1,0:T(8,128)S(1)} %bitcast.9), custom_call_target="tpu_custom_call" | custom-call | tf_op jit(solution)/shard_map/row_pass/pallas_call | solution.py:123
  30.7 0.0 copy-start.1
  30.7 0.0 copy-start.4
  30.7 22.4 %all_to_all.20.l_ref.p_ref = f32[16,1,896]{2,1,0:T(1,128)S(1)} all-to-all(f32[16,1,896]{2,1,0:T(1,128)S(1)} %row_pass.1), channel_id=1, replica_groups=mesh['blk'=16,'wide'=32] {'blk'}, dimensions={0} | all-to-all | bytes 114688 | tf_op jit(solution)/shard_map/all_to_all | solution.py:25
  53.1 4.2 %column_pass.1 = (f32[1,48]{1,0:T(1,128)}, f32[1,768]{1,0:T(1,128)S(1)}, f32[64,128]{1,0:T(8,128)S(1)}) custom-call(bf16[16,48,128]{2,1,0:T(8,128)(2,1)S(1)} %all-to-all-done.x_ref, bf16[8192,128]{1,0:T(8,128)(2,1)S(1)} %stage.1.c_ref, f32[16,1,896]{2,1,0:T(1,128)S(1)} %all_to_all.20.l_ref.p_ref), custom_call_target="tpu_custom_call" | custom-call | tf_op jit(solution)/shard_map/column_pass/pallas_call | solution.py:199
  57.3 4.8 %all_gather.6.p_ref = f32[128,128]{1,0:T(8,128)S(1)} all-gather(f32[64,128]{1,0:T(8,128)S(1)} %get-tuple-element.15), channel_id=1, replica_groups={{0,1},{2,3},{4,5},{6,7},{8,9},{10,11},{12,13},{14,15},{16,17},{18,19},{..., dimensions={0}, use_global_device_ids=true | all-gather | bytes 98304 | tf_op jit(solution)/shard_map/all_gather | solution.py:431
  62.1 0.7 spread.1
  62.8 11.7 %all-to-all-start.2 = ((f32[16,32,128]{2,1,0:T(8,128)}), f32[16,32,128]{2,1,0:T(8,128)S(1)}, u32[]{:S(2)}, u32[]{:S(2)}) async-start(f32[16,32,128]{2,1,0:T(8,128)} %spread.1), calls=%async_computation.2 | async-start | bytes 524288 | tf_op jit(solution)/shard_map/all_to_all | solution.py:25
  74.5 0.0 copy-done.1
  74.5 0.0 copy-done.4
  74.5 0.9 prepare.1
  75.4 0.2 unpack.1.i_ref
  75.6 1.3 %gather_fusion = bf16[512,128]{1,0:T(8,128)(2,1)S(1)} fusion(bf16[8192,128]{1,0:T(8,128)(2,1)S(1)} %stage.1.c_ref, s32[1024]{0:T(1024)S(1)} %pad_clamp_fusion), kind=kCustom, calls=%fused_computation | custom fusion | bytes 264192 | tf_op jit(solution)/shard_map/gather | solution.py:434
  77.0 2.8 %ask_scores.1.s_ref = f32[1,512]{1,0:T(1,128)S(1)} custom-call(bf16[16,48,128]{2,1,0:T(8,128)(2,1)S(1)} %all-to-all-done.x_ref, bf16[512,128]{1,0:T(8,128)(2,1)S(1)} %gather_fusion, f32[16,1,896]{2,1,0:T(1,128)S(1)} %all_to_all.20.l_ref.p_ref, f32[1,768]{1,0:T(1,128)S(1)} %get-tuple-element.16.d_ref), custom_call_target="tpu_custom_call" | custom-call | tf_op jit(solution)/shard_map/ask_scores/pallas_call | solution.py:287
  79.8 7.2 %all-to-all-done.2.p_ref = f32[16,32,128]{2,1,0:T(8,128)S(1)} async-done(((f32[16,32,128]{2,1,0:T(8,128)}), f32[16,32,128]{2,1,0:T(8,128)S(1)}, u32[]{:S(2)}, u32[]{:S(2)}) %all-to-all-start.2) | async-done | bytes 262176 | tf_op jit(solution)/shard_map/all_to_all | solution.py:25
  87.0 3.1 %all_gather.7.m_ref = f32[64,128]{1,0:T(8,128)S(1)} all-gather(f32[32,128]{1,0:T(8,128)S(1)} %add_up.1), channel_id=1, replica_groups={{0,1},{2,3},{4,5},{6,7},{8,9},{10,11},{12,13},{14,15},{16,17},{18,19},{..., dimensions={0}, use_global_device_ids=true | all-gather | bytes 49152 | tf_op jit(solution)/shard_map/all_gather | solution.py:438
  90.1 0.6 look_up.1
  90.8 12.0 %all_to_all.21.g_ref = bf16[16,33,128]{2,1,0:T(8,128)(2,1)S(1)} all-to-all(bf16[16,33,128]{2,1,0:T(8,128)(2,1)S(1)} %get-tuple-element.22), channel_id=1, replica_groups=mesh['blk'=16,'wide'=32] {'blk'}, dimensions={0} | all-to-all | bytes 270336 | tf_op jit(solution)/shard_map/all_to_all | solution.py:25
  102.7 1.0 finish.1
  (3 shorter events, 0.0 us)
Async XLA Ops:
  7.8 18.8 %all-to-all-start = ((bf16[16,48,128]{2,1,0:T(8,128)(2,1)}), bf16[16,48,128]{2,1,0:T(8,128)(2,1)S(1)}, u32[]{:S(2)}, u32[]{:S(2)}) async-start(bf16[16,48,128]{2,1,0:T(8,128)(2,1)} %copies.1), calls=%async_computation | async-start | bytes 393216 | tf_op jit(solution)/shard_map/all_to_all | solution.py:25
  17.4 1.6 %copy-start = (bf16[8192,128]{1,0:T(8,128)(2,1)S(1)}, bf16[8192,128]{1,0:T(8,128)(2,1)}, u32[]{:S(2)}) copy-start(bf16[8192,128]{1,0:T(8,128)(2,1)} %x_ref.3) | copy-start | bytes 6291460
  19.0 7.7 %copy-start.2 = (s32[1,16,32]{2,1,0:T(8,128)S(1)}, s32[1,16,32]{2,1,0:T(8,128)}, u32[]{:S(2)}) copy-start(s32[1,16,32]{2,1,0:T(8,128)} %param.7) | copy-start | bytes 6148
  19.0 7.7 %copy-start.3 = (s32[1,16,32]{2,1,0:T(8,128)S(1)}, s32[1,16,32]{2,1,0:T(8,128)}, u32[]{:S(2)}) copy-start(s32[1,16,32]{2,1,0:T(8,128)} %param.8) | copy-start | bytes 6148
  30.7 43.8 %copy-start.1 = (bf16[48,128]{1,0:T(8,128)(2,1)S(1)}, bf16[48,128]{1,0:T(8,128)(2,1)}, u32[]{:S(2)}) copy-start(bf16[48,128]{1,0:T(8,128)(2,1)} %t_ref.1) | copy-start | bytes 36868
  30.7 43.8 %copy-start.4 = (s32[1,16]{1,0:T(1,128)S(1)}, s32[1,16]{1,0:T(1,128)}, u32[]{:S(2)}) copy-start(s32[1,16]{1,0:T(1,128)} %n_ref.1) | copy-start | bytes 196
  62.8 24.2 %all-to-all-start.2 = ((f32[16,32,128]{2,1,0:T(8,128)}), f32[16,32,128]{2,1,0:T(8,128)S(1)}, u32[]{:S(2)}, u32[]{:S(2)}) async-start(f32[16,32,128]{2,1,0:T(8,128)} %spread.1), calls=%async_computation.2 | async-start | bytes 524288 | tf_op jit(solution)/shard_map/all_to_all | solution.py:25

commit v5 on v4

--- a/solution.py
+++ b/solution.py
@@ -29,22 +29,32 @@
     return pltpu.CompilerParams(vmem_limit_bytes=mib << 20)
 
 
-def stage(x):
-    def kernel(x_ref, out_ref, sem):
-        copy = pltpu.make_async_copy(x_ref, out_ref, sem)
-        copy.start()
-        copy.wait()
-
-    return pl.pallas_call(
-        kernel,
-        out_shape=jax.ShapeDtypeStruct(x.shape, x.dtype),
-        in_specs=[pl.BlockSpec(memory_space=pl.ANY)],
-        out_specs=pl.BlockSpec(memory_space=pltpu.VMEM),
-        scratch_shapes=[pltpu.SemaphoreType.DMA],
-        compiler_params=params(4),
-        cost_estimate=pl.CostEstimate(flops=0, transcendentals=0, bytes_accessed=2 * x.size * x.dtype.itemsize),
+def stage(tokens, centroids, count):
+    tok, width = tokens.shape
+
+    def kernel(t_ref, c_ref, copies_ref, near_ref, t_scr, sems):
+        first = pltpu.make_async_copy(t_ref, t_scr, sems.at[0])
+        second = pltpu.make_async_copy(c_ref, near_ref, sems.at[1])
+        first.start()
+        second.start()
+        first.wait()
+        rows = t_scr[...]
+        for i in range(count):
+            copies_ref[i] = rows
+        second.wait()
+
+    return pl.pallas_call(
+        kernel,
+        out_shape=(
+            pltpu.VMEM((count, tok, width), tokens.dtype),
+            pltpu.VMEM(centroids.shape, centroids.dtype),
+        ),
+        in_specs=[pl.BlockSpec(memory_space=pltpu.HBM)] * 2,
+        out_specs=tuple(vmem(2)),
+        scratch_shapes=[pltpu.VMEM((tok, width), tokens.dtype), pltpu.SemaphoreType.DMA((2,))],
+        compiler_params=params(56),
         name="stage",
-    )(x)
+    )(tokens, centroids)
 
 
 def row_pass(x, centroids, alt_ids, row_ids, tok, scaling):
@@ -396,24 +406,6 @@
     )(answers, rows, live)
 
 
-def copies(x, count):
-    def kernel(x_ref, out_ref, sems):
-        moves = [pltpu.make_async_copy(x_ref, out_ref.at[i], sems.at[i]) for i in range(count)]
-        for move in moves:
-            move.start()
-        for move in moves:
-            move.wait()
-
-    return pl.pallas_call(
-        kernel,
-        out_shape=jax.ShapeDtypeStruct((count,) + x.shape, x.dtype),
-        in_specs=[pl.BlockSpec(memory_space=pl.ANY)],
-        out_specs=pl.BlockSpec(memory_space=pl.ANY),
-        scratch_shapes=[pltpu.SemaphoreType.DMA((count,))],
-        name="copies",
-    )(x)
-
-
 def local(tokens, centroids, row_ids, alt_ids, counts):
     tok, width = tokens.shape
     slab = centroids.shape[0]
@@ -424,8 +416,8 @@
     pairs = [[k, k + 1] for k in range(0, n_wide, 2)]
     same_core = [list(range(core, n_wide, 2)) for core in range(2)]
 
-    gathered = exchange(copies(tokens, n_blk), "blk")
-    near = stage(centroids)
+    outgoing, near = stage(tokens, centroids, n_blk)
+    gathered = exchange(outgoing, "blk")
     parts = exchange(row_pass(gathered, near, alt_ids[0], row_ids[0], tok, scaling), "blk")
     own_duals, duals, mass = column_pass(gathered, near, parts, tok, scaling, slab * n_blk)
     both = lax.all_gather(mass, "wide", axis=0, axis_index_groups=pairs, tiled=True)

time: 104 us -> 98.4 us (0.946)
  blocking collectives: 42.3 us -> 60.8 us
  starting transfers between devices: 21.2 us -> 11.7 us
  waiting for transfers between devices: 14.7 us -> 7.38 us
  Pallas kernels: 21.7 us -> 16 us
  local copies, waits for them, and re-layouts: 2.95 us -> 1.36 us
    all_to_all x2 -> x3, blocking collectives: 34.4 us -> 53 us  [exchange(): lax.all_to_all(x, axis, split_axis=0, concat_axis=0, axis_index_groups=gr...]
    all_to_all x2 -> x1, starting transfers between devices: 21.2 us -> 11.7 us  [exchange(): lax.all_to_all(x, axis, split_axis=0, concat_axis=0, axis_index_groups=gr...]
    all_to_all x2 -> x1, waiting for transfers between devices: 14.7 us -> 7.38 us  [exchange(): lax.all_to_all(x, axis, split_axis=0, concat_axis=0, axis_index_groups=gr...]
    pallas_call x2 -> x1, Pallas kernels: 7.36 us -> 1.64 us  [stage(): pl.pallas_call(kernel, out_shape=(pltpu.VMEM((count, tok, width), tokens....]
    unnamed x10 -> x8, local copies, waits for them, and re-layouts: 1.61 us -> 0.02 us
  transfers between devices with their start and end apart: 2 -> 1, of which waited for: 2 -> 1; matrix products, arithmetic and copies ran while one was open for 1% -> 1% of each run, Pallas kernels for 4% -> 4%
where the time goes in v5:
time: 98.4 us; the launch traced here: 98 us
  blocking collectives  60.8 us (62%)
  Pallas kernels  16 us (16%)
  starting transfers between devices  11.7 us (12%)
  waiting for transfers between devices  7.38 us (8%)
  local copies, waits for them, and re-layouts  1.36 us (1%)
    all_to_all x3, blocking collectives, exchange(): lax.all_to_all(x, axis, split_axis=0, concat_axis=0, axis_index_groups=gr...  53 us
    all_to_all x1, starting transfers between devices, exchange(): lax.all_to_all(x, axis, split_axis=0, concat_axis=0, axis_index_groups=gr...  11.7 us
    all_gather x2, blocking collectives, local(): lax.all_gather(mass, 'wide', axis=0, axis_index_groups=pairs, tiled=True)  7.74 us
    all_to_all x1, waiting for transfers between devices, exchange(): lax.all_to_all(x, axis, split_axis=0, concat_axis=0, axis_index_groups=gr...  7.38 us
    pallas_call x1, Pallas kernels, column_pass(): pl.pallas_call(kernel, out_shape=(jax.ShapeDtypeStruct((1, tok), jnp.floa...  4.15 us
    pallas_call x1, Pallas kernels, row_pass(): pl.pallas_call(kernel, out_shape=jax.ShapeDtypeStruct((n_blk, 1, rows + 1...  3.97 us
    pallas_call x1, Pallas kernels, ask_scores(): pl.pallas_call(kernel, out_shape=jax.ShapeDtypeStruct((1, n_blk * capacit...  2.79 us
  transfers between devices with their start and end apart: 1, of which 1 were waited for; matrix products, arithmetic and copies ran while one was open for 1% of the time, Pallas kernels for 4%

profile of v5, /device:TPU:1, one launch (start us, length us, event | category | flops | bytes accessed | tf_op | source)
XLA Modules:
  0.0 98.0 jit_solution(3095561168066726992)
XLA Ops:
  0.6 0.0 copy-start.1
  0.6 0.0 copy-start.2
  0.7 1.6 %stage.1 = (bf16[16,48,128]{2,1,0:T(8,128)(2,1)S(1)}, bf16[8192,128]{1,0:T(8,128)(2,1)S(1)}) custom-call(bf16[48,128]{1,0:T(8,128)(2,1)} %t_ref.3, bf16[8192,128]{1,0:T(8,128)(2,1)} %c_ref.1), custom_call_target="tpu_custom_call" | custom-call | tf_op jit(solution)/shard_map/stage/pallas_call | solution.py:46
  2.3 18.6 %all_to_all.20.x_ref = bf16[16,48,128]{2,1,0:T(8,128)(2,1)S(1)} all-to-all(bf16[16,48,128]{2,1,0:T(8,128)(2,1)S(1)} %get-tuple-element.16), channel_id=1, replica_groups=mesh['blk'=16,'wide'=32] {'blk'}, dimensions={0} | all-to-all | bytes 393216 | tf_op jit(solution)/shard_map/all_to_all | solution.py:25
  20.9 0.0 copy-done.1
  20.9 0.0 copy-done.2
  20.9 4.0 %row_pass.1 = f32[16,1,896]{2,1,0:T(1,128)S(1)} custom-call(bf16[16,48,128]{2,1,0:T(8,128)(2,1)S(1)} %all_to_all.20.x_ref, bf16[8192,128]{1,0:T(8,128)(2,1)S(1)} %get-tuple-element.17.c_ref, s32[16,32]{1,0:T(8,128)S(1)} %bitcast.11, s32[16,32]{1,0:T(8,128)S(1)} %bitcast.9), custom_call_target="tpu_custom_call" | custom-call | tf_op jit(solution)/shard_map/row_pass/pallas_call | solution.py:133
  24.9 0.0 copy-start
  24.9 0.0 copy-start.3
  24.9 22.4 %all_to_all.21.l_ref.p_ref = f32[16,1,896]{2,1,0:T(1,128)S(1)} all-to-all(f32[16,1,896]{2,1,0:T(1,128)S(1)} %row_pass.1), channel_id=1, replica_groups=mesh['blk'=16,'wide'=32] {'blk'}, dimensions={0} | all-to-all | bytes 114688 | tf_op jit(solution)/shard_map/all_to_all | solution.py:25
  47.4 4.2 %column_pass.1 = (f32[1,48]{1,0:T(1,128)}, f32[1,768]{1,0:T(1,128)S(1)}, f32[64,128]{1,0:T(8,128)S(1)}) custom-call(bf16[16,48,128]{2,1,0:T(8,128)(2,1)S(1)} %all_to_all.20.x_ref, bf16[8192,128]{1,0:T(8,128)(2,1)S(1)} %get-tuple-element.17.c_ref, f32[16,1,896]{2,1,0:T(1,128)S(1)} %all_to_all.21.l_ref.p_ref), custom_call_target="tpu_custom_call" | custom-call | tf_op jit(solution)/shard_map/column_pass/pallas_call | solution.py:209
  51.5 4.8 %all_gather.6.p_ref = f32[128,128]{1,0:T(8,128)S(1)} all-gather(f32[64,128]{1,0:T(8,128)S(1)} %get-tuple-element.19), channel_id=1, replica_groups={{0,1},{2,3},{4,5},{6,7},{8,9},{10,11},{12,13},{14,15},{16,17},{18,19},{..., dimensions={0}, use_global_device_ids=true | all-gather | bytes 98304 | tf_op jit(solution)/shard_map/all_gather | solution.py:423
  56.3 0.7 spread.1
  57.0 11.7 %all-to-all-start.2 = ((f32[16,32,128]{2,1,0:T(8,128)}), f32[16,32,128]{2,1,0:T(8,128)S(1)}, u32[]{:S(2)}, u32[]{:S(2)}) async-start(f32[16,32,128]{2,1,0:T(8,128)} %spread.1), calls=%async_computation.2 | async-start | bytes 524288 | tf_op jit(solution)/shard_map/all_to_all | solution.py:25
  68.7 0.0 copy-done
  68.8 0.0 copy-done.3
  68.8 0.9 prepare.1
  69.7 0.2 unpack.1.i_ref
  69.9 1.3 %gather_fusion = bf16[512,128]{1,0:T(8,128)(2,1)S(1)} fusion(bf16[8192,128]{1,0:T(8,128)(2,1)S(1)} %get-tuple-element.17.c_ref, s32[1024]{0:T(1024)S(1)} %pad_clamp_fusion), kind=kCustom, calls=%fused_computation | custom fusion | bytes 264192 | tf_op jit(solution)/shard_map/gather | solution.py:426
  71.2 2.8 %ask_scores.1.s_ref = f32[1,512]{1,0:T(1,128)S(1)} custom-call(bf16[16,48,128]{2,1,0:T(8,128)(2,1)S(1)} %all_to_all.20.x_ref, bf16[512,128]{1,0:T(8,128)(2,1)S(1)} %gather_fusion, f32[16,1,896]{2,1,0:T(1,128)S(1)} %all_to_all.21.l_ref.p_ref, f32[1,768]{1,0:T(1,128)S(1)} %get-tuple-element.20.d_ref), custom_call_target="tpu_custom_call" | custom-call | tf_op jit(solution)/shard_map/ask_scores/pallas_call | solution.py:297
  74.0 7.4 %all-to-all-done.2.p_ref = f32[16,32,128]{2,1,0:T(8,128)S(1)} async-done(((f32[16,32,128]{2,1,0:T(8,128)}), f32[16,32,128]{2,1,0:T(8,128)S(1)}, u32[]{:S(2)}, u32[]{:S(2)}) %all-to-all-start.2) | async-done | bytes 262176 | tf_op jit(solution)/shard_map/all_to_all | solution.py:25
  81.4 3.0 %all_gather.7.m_ref = f32[64,128]{1,0:T(8,128)S(1)} all-gather(f32[32,128]{1,0:T(8,128)S(1)} %add_up.1), channel_id=1, replica_groups={{0,1},{2,3},{4,5},{6,7},{8,9},{10,11},{12,13},{14,15},{16,17},{18,19},{..., dimensions={0}, use_global_device_ids=true | all-gather | bytes 49152 | tf_op jit(solution)/shard_map/all_gather | solution.py:430
  84.4 0.6 look_up.1
  85.0 12.0 %all_to_all.22.g_ref = bf16[16,33,128]{2,1,0:T(8,128)(2,1)S(1)} all-to-all(bf16[16,33,128]{2,1,0:T(8,128)(2,1)S(1)} %get-tuple-element.26), channel_id=1, replica_groups=mesh['blk'=16,'wide'=32] {'blk'}, dimensions={0} | all-to-all | bytes 270336 | tf_op jit(solution)/shard_map/all_to_all | solution.py:25
  97.0 1.0 %finish.1 = f32[1,16,32,128]{3,2,1,0:T(8,128)} custom-call(bf16[16,33,128]{2,1,0:T(8,128)(2,1)S(1)} %all_to_all.22.g_ref, f32[512,128]{1,0:T(8,128)S(1)} %get-tuple-element.27.t_ref, f32[16,128]{1,0:T(8,128)S(1)} %get-tuple-element.28.v_ref), custom_call_target="tpu_custom_call" | custom-call | tf_op jit(solution)/shard_map/finish/pallas_call | solution.py:398
  (3 shorter events, 0.0 us)
Async XLA Ops:
  0.6 20.3 %copy-start.1 = (s32[1,16,32]{2,1,0:T(8,128)S(1)}, s32[1,16,32]{2,1,0:T(8,128)}, u32[]{:S(2)}) copy-start(s32[1,16,32]{2,1,0:T(8,128)} %param.7) | copy-start | bytes 6148
  0.6 20.3 %copy-start.2 = (s32[1,16,32]{2,1,0:T(8,128)S(1)}, s32[1,16,32]{2,1,0:T(8,128)}, u32[]{:S(2)}) copy-start(s32[1,16,32]{2,1,0:T(8,128)} %param.8) | copy-start | bytes 6148
  24.9 43.8 %copy-start = (bf16[48,128]{1,0:T(8,128)(2,1)S(1)}, bf16[48,128]{1,0:T(8,128)(2,1)}, u32[]{:S(2)}) copy-start(bf16[48,128]{1,0:T(8,128)(2,1)} %t_ref.3) | copy-start | bytes 36868
  24.9 43.8 %copy-start.3 = (s32[1,16]{1,0:T(1,128)S(1)}, s32[1,16]{1,0:T(1,128)}, u32[]{:S(2)}) copy-start(s32[1,16]{1,0:T(1,128)} %n_ref.1) | copy-start | bytes 196
  57.0 24.3 %all-to-all-start.2 = ((f32[16,32,128]{2,1,0:T(8,128)}), f32[16,32,128]{2,1,0:T(8,128)S(1)}, u32[]{:S(2)}, u32[]{:S(2)}) async-start(f32[16,32,128]{2,1,0:T(8,128)} %spread.1), calls=%async_computation.2 | async-start | bytes 524288 | tf_op jit(solution)/shard_map/all_to_all | solution.py:25

commit v6 on v5

--- a/solution.py
+++ b/solution.py
@@ -63,46 +63,55 @@
     capacity = alt_ids.shape[1]
     slab, width = centroids.shape
     factor = scaling * log2e
-    block = math.gcd(slab, 8192)
+    block = math.gcd(slab, 1024)
     small = math.gcd(slab, 256)
-
-    def kernel(x_ref, c_ref, i_ref, r_ref, out_ref, t_ref, m_ref, a_ref):
+    height = 256
+
+    def kernel(x_ref, c_ref, i_ref, r_ref, out_ref, e_ref, base_ref, t_ref, s_ref, m_ref, a_ref, l_ref):
         load_rows(x_ref, t_ref, n_blk, tok)
 
-        def scores(start, size, lanes):
+        def scores(band, start, size):
             return lax.dot_general(
-                c_ref[pl.ds(start, size), :],
-                t_ref[lanes, :],
+                t_ref[band, :],
+                c_ref[start : start + size, :],
                 (((1,), (1,)), ((), ())),
                 preferred_element_type=jnp.float32,
-            ).reshape(size // 8, 8, 256)
-
-        def rescale_free():
-            for g in range(rows // 256):
-                lanes = slice(g * 256, (g + 1) * 256)
-                first = jnp.max(scores(0, small, lanes), axis=(0, 1)).reshape(1, 256)
-                m_ref[:, lanes] = jnp.broadcast_to(first, (8, 256))
-            a_ref[...] = jnp.zeros_like(a_ref)
-
-            def step(j, carry):
-                start = pl.multiple_of(j * block, block)
-                for g in range(rows // 256):
-                    lanes = slice(g * 256, (g + 1) * 256)
-                    e = jnp.exp2((scores(start, block, lanes) - m_ref[:, lanes][None]) * factor)
-                    a_ref[:, lanes] = a_ref[:, lanes] + jnp.sum(e, axis=0)
-                return carry
-
-            lax.fori_loop(0, slab // block, step, 0)
-
-        def rescaled():
+            )
+
+        bands = [slice(r, r + height) for r in range(0, rows, height)]
+        for band in bands:
+            first = jnp.max(scores(band, 0, small), axis=1, keepdims=True)
+            base_ref[band, :] = jnp.broadcast_to(first, (height, 128))
+        s_ref[...] = jnp.zeros_like(s_ref)
+        for start in range(0, slab, block):
+            for band in bands:
+                s = scores(band, start, block)
+                total = s_ref[band, :]
+                for g in range(0, block, 128):
+                    e = jnp.exp2((s[:, g : g + 128] - base_ref[band, :]) * factor)
+                    e_ref[band, start + g : start + g + 128] = e
+                    total = total + e
+                s_ref[band, :] = total
+        base = jnp.transpose(base_ref[...])[:1, :]
+        total = jnp.sum(jnp.transpose(s_ref[...]), axis=0, keepdims=True)
+        l_ref[...] = base * scaling + jnp.log(total)
+
+        @pl.when(jnp.logical_not(jnp.max(total) < 1.0e15))
+        def _():
             m_ref[...] = jnp.full_like(m_ref, dead)
             a_ref[...] = jnp.zeros_like(a_ref)
 
             def step(j, carry):
                 start = pl.multiple_of(j * small, small)
-                for g in range(rows // 256):
-                    lanes = slice(g * 256, (g + 1) * 256)
-                    s = scores(start, small, lanes)
+                e_ref[:, pl.ds(start, small)] = jnp.zeros((rows, small), jnp.float32)
+                for g in range(0, rows, 256):
+                    lanes = slice(g, g + 256)
+                    s = lax.dot_general(
+                        c_ref[pl.ds(start, small), :],
+                        t_ref[lanes, :],
+                        (((1,), (1,)), ((), ())),
+                        preferred_element_type=jnp.float32,
+                    ).reshape(small // 8, 8, 256)
                     old = m_ref[:, lanes]
                     new = jnp.maximum(old, jnp.max(s, axis=0))
                     m_ref[:, lanes] = new
@@ -111,17 +120,12 @@
                 return carry
 
             lax.fori_loop(0, slab // small, step, 0)
-
-        rescale_free()
-
-        @pl.when(jnp.logical_not(jnp.max(a_ref[...]) < 1.0e38))
-        def _():
-            rescaled()
-
-        m = m_ref[...]
-        top = jnp.max(m, axis=0, keepdims=True)
-        total = jnp.sum(a_ref[...] * jnp.exp2((m - top) * factor), axis=0, keepdims=True)
-        lse = top * scaling + jnp.log(total)
+            m = m_ref[...]
+            top = jnp.max(m, axis=0, keepdims=True)
+            sums = jnp.sum(a_ref[...] * jnp.exp2((m - top) * factor), axis=0, keepdims=True)
+            l_ref[...] = top * scaling + jnp.log(sums)
+
+        lse = l_ref[...]
         ids = i_ref[...]
         line = jnp.concatenate(
             [ids >> 7, ids & 127, r_ref[...], jnp.zeros((n_blk, 128 - 3 * capacity), jnp.int32)], axis=1
@@ -132,15 +136,21 @@
 
     return pl.pallas_call(
         kernel,
-        out_shape=jax.ShapeDtypeStruct((n_blk, 1, rows + 128), jnp.float32),
+        out_shape=(
+            jax.ShapeDtypeStruct((n_blk, 1, rows + 128), jnp.float32),
+            pltpu.VMEM((rows, slab), jnp.float32),
+            pltpu.VMEM((rows, 128), jnp.float32),
+        ),
         in_specs=vmem(4),
-        out_specs=pl.BlockSpec(memory_space=pltpu.VMEM),
+        out_specs=tuple(vmem(3)),
         scratch_shapes=[
             pltpu.VMEM((rows, width), jnp.bfloat16),
+            pltpu.VMEM((rows, 128), jnp.float32),
             pltpu.VMEM((8, rows), jnp.float32),
             pltpu.VMEM((8, rows), jnp.float32),
+            pltpu.VMEM((1, rows), jnp.float32),
         ],
-        compiler_params=params(16),
+        compiler_params=params(8),
         name="row_pass",
     )(x, centroids, alt_ids, row_ids)
 
@@ -166,16 +176,16 @@
     )(parts)
 
 
-def column_pass(x, centroids, parts, tok, scaling, all_cols):
+def column_pass(x, centroids, parts, kept, base, tok, scaling, all_cols):
     n_blk = x.shape[0]
     rows = n_blk * tok
     slab, width = centroids.shape
     block = 256
-    group = math.gcd(slab // block, 32)
     factor = scaling * log2e
-
-    def kernel(x_ref, c_ref, l_ref, own_ref, dual_ref, mass_ref, t_ref, d_ref):
-        load_rows(x_ref, t_ref, n_blk, tok)
+    lines = slab // 128
+    held = math.gcd(lines, 32)
+
+    def kernel(x_ref, c_ref, l_ref, e_ref, b_ref, own_ref, dual_ref, mass_ref, t_ref, d_ref, w_ref):
         lse = l_ref[:, 0, :rows]
         top = jnp.max(lse, axis=0, keepdims=True)
         total = jnp.sum(jnp.exp(lse - top), axis=0, keepdims=True)
@@ -187,10 +197,32 @@
             own = own + jnp.where(position == i, dual[:, i * tok : (i + 1) * tok], 0.0)
         own_ref[...] = own
         d_ref[...] = jnp.transpose(jnp.broadcast_to(dual * log2e, (128, rows)))
-
-        def step(j, carry):
-            for g in range(group):
-                k = j * group + g
+        w_ref[...] = jnp.exp2(b_ref[...] * factor + d_ref[...])
+
+        for first in range(0, lines, held):
+
+            def add(r, sums):
+                sums = list(sums)
+                start = pl.multiple_of(r * 32, 32)
+                for q in range(0, 32, 8):
+                    w = w_ref[pl.ds(start + q, 8), :]
+                    for g in range(held):
+                        k = (first + g) * 128
+                        sums[g] = sums[g] + e_ref[pl.ds(start + q, 8), k : k + 128] * w
+                return tuple(sums)
+
+            sums = lax.fori_loop(0, rows // 32, add, tuple(jnp.zeros((8, 128), jnp.float32) for _ in range(held)))
+            for g in range(held):
+                mass_ref[first + g : first + g + 1, :] = jnp.sum(sums[g], axis=0, keepdims=True)
+
+        mass = mass_ref[...]
+        sound = jnp.logical_and(jnp.min(mass) > 1.0e-12, jnp.max(mass) < 1.0e12)
+
+        @pl.when(jnp.logical_not(sound))
+        def _():
+            load_rows(x_ref, t_ref, n_blk, tok)
+
+            def step(k, carry):
                 s = lax.dot_general(
                     t_ref[...],
                     c_ref[pl.ds(pl.multiple_of(k * block, block), block), :],
@@ -199,29 +231,30 @@
                 )
                 d = d_ref[...]
                 e = jnp.exp2(s * factor + jnp.concatenate([d] * (block // 128), axis=1))
-                mass = jnp.sum(e, axis=0, keepdims=True)
+                part = jnp.sum(e, axis=0, keepdims=True)
                 for h in range(block // 128):
-                    mass_ref[pl.ds(k * (block // 128) + h, 1), :] = mass[:, h * 128 : (h + 1) * 128]
-            return carry
-
-        lax.fori_loop(0, slab // (block * group), step, 0)
+                    mass_ref[pl.ds(k * (block // 128) + h, 1), :] = part[:, h * 128 : (h + 1) * 128]
+                return carry
+
+            lax.fori_loop(0, slab // block, step, 0)
 
     return pl.pallas_call(
         kernel,
         out_shape=(
             jax.ShapeDtypeStruct((1, tok), jnp.float32),
             jax.ShapeDtypeStruct((1, rows), jnp.float32),
-            jax.ShapeDtypeStruct((slab // 128, 128), jnp.float32),
+            jax.ShapeDtypeStruct((lines, 128), jnp.float32),
         ),
-        in_specs=vmem(3),
+        in_specs=vmem(5),
         out_specs=tuple(vmem(3)),
         scratch_shapes=[
             pltpu.VMEM((rows, width), jnp.bfloat16),
             pltpu.VMEM((rows, 128), jnp.float32),
+            pltpu.VMEM((rows, 128), jnp.float32),
         ],
-        compiler_params=params(16),
+        compiler_params=params(8),
         name="column_pass",
-    )(x, centroids, parts)
+    )(x, centroids, parts, kept, base)
 
 
 def spread(both, copies):
@@ -418,8 +451,9 @@
 
     outgoing, near = stage(tokens, centroids, n_blk)
     gathered = exchange(outgoing, "blk")
-    parts = exchange(row_pass(gathered, near, alt_ids[0], row_ids[0], tok, scaling), "blk")
-    own_duals, duals, mass = column_pass(gathered, near, parts, tok, scaling, slab * n_blk)
+    sent, kept, base = row_pass(gathered, near, alt_ids[0], row_ids[0], tok, scaling)
+    parts = exchange(sent, "blk")
+    own_duals, duals, mass = column_pass(gathered, near, parts, kept, base, tok, scaling, slab * n_blk)
     both = lax.all_gather(mass, "wide", axis=0, axis_index_groups=pairs, tiled=True)
     mass = add_up(exchange(spread(both, n_wide // 2), "wide", same_core))
     ids = unpack(parts, n_blk * tok, capacity)

time: 98.4 us -> 108 us (1.098)
  Pallas kernels: 16 us -> 37.1 us
  blocking collectives: 60.8 us -> 49.2 us
    pallas_call x1, Pallas kernels: 3.97 us -> 15.6 us  [row_pass(): pl.pallas_call(kernel, out_shape=(jax.ShapeDtypeStruct((n_blk, 1, rows +...]
    all_to_all x3, blocking collectives: 53 us -> 41.4 us  [exchange(): lax.all_to_all(x, axis, split_axis=0, concat_axis=0, axis_index_groups=gr...]
    pallas_call x1, Pallas kernels: 4.15 us -> 13.6 us  [column_pass(): pl.pallas_call(kernel, out_shape=(jax.ShapeDtypeStruct((1, tok), jnp.floa...]
where the time goes in v6:
time: 108 us; the launch traced here: 107 us
  blocking collectives  49.2 us (46%)
  Pallas kernels  37.1 us (34%)
  starting transfers between devices  11.7 us (11%)
  waiting for transfers between devices  7.38 us (7%)
  local copies, waits for them, and re-layouts  1.36 us (1%)
    all_to_all x3, blocking collectives, exchange(): lax.all_to_all(x, axis, split_axis=0, concat_axis=0, axis_index_groups=gr...  41.4 us
    pallas_call x1, Pallas kernels, row_pass(): pl.pallas_call(kernel, out_shape=(jax.ShapeDtypeStruct((n_blk, 1, rows +...  15.6 us
    pallas_call x1, Pallas kernels, column_pass(): pl.pallas_call(kernel, out_shape=(jax.ShapeDtypeStruct((1, tok), jnp.floa...  13.6 us
    all_to_all x1, starting transfers between devices, exchange(): lax.all_to_all(x, axis, split_axis=0, concat_axis=0, axis_index_groups=gr...  11.7 us
    all_gather x2, blocking collectives, local(): lax.all_gather(mass, 'wide', axis=0, axis_index_groups=pairs, tiled=True)  7.74 us
    all_to_all x1, waiting for transfers between devices, exchange(): lax.all_to_all(x, axis, split_axis=0, concat_axis=0, axis_index_groups=gr...  7.38 us
    pallas_call x1, Pallas kernels, ask_scores(): pl.pallas_call(kernel, out_shape=jax.ShapeDtypeStruct((1, n_blk * capacit...  2.79 us
  transfers between devices with their start and end apart: 1, of which 1 were waited for; matrix products, arithmetic and copies ran while one was open for 1% of the time, Pallas kernels for 4%

profile of v6, /device:TPU:1, one launch (start us, length us, event | category | flops | bytes accessed | tf_op | source)
XLA Modules:
  0.0 107.5 jit_solution(16115908017118732353)
XLA Ops:
  0.6 0.0 copy-start.1
  0.6 0.0 copy-start.2
  0.7 1.6 %stage.1 = (bf16[16,48,128]{2,1,0:T(8,128)(2,1)S(1)}, bf16[8192,128]{1,0:T(8,128)(2,1)S(1)}) custom-call(bf16[48,128]{1,0:T(8,128)(2,1)} %t_ref.3, bf16[8192,128]{1,0:T(8,128)(2,1)} %c_ref.1), custom_call_target="tpu_custom_call" | custom-call | tf_op jit(solution)/shard_map/stage/pallas_call | solution.py:46
  2.3 18.6 %all_to_all.20.x_ref = bf16[16,48,128]{2,1,0:T(8,128)(2,1)S(1)} all-to-all(bf16[16,48,128]{2,1,0:T(8,128)(2,1)S(1)} %get-tuple-element.19), channel_id=1, replica_groups=mesh['blk'=16,'wide'=32] {'blk'}, dimensions={0} | all-to-all | bytes 393216 | tf_op jit(solution)/shard_map/all_to_all | solution.py:25
  20.9 0.0 copy-done.1
  20.9 0.0 copy-done.2
  20.9 15.6 %row_pass.1 = (f32[16,1,896]{2,1,0:T(1,128)S(1)}, f32[768,8192]{1,0:T(8,128)S(1)}, f32[768,128]{1,0:T(8,128)S(1)}) custom-call(bf16[16,48,128]{2,1,0:T(8,128)(2,1)S(1)} %all_to_all.20.x_ref, bf16[8192,128]{1,0:T(8,128)(2,1)S(1)} %get-tuple-element.20.c_ref, s32[16,32]{1,0:T(8,128)S(1)} %bitcast.11, s32[16,32]{1,0:T(8,128)S(1)} %bitcast.9), custom_call_target="tpu_custom_call" | custom-call | tf_op jit(solution)/shard_map/row_pass/pallas_call | solution.py:137
  36.6 10.9 %all_to_all.21.l_ref.p_ref = f32[16,1,896]{2,1,0:T(1,128)S(1)} all-to-all(f32[16,1,896]{2,1,0:T(1,128)S(1)} %get-tuple-element.21), channel_id=1, replica_groups=mesh['blk'=16,'wide'=32] {'blk'}, dimensions={0} | all-to-all | bytes 114688 | tf_op jit(solution)/shard_map/all_to_all | solution.py:25
  47.4 0.0 copy-start
  47.4 0.0 copy-start.3
  47.4 13.6 %column_pass.1 = (f32[1,48]{1,0:T(1,128)}, f32[1,768]{1,0:T(1,128)S(1)}, f32[64,128]{1,0:T(8,128)S(1)}) custom-call(bf16[16,48,128]{2,1,0:T(8,128)(2,1)S(1)} %all_to_all.20.x_ref, bf16[8192,128]{1,0:T(8,128)(2,1)S(1)} %get-tuple-element.20.c_ref, f32[16,1,896]{2,1,0:T(1,128)S(1)} %all_to_all.21.l_ref.p_ref, f32[768,8192]{1,0:T(8,128)S(1)} %get-tuple-element.22.e_ref, ...), custom_call_target="tpu_custom_call" | custom-call | tf_op jit(solution)/shard_map/column_pass/pallas_call | solution.py:241
  61.0 4.8 %all_gather.6.p_ref = f32[128,128]{1,0:T(8,128)S(1)} all-gather(f32[64,128]{1,0:T(8,128)S(1)} %get-tuple-element.25), channel_id=1, replica_groups={{0,1},{2,3},{4,5},{6,7},{8,9},{10,11},{12,13},{14,15},{16,17},{18,19},{..., dimensions={0}, use_global_device_ids=true | all-gather | bytes 98304 | tf_op jit(solution)/shard_map/all_gather | solution.py:457
  65.8 0.7 spread.1
  66.5 11.7 %all-to-all-start.2 = ((f32[16,32,128]{2,1,0:T(8,128)}), f32[16,32,128]{2,1,0:T(8,128)S(1)}, u32[]{:S(2)}, u32[]{:S(2)}) async-start(f32[16,32,128]{2,1,0:T(8,128)} %spread.1), calls=%async_computation.2 | async-start | bytes 524288 | tf_op jit(solution)/shard_map/all_to_all | solution.py:25
  78.2 0.0 copy-done
  78.2 0.0 copy-done.3
  78.2 0.9 prepare.1
  79.2 0.2 unpack.1.i_ref
  79.3 1.3 %gather_fusion = bf16[512,128]{1,0:T(8,128)(2,1)S(1)} fusion(bf16[8192,128]{1,0:T(8,128)(2,1)S(1)} %get-tuple-element.20.c_ref, s32[1024]{0:T(1024)S(1)} %pad_clamp_fusion), kind=kCustom, calls=%fused_computation | custom fusion | bytes 264192 | tf_op jit(solution)/shard_map/gather | solution.py:460
  80.7 2.8 %ask_scores.1.s_ref = f32[1,512]{1,0:T(1,128)S(1)} custom-call(bf16[16,48,128]{2,1,0:T(8,128)(2,1)S(1)} %all_to_all.20.x_ref, bf16[512,128]{1,0:T(8,128)(2,1)S(1)} %gather_fusion, f32[16,1,896]{2,1,0:T(1,128)S(1)} %all_to_all.21.l_ref.p_ref, f32[1,768]{1,0:T(1,128)S(1)} %get-tuple-element.26.d_ref), custom_call_target="tpu_custom_call" | custom-call | tf_op jit(solution)/shard_map/ask_scores/pallas_call | solution.py:330
  83.5 7.4 %all-to-all-done.2.p_ref = f32[16,32,128]{2,1,0:T(8,128)S(1)} async-done(((f32[16,32,128]{2,1,0:T(8,128)}), f32[16,32,128]{2,1,0:T(8,128)S(1)}, u32[]{:S(2)}, u32[]{:S(2)}) %all-to-all-start.2) | async-done | bytes 262176 | tf_op jit(solution)/shard_map/all_to_all | solution.py:25
  90.9 3.0 %all_gather.7.m_ref = f32[64,128]{1,0:T(8,128)S(1)} all-gather(f32[32,128]{1,0:T(8,128)S(1)} %add_up.1), channel_id=1, replica_groups={{0,1},{2,3},{4,5},{6,7},{8,9},{10,11},{12,13},{14,15},{16,17},{18,19},{..., dimensions={0}, use_global_device_ids=true | all-gather | bytes 49152 | tf_op jit(solution)/shard_map/all_gather | solution.py:464
  93.8 0.6 look_up.1
  94.5 12.0 %all_to_all.22.g_ref = bf16[16,33,128]{2,1,0:T(8,128)(2,1)S(1)} all-to-all(bf16[16,33,128]{2,1,0:T(8,128)(2,1)S(1)} %get-tuple-element.32), channel_id=1, replica_groups=mesh['blk'=16,'wide'=32] {'blk'}, dimensions={0} | all-to-all | bytes 270336 | tf_op jit(solution)/shard_map/all_to_all | solution.py:25
  106.4 1.0 finish.1
  (3 shorter events, 0.0 us)
Async XLA Ops:
  0.6 20.3 %copy-start.1 = (s32[1,16,32]{2,1,0:T(8,128)S(1)}, s32[1,16,32]{2,1,0:T(8,128)}, u32[]{:S(2)}) copy-start(s32[1,16,32]{2,1,0:T(8,128)} %param.7) | copy-start | bytes 6148
  0.6 20.3 %copy-start.2 = (s32[1,16,32]{2,1,0:T(8,128)S(1)}, s32[1,16,32]{2,1,0:T(8,128)}, u32[]{:S(2)}) copy-start(s32[1,16,32]{2,1,0:T(8,128)} %param.8) | copy-start | bytes 6148
  47.4 30.8 %copy-start = (bf16[48,128]{1,0:T(8,128)(2,1)S(1)}, bf16[48,128]{1,0:T(8,128)(2,1)}, u32[]{:S(2)}) copy-start(bf16[48,128]{1,0:T(8,128)(2,1)} %t_ref.3) | copy-start | bytes 36868
  47.4 30.8 %copy-start.3 = (s32[1,16]{1,0:T(1,128)S(1)}, s32[1,16]{1,0:T(1,128)}, u32[]{:S(2)}) copy-start(s32[1,16]{1,0:T(1,128)} %n_ref.1) | copy-start | bytes 196
  66.5 24.3 %all-to-all-start.2 = ((f32[16,32,128]{2,1,0:T(8,128)}), f32[16,32,128]{2,1,0:T(8,128)S(1)}, u32[]{:S(2)}, u32[]{:S(2)}) async-start(f32[16,32,128]{2,1,0:T(8,128)} %spread.1), calls=%async_computation.2 | async-start | bytes 524288 | tf_op jit(solution)/shard_map/all_to_all | solution.py:25

commit v7 on v6

--- a/solution.py
+++ b/solution.py
@@ -32,26 +32,20 @@
 def stage(tokens, centroids, count):
     tok, width = tokens.shape
 
-    def kernel(t_ref, c_ref, copies_ref, near_ref, t_scr, sems):
-        first = pltpu.make_async_copy(t_ref, t_scr, sems.at[0])
-        second = pltpu.make_async_copy(c_ref, near_ref, sems.at[1])
-        first.start()
-        second.start()
-        first.wait()
+    def kernel(t_ref, c_ref, copies_ref, t_scr, sem):
+        copy = pltpu.make_async_copy(t_ref, t_scr, sem)
+        copy.start()
+        copy.wait()
         rows = t_scr[...]
         for i in range(count):
             copies_ref[i] = rows
-        second.wait()
-
-    return pl.pallas_call(
-        kernel,
-        out_shape=(
-            pltpu.VMEM((count, tok, width), tokens.dtype),
-            pltpu.VMEM(centroids.shape, centroids.dtype),
-        ),
+
+    return pl.pallas_call(
+        kernel,
+        out_shape=pltpu.VMEM((count, tok, width), tokens.dtype),
         in_specs=[pl.BlockSpec(memory_space=pltpu.HBM)] * 2,
-        out_specs=tuple(vmem(2)),
-        scratch_shapes=[pltpu.VMEM((tok, width), tokens.dtype), pltpu.SemaphoreType.DMA((2,))],
+        out_specs=pl.BlockSpec(memory_space=pltpu.VMEM),
+        scratch_shapes=[pltpu.VMEM((tok, width), tokens.dtype), pltpu.SemaphoreType.DMA],
         compiler_params=params(56),
         name="stage",
     )(tokens, centroids)
@@ -184,6 +178,7 @@
     factor = scaling * log2e
     lines = slab // 128
     held = math.gcd(lines, 32)
+    stride = math.gcd(rows, 256)
 
     def kernel(x_ref, c_ref, l_ref, e_ref, b_ref, own_ref, dual_ref, mass_ref, t_ref, d_ref, w_ref):
         lse = l_ref[:, 0, :rows]
@@ -203,15 +198,15 @@
 
             def add(r, sums):
                 sums = list(sums)
-                start = pl.multiple_of(r * 32, 32)
-                for q in range(0, 32, 8):
+                start = pl.multiple_of(r * stride, stride)
+                for q in range(0, stride, 8):
                     w = w_ref[pl.ds(start + q, 8), :]
                     for g in range(held):
                         k = (first + g) * 128
                         sums[g] = sums[g] + e_ref[pl.ds(start + q, 8), k : k + 128] * w
                 return tuple(sums)
 
-            sums = lax.fori_loop(0, rows // 32, add, tuple(jnp.zeros((8, 128), jnp.float32) for _ in range(held)))
+            sums = lax.fori_loop(0, rows // stride, add, tuple(jnp.zeros((8, 128), jnp.float32) for _ in range(held)))
             for g in range(held):
                 mass_ref[first + g : first + g + 1, :] = jnp.sum(sums[g], axis=0, keepdims=True)
 
@@ -449,15 +444,14 @@
     pairs = [[k, k + 1] for k in range(0, n_wide, 2)]
     same_core = [list(range(core, n_wide, 2)) for core in range(2)]
 
-    outgoing, near = stage(tokens, centroids, n_blk)
-    gathered = exchange(outgoing, "blk")
-    sent, kept, base = row_pass(gathered, near, alt_ids[0], row_ids[0], tok, scaling)
+    gathered = exchange(stage(tokens, centroids, n_blk), "blk")
+    sent, kept, base = row_pass(gathered, centroids, alt_ids[0], row_ids[0], tok, scaling)
     parts = exchange(sent, "blk")
-    own_duals, duals, mass = column_pass(gathered, near, parts, kept, base, tok, scaling, slab * n_blk)
+    own_duals, duals, mass = column_pass(gathered, centroids, parts, kept, base, tok, scaling, slab * n_blk)
     both = lax.all_gather(mass, "wide", axis=0, axis_index_groups=pairs, tiled=True)
     mass = add_up(exchange(spread(both, n_wide // 2), "wide", same_core))
     ids = unpack(parts, n_blk * tok, capacity)
-    centres = near[ids[2]]
+    centres = centroids[ids[2]]
     sums = ask_scores(gathered, centres, parts, duals, scaling)
     rows, live = prepare(tokens, row_ids[0], counts)
     mass, sums, rows, live = lax.optimization_barrier((mass, sums, rows, live))

time: 108 us -> 107 us (level)
  Pallas kernels: 37.1 us -> 36 us
where the time goes in v7:
time: 107 us; the launch traced here: 106 us
  blocking collectives  49.3 us (46%)
  Pallas kernels  36 us (34%)
  starting transfers between devices  11.7 us (11%)
  waiting for transfers between devices  7.22 us (7%)
  local copies, waits for them, and re-layouts  1.36 us (1%)
    all_to_all x3, blocking collectives, exchange(): lax.all_to_all(x, axis, split_axis=0, concat_axis=0, axis_index_groups=gr...  41.4 us
    pallas_call x1, Pallas kernels, row_pass(): pl.pallas_call(kernel, out_shape=(jax.ShapeDtypeStruct((n_blk, 1, rows +...  15.6 us
    pallas_call x1, Pallas kernels, column_pass(): pl.pallas_call(kernel, out_shape=(jax.ShapeDtypeStruct((1, tok), jnp.floa...  13.2 us
    all_to_all x1, starting transfers between devices, exchange(): lax.all_to_all(x, axis, split_axis=0, concat_axis=0, axis_index_groups=gr...  11.7 us
    all_gather x2, blocking collectives, local(): lax.all_gather(mass, 'wide', axis=0, axis_index_groups=pairs, tiled=True)  7.89 us
    all_to_all x1, waiting for transfers between devices, exchange(): lax.all_to_all(x, axis, split_axis=0, concat_axis=0, axis_index_groups=gr...  7.22 us
    pallas_call x1, Pallas kernels, ask_scores(): pl.pallas_call(kernel, out_shape=jax.ShapeDtypeStruct((1, n_blk * capacit...  2.79 us
  transfers between devices with their start and end apart: 1, of which 1 were waited for; matrix products, arithmetic and copies ran while one was open for 1% of the time, Pallas kernels for 4%

profile of v7, /device:TPU:1, one launch (start us, length us, event | category | flops | bytes accessed | tf_op | source)
XLA Modules:
  0.0 106.3 jit_solution(1126506927863752097)
XLA Ops:
  0.6 0.0 copy-start
  0.6 0.0 copy-start.2
  0.7 0.0 copy-start.3
  0.7 0.9 stage.1
  1.6 18.6 %all_to_all.20.x_ref = bf16[16,48,128]{2,1,0:T(8,128)(2,1)S(1)} all-to-all(bf16[16,48,128]{2,1,0:T(8,128)(2,1)S(1)} %stage.1), channel_id=1, replica_groups=mesh['blk'=16,'wide'=32] {'blk'}, dimensions={0} | all-to-all | bytes 393216 | tf_op jit(solution)/shard_map/all_to_all | solution.py:25
  20.2 0.0 copy-done
  20.2 0.0 copy-done.2
  20.2 0.0 copy-done.3
  20.2 15.6 %row_pass.1 = (f32[16,1,896]{2,1,0:T(1,128)S(1)}, f32[768,8192]{1,0:T(8,128)S(1)}, f32[768,128]{1,0:T(8,128)S(1)}) custom-call(bf16[16,48,128]{2,1,0:T(8,128)(2,1)S(1)} %all_to_all.20.x_ref, bf16[8192,128]{1,0:T(8,128)(2,1)S(1)} %copy-done, s32[16,32]{1,0:T(8,128)S(1)} %bitcast.11, s32[16,32]{1,0:T(8,128)S(1)} %bitcast.9), custom_call_target="tpu_custom_call" | custom-call | tf_op jit(solution)/shard_map/row_pass/pallas_call | solution.py:131
  35.8 10.9 %all_to_all.21.l_ref.p_ref = f32[16,1,896]{2,1,0:T(1,128)S(1)} all-to-all(f32[16,1,896]{2,1,0:T(1,128)S(1)} %get-tuple-element.17), channel_id=1, replica_groups=mesh['blk'=16,'wide'=32] {'blk'}, dimensions={0} | all-to-all | bytes 114688 | tf_op jit(solution)/shard_map/all_to_all | solution.py:25
  46.7 0.0 copy-start.1
  46.7 0.0 copy-start.4
  46.7 13.2 %column_pass.1 = (f32[1,48]{1,0:T(1,128)}, f32[1,768]{1,0:T(1,128)S(1)}, f32[64,128]{1,0:T(8,128)S(1)}) custom-call(bf16[16,48,128]{2,1,0:T(8,128)(2,1)S(1)} %all_to_all.20.x_ref, bf16[8192,128]{1,0:T(8,128)(2,1)S(1)} %copy-done, f32[16,1,896]{2,1,0:T(1,128)S(1)} %all_to_all.21.l_ref.p_ref, f32[768,8192]{1,0:T(8,128)S(1)} %get-tuple-element.18.e_ref, ...), custom_call_target="tpu_custom_call" | custom-call | tf_op jit(solution)/shard_map/column_pass/pallas_call | solution.py:236
  59.9 4.8 %all_gather.6.p_ref = f32[128,128]{1,0:T(8,128)S(1)} all-gather(f32[64,128]{1,0:T(8,128)S(1)} %get-tuple-element.21), channel_id=1, replica_groups={{0,1},{2,3},{4,5},{6,7},{8,9},{10,11},{12,13},{14,15},{16,17},{18,19},{..., dimensions={0}, use_global_device_ids=true | all-gather | bytes 98304 | tf_op jit(solution)/shard_map/all_gather | solution.py:451
  64.7 0.7 spread.1
  65.4 11.7 %all-to-all-start.2 = ((f32[16,32,128]{2,1,0:T(8,128)}), f32[16,32,128]{2,1,0:T(8,128)S(1)}, u32[]{:S(2)}, u32[]{:S(2)}) async-start(f32[16,32,128]{2,1,0:T(8,128)} %spread.1), calls=%async_computation.2 | async-start | bytes 524288 | tf_op jit(solution)/shard_map/all_to_all | solution.py:25
  77.1 0.0 copy-done.1
  77.1 0.0 copy-done.4
  77.1 0.9 prepare.1
  78.0 0.2 unpack.1.i_ref
  78.2 1.3 %gather_fusion = bf16[512,128]{1,0:T(8,128)(2,1)S(1)} fusion(bf16[8192,128]{1,0:T(8,128)(2,1)S(1)} %copy-done, s32[1024]{0:T(1024)S(1)} %pad_clamp_fusion), kind=kCustom, calls=%fused_computation | custom fusion | bytes 264192 | tf_op jit(solution)/shard_map/gather | solution.py:454
  79.6 2.8 %ask_scores.1.s_ref = f32[1,512]{1,0:T(1,128)S(1)} custom-call(bf16[16,48,128]{2,1,0:T(8,128)(2,1)S(1)} %all_to_all.20.x_ref, bf16[512,128]{1,0:T(8,128)(2,1)S(1)} %gather_fusion, f32[16,1,896]{2,1,0:T(1,128)S(1)} %all_to_all.21.l_ref.p_ref, f32[1,768]{1,0:T(1,128)S(1)} %get-tuple-element.22.d_ref), custom_call_target="tpu_custom_call" | custom-call | tf_op jit(solution)/shard_map/ask_scores/pallas_call | solution.py:325
  82.4 7.2 %all-to-all-done.2.p_ref = f32[16,32,128]{2,1,0:T(8,128)S(1)} async-done(((f32[16,32,128]{2,1,0:T(8,128)}), f32[16,32,128]{2,1,0:T(8,128)S(1)}, u32[]{:S(2)}, u32[]{:S(2)}) %all-to-all-start.2) | async-done | bytes 262176 | tf_op jit(solution)/shard_map/all_to_all | solution.py:25
  89.6 3.1 %all_gather.7.m_ref = f32[64,128]{1,0:T(8,128)S(1)} all-gather(f32[32,128]{1,0:T(8,128)S(1)} %add_up.1), channel_id=1, replica_groups={{0,1},{2,3},{4,5},{6,7},{8,9},{10,11},{12,13},{14,15},{16,17},{18,19},{..., dimensions={0}, use_global_device_ids=true | all-gather | bytes 49152 | tf_op jit(solution)/shard_map/all_gather | solution.py:458
  92.7 0.6 look_up.1
  93.4 12.0 %all_to_all.22.g_ref = bf16[16,33,128]{2,1,0:T(8,128)(2,1)S(1)} all-to-all(bf16[16,33,128]{2,1,0:T(8,128)(2,1)S(1)} %get-tuple-element.28), channel_id=1, replica_groups=mesh['blk'=16,'wide'=32] {'blk'}, dimensions={0} | all-to-all | bytes 270336 | tf_op jit(solution)/shard_map/all_to_all | solution.py:25
  105.3 1.0 finish.1
  (3 shorter events, 0.0 us)
Async XLA Ops:
  0.6 19.6 %copy-start = (bf16[8192,128]{1,0:T(8,128)(2,1)S(1)}, bf16[8192,128]{1,0:T(8,128)(2,1)}, u32[]{:S(2)}) copy-start(bf16[8192,128]{1,0:T(8,128)(2,1)} %c_ref.5) | copy-start | bytes 6291460
  0.6 19.5 %copy-start.2 = (s32[1,16,32]{2,1,0:T(8,128)S(1)}, s32[1,16,32]{2,1,0:T(8,128)}, u32[]{:S(2)}) copy-start(s32[1,16,32]{2,1,0:T(8,128)} %param.7) | copy-start | bytes 6148
  0.7 19.5 %copy-start.3 = (s32[1,16,32]{2,1,0:T(8,128)S(1)}, s32[1,16,32]{2,1,0:T(8,128)}, u32[]{:S(2)}) copy-start(s32[1,16,32]{2,1,0:T(8,128)} %param.8) | copy-start | bytes 6148
  46.7 30.4 %copy-start.1 = (bf16[48,128]{1,0:T(8,128)(2,1)S(1)}, bf16[48,128]{1,0:T(8,128)(2,1)}, u32[]{:S(2)}) copy-start(bf16[48,128]{1,0:T(8,128)(2,1)} %t_ref.3) | copy-start | bytes 36868
  46.7 30.4 %copy-start.4 = (s32[1,16]{1,0:T(1,128)S(1)}, s32[1,16]{1,0:T(1,128)}, u32[]{:S(2)}) copy-start(s32[1,16]{1,0:T(1,128)} %n_ref.1) | copy-start | bytes 196
  65.4 24.2 %all-to-all-start.2 = ((f32[16,32,128]{2,1,0:T(8,128)}), f32[16,32,128]{2,1,0:T(8,128)S(1)}, u32[]{:S(2)}, u32[]{:S(2)}) async-start(f32[16,32,128]{2,1,0:T(8,128)} %spread.1), calls=%async_computation.2 | async-start | bytes 524288 | tf_op jit(solution)/shard_map/all_to_all | solution.py:25

commit v8 on v7

--- a/solution.py
+++ b/solution.py
@@ -149,22 +149,32 @@
     )(x, centroids, alt_ids, row_ids)
 
 
-def unpack(parts, rows, capacity):
+def unpack(parts, rows, lines, capacity):
     n_blk = parts.shape[0]
-
-    def kernel(p_ref, ids_ref):
+    slots = n_blk * capacity
+
+    def kernel(p_ref, ids_ref, pick_ref, here_ref, h_ref, l_ref):
         for i in range(n_blk):
             line = p_ref[i, :, rows:].astype(jnp.int32)
             part = slice(i * capacity, (i + 1) * capacity)
-            ids_ref[0:1, part] = line[:, :capacity]
-            ids_ref[1:2, part] = line[:, capacity : 2 * capacity]
-            ids_ref[2:3, part] = line[:, :capacity] * 128 + line[:, capacity : 2 * capacity]
-
-    return pl.pallas_call(
-        kernel,
-        out_shape=jax.ShapeDtypeStruct((3, n_blk * capacity), jnp.int32),
+            h_ref[:, part] = line[:, :capacity]
+            l_ref[:, part] = line[:, capacity : 2 * capacity]
+        ids_ref[...] = h_ref[...] * 128 + l_ref[...]
+        line = lax.broadcasted_iota(jnp.int32, (lines, slots), 0)
+        pick_ref[...] = jnp.where(line == h_ref[...], 1.0, 0.0).astype(jnp.bfloat16)
+        lane = lax.broadcasted_iota(jnp.int32, (128, slots), 0)
+        here_ref[...] = jnp.where(lane == l_ref[...], 1.0, 0.0)
+
+    return pl.pallas_call(
+        kernel,
+        out_shape=(
+            jax.ShapeDtypeStruct((1, slots), jnp.int32),
+            jax.ShapeDtypeStruct((lines, slots), jnp.bfloat16),
+            jax.ShapeDtypeStruct((128, slots), jnp.float32),
+        ),
         in_specs=vmem(1),
-        out_specs=pl.BlockSpec(memory_space=pltpu.VMEM),
+        out_specs=tuple(vmem(3)),
+        scratch_shapes=[pltpu.VMEM((1, slots), jnp.int32)] * 2,
         compiler_params=params(4),
         name="unpack",
     )(parts)
@@ -255,19 +265,32 @@
 def spread(both, copies):
     lines = both.shape[0] // 2
     half = lines // 2
-
-    def kernel(p_ref, out_ref):
+    group = math.gcd(copies, 4)
+
+    def kernel(p_ref, out_ref, part_ref, sems):
         core = lax.rem(lax.axis_index("wide"), 2)
         start = pl.multiple_of(core * half, half)
         part = p_ref[pl.ds(start, half), :] + p_ref[pl.ds(lines + start, half), :]
-        for j in range(copies):
-            out_ref[j] = part
+        for j in range(group):
+            part_ref[j] = part
+        moves = [
+            pltpu.make_async_copy(part_ref, out_ref.at[pl.ds(j * group, group)], sems.at[j])
+            for j in range(copies // group)
+        ]
+        for move in moves:
+            move.start()
+        for move in moves:
+            move.wait()
 
     return pl.pallas_call(
         kernel,
         out_shape=jax.ShapeDtypeStruct((copies, half, 128), jnp.float32),
         in_specs=vmem(1),
-        out_specs=pl.BlockSpec(memory_space=pltpu.VMEM),
+        out_specs=pl.BlockSpec(memory_space=pltpu.HBM),
+        scratch_shapes=[
+            pltpu.VMEM((group, half, 128), jnp.float32),
+            pltpu.SemaphoreType.DMA((copies // group,)),
+        ],
         compiler_params=params(4),
         name="spread",
     )(both)
@@ -333,23 +356,20 @@
     )(x, centres, parts, duals)
 
 
-def look_up(masses, ids, centres, sums, all_rows, n_blk, capacity):
+def look_up(masses, pick, here, centres, sums, all_rows, n_blk, capacity):
     lines = masses.shape[0]
     slots = n_blk * capacity
 
-    def kernel(m_ref, i_ref, c_ref, s_ref, dual_ref, out_ref):
+    def kernel(m_ref, k_ref, h_ref, c_ref, s_ref, dual_ref, out_ref):
         dual = math.log(all_rows) - jnp.log(m_ref[...])
         dual_ref[...] = dual
-        line = lax.broadcasted_iota(jnp.int32, (lines, slots), 0)
-        pick = jnp.where(line == i_ref[0:1, :], 1.0, 0.0).astype(jnp.bfloat16)
-        lane = lax.broadcasted_iota(jnp.int32, (128, slots), 0)
-        here = lane == i_ref[1:2, :]
+        picks = k_ref[...]
         total = jnp.zeros((128, slots), jnp.float32)
         for piece in pieces_of(dual):
             total = total + lax.dot_general(
-                piece, pick, (((0,), (0,)), ((), ())), preferred_element_type=jnp.float32
+                piece, picks, (((0,), (0,)), ((), ())), preferred_element_type=jnp.float32
             )
-        total = jnp.sum(jnp.where(here, total, 0.0), axis=0, keepdims=True) + s_ref[...]
+        total = jnp.sum(jnp.where(h_ref[...] > 0.0, total, 0.0), axis=0, keepdims=True) + s_ref[...]
         pieces = [piece.astype(jnp.float32) for piece in pieces_of(total)]
         blank = jnp.zeros((1, 128 - 3 * capacity), jnp.float32)
         for i in range(n_blk):
@@ -364,11 +384,11 @@
             jax.ShapeDtypeStruct((lines, 128), jnp.float32),
             jax.ShapeDtypeStruct((n_blk, capacity + 1, 128), jnp.bfloat16),
         ),
-        in_specs=vmem(4),
+        in_specs=vmem(5),
         out_specs=tuple(vmem(2)),
         compiler_params=params(4),
         name="look_up",
-    )(masses, ids, centres, sums)
+    )(masses, pick, here, centres, sums)
 
 
 def prepare(tokens, row_ids, counts):
@@ -408,8 +428,9 @@
 def finish(answers, rows, live):
     n_blk, _, width = answers.shape
     capacity = rows.shape[0] // n_blk
-
-    def kernel(g_ref, t_ref, v_ref, out_ref, w_ref):
+    batch = n_blk // 4
+
+    def kernel(g_ref, t_ref, v_ref, out_ref, w_ref, o_ref, sems):
         for i in range(n_blk):
             w_ref[i : i + 1, :] = g_ref[i, capacity:, :].astype(jnp.float32)
         pieces = w_ref[...]
@@ -418,17 +439,31 @@
             exponent = exponent + pieces[:, k * capacity : (k + 1) * capacity]
         w_ref[:, :capacity] = jnp.where(v_ref[:, :capacity] > 0.0, jnp.exp(exponent), 0.0)
         turned = jnp.transpose(w_ref[...])
+        moves = []
         for i in range(n_blk):
             part = slice(i * capacity, (i + 1) * capacity)
             centre = g_ref[i, :capacity, :].astype(jnp.float32)
-            out_ref[0, i] = turned[:capacity, i : i + 1] * (t_ref[part, :] - centre)
+            o_ref[i] = turned[:capacity, i : i + 1] * (t_ref[part, :] - centre)
+            if (i + 1) % batch == 0:
+                first = i + 1 - batch
+                move = pltpu.make_async_copy(
+                    o_ref.at[pl.ds(first, batch)], out_ref.at[0, pl.ds(first, batch)], sems.at[len(moves)]
+                )
+                move.start()
+                moves.append(move)
+        for move in moves:
+            move.wait()
 
     return pl.pallas_call(
         kernel,
         out_shape=jax.ShapeDtypeStruct((1, n_blk, capacity, width), jnp.float32),
         in_specs=vmem(3),
-        out_specs=pl.BlockSpec(memory_space=pltpu.VMEM),
-        scratch_shapes=[pltpu.VMEM((n_blk, 128), jnp.float32)],
+        out_specs=pl.BlockSpec(memory_space=pltpu.HBM),
+        scratch_shapes=[
+            pltpu.VMEM((n_blk, 128), jnp.float32),
+            pltpu.VMEM((n_blk, capacity, width), jnp.float32),
+            pltpu.SemaphoreType.DMA((4,)),
+        ],
         compiler_params=params(4),
         name="finish",
     )(answers, rows, live)
@@ -450,13 +485,13 @@
     own_duals, duals, mass = column_pass(gathered, centroids, parts, kept, base, tok, scaling, slab * n_blk)
     both = lax.all_gather(mass, "wide", axis=0, axis_index_groups=pairs, tiled=True)
     mass = add_up(exchange(spread(both, n_wide // 2), "wide", same_core))
-    ids = unpack(parts, n_blk * tok, capacity)
-    centres = centroids[ids[2]]
+    ids, pick, here = unpack(parts, n_blk * tok, slab // 128, capacity)
+    centres = centroids[ids[0]]
     sums = ask_scores(gathered, centres, parts, duals, scaling)
     rows, live = prepare(tokens, row_ids[0], counts)
     mass, sums, rows, live = lax.optimization_barrier((mass, sums, rows, live))
     mass = lax.all_gather(mass, "wide", axis=0, axis_index_groups=pairs, tiled=True)
-    col_duals, answers = look_up(mass, ids, centres, sums, tok * n_blk * n_wide, n_blk, capacity)
+    col_duals, answers = look_up(mass, pick, here, centres, sums, tok * n_blk * n_wide, n_blk, capacity)
     residuals = finish(exchange(answers, "blk"), rows, live)
     return (own_duals.reshape(tok), col_duals.reshape(slab), residuals)
 

time: 107 us -> 107 us (level)
  no operation moved by 1% of the time
where the time goes in v8:
time: 107 us; the launch traced here: 106 us
  blocking collectives  49.3 us (46%)
  Pallas kernels  36 us (34%)
  starting transfers between devices  11.7 us (11%)
  waiting for transfers between devices  7.23 us (7%)
  local copies, waits for them, and re-layouts  1.36 us (1%)
    all_to_all x3, blocking collectives, exchange(): lax.all_to_all(x, axis, split_axis=0, concat_axis=0, axis_index_groups=gr...  41.4 us
    pallas_call x1, Pallas kernels, row_pass(): pl.pallas_call(kernel, out_shape=(jax.ShapeDtypeStruct((n_blk, 1, rows +...  15.6 us
    pallas_call x1, Pallas kernels, column_pass(): pl.pallas_call(kernel, out_shape=(jax.ShapeDtypeStruct((1, tok), jnp.floa...  13.2 us
    all_to_all x1, starting transfers between devices, exchange(): lax.all_to_all(x, axis, split_axis=0, concat_axis=0, axis_index_groups=gr...  11.7 us
    all_gather x2, blocking collectives, local(): lax.all_gather(mass, 'wide', axis=0, axis_index_groups=pairs, tiled=True)  7.89 us
    all_to_all x1, waiting for transfers between devices, exchange(): lax.all_to_all(x, axis, split_axis=0, concat_axis=0, axis_index_groups=gr...  7.23 us
    pallas_call x1, Pallas kernels, ask_scores(): pl.pallas_call(kernel, out_shape=jax.ShapeDtypeStruct((1, n_blk * capacit...  2.79 us
  transfers between devices with their start and end apart: 1, of which 1 were waited for; matrix products, arithmetic and copies ran while one was open for 1% of the time, Pallas kernels for 4%

profile of v8, /device:TPU:1, one launch (start us, length us, event | category | flops | bytes accessed | tf_op | source)
XLA Modules:
  0.0 106.4 jit_solution(18076768672548479087)
XLA Ops:
  0.6 0.0 copy-start
  0.6 0.0 copy-start.2
  0.7 0.0 copy-start.3
  0.7 0.9 stage.1
  1.6 18.6 %all_to_all.20.x_ref = bf16[16,48,128]{2,1,0:T(8,128)(2,1)S(1)} all-to-all(bf16[16,48,128]{2,1,0:T(8,128)(2,1)S(1)} %stage.1), channel_id=1, replica_groups=mesh['blk'=16,'wide'=32] {'blk'}, dimensions={0} | all-to-all | bytes 393216 | tf_op jit(solution)/shard_map/all_to_all | solution.py:25
  20.2 0.0 copy-done
  20.2 0.0 copy-done.2
  20.2 0.0 copy-done.3
  20.2 15.6 %row_pass.1 = (f32[16,1,896]{2,1,0:T(1,128)S(1)}, f32[768,8192]{1,0:T(8,128)S(1)}, f32[768,128]{1,0:T(8,128)S(1)}) custom-call(bf16[16,48,128]{2,1,0:T(8,128)(2,1)S(1)} %all_to_all.20.x_ref, bf16[8192,128]{1,0:T(8,128)(2,1)S(1)} %copy-done, s32[16,32]{1,0:T(8,128)S(1)} %bitcast.9, s32[16,32]{1,0:T(8,128)S(1)} %bitcast.7), custom_call_target="tpu_custom_call" | custom-call | tf_op jit(solution)/shard_map/row_pass/pallas_call | solution.py:131
  35.8 10.9 %all_to_all.21.l_ref.p_ref = f32[16,1,896]{2,1,0:T(1,128)S(1)} all-to-all(f32[16,1,896]{2,1,0:T(1,128)S(1)} %get-tuple-element.20), channel_id=1, replica_groups=mesh['blk'=16,'wide'=32] {'blk'}, dimensions={0} | all-to-all | bytes 114688 | tf_op jit(solution)/shard_map/all_to_all | solution.py:25
  46.7 0.0 copy-start.1
  46.7 0.0 copy-start.4
  46.7 13.2 %column_pass.1 = (f32[1,48]{1,0:T(1,128)}, f32[1,768]{1,0:T(1,128)S(1)}, f32[64,128]{1,0:T(8,128)S(1)}) custom-call(bf16[16,48,128]{2,1,0:T(8,128)(2,1)S(1)} %all_to_all.20.x_ref, bf16[8192,128]{1,0:T(8,128)(2,1)S(1)} %copy-done, f32[16,1,896]{2,1,0:T(1,128)S(1)} %all_to_all.21.l_ref.p_ref, f32[768,8192]{1,0:T(8,128)S(1)} %get-tuple-element.21.e_ref, ...), custom_call_target="tpu_custom_call" | custom-call | tf_op jit(solution)/shard_map/column_pass/pallas_call | solution.py:246
  59.9 4.8 %all_gather.6.p_ref = f32[128,128]{1,0:T(8,128)S(1)} all-gather(f32[64,128]{1,0:T(8,128)S(1)} %get-tuple-element.24), channel_id=1, replica_groups={{0,1},{2,3},{4,5},{6,7},{8,9},{10,11},{12,13},{14,15},{16,17},{18,19},{..., dimensions={0}, use_global_device_ids=true | all-gather | bytes 98304 | tf_op jit(solution)/shard_map/all_gather | solution.py:486
  64.7 0.7 spread.1
  65.4 11.7 %all-to-all-start.2 = ((f32[16,32,128]{2,1,0:T(8,128)}), f32[16,32,128]{2,1,0:T(8,128)S(1)}, u32[]{:S(2)}, u32[]{:S(2)}) async-start(f32[16,32,128]{2,1,0:T(8,128)} %spread.1), calls=%async_computation.2 | async-start | bytes 524288 | tf_op jit(solution)/shard_map/all_to_all | solution.py:25
  77.1 0.0 copy-done.1
  77.1 0.0 copy-done.4
  77.1 0.9 prepare.1
  78.1 0.1 unpack.1
  78.2 1.3 %gather_fusion = bf16[512,128]{1,0:T(8,128)(2,1)S(1)} fusion(bf16[8192,128]{1,0:T(8,128)(2,1)S(1)} %copy-done, s32[1024]{0:T(1024)S(1)} %pad_clamp_fusion), kind=kCustom, calls=%fused_computation | custom fusion | bytes 264192 | tf_op jit(solution)/shard_map/gather | solution.py:489
  79.6 2.8 %ask_scores.1.s_ref = f32[1,512]{1,0:T(1,128)S(1)} custom-call(bf16[16,48,128]{2,1,0:T(8,128)(2,1)S(1)} %all_to_all.20.x_ref, bf16[512,128]{1,0:T(8,128)(2,1)S(1)} %gather_fusion, f32[16,1,896]{2,1,0:T(1,128)S(1)} %all_to_all.21.l_ref.p_ref, f32[1,768]{1,0:T(1,128)S(1)} %get-tuple-element.26.d_ref), custom_call_target="tpu_custom_call" | custom-call | tf_op jit(solution)/shard_map/ask_scores/pallas_call | solution.py:348
  82.4 7.2 %all-to-all-done.2.p_ref = f32[16,32,128]{2,1,0:T(8,128)S(1)} async-done(((f32[16,32,128]{2,1,0:T(8,128)}), f32[16,32,128]{2,1,0:T(8,128)S(1)}, u32[]{:S(2)}, u32[]{:S(2)}) %all-to-all-start.2) | async-done | bytes 262176 | tf_op jit(solution)/shard_map/all_to_all | solution.py:25
  89.6 3.1 %all_gather.7.m_ref = f32[64,128]{1,0:T(8,128)S(1)} all-gather(f32[32,128]{1,0:T(8,128)S(1)} %add_up.1), channel_id=1, replica_groups={{0,1},{2,3},{4,5},{6,7},{8,9},{10,11},{12,13},{14,15},{16,17},{18,19},{..., dimensions={0}, use_global_device_ids=true | all-gather | bytes 49152 | tf_op jit(solution)/shard_map/all_gather | solution.py:493
  92.7 0.6 look_up.1
  93.4 12.0 %all_to_all.22.g_ref = bf16[16,33,128]{2,1,0:T(8,128)(2,1)S(1)} all-to-all(bf16[16,33,128]{2,1,0:T(8,128)(2,1)S(1)} %get-tuple-element.34), channel_id=1, replica_groups=mesh['blk'=16,'wide'=32] {'blk'}, dimensions={0} | all-to-all | bytes 270336 | tf_op jit(solution)/shard_map/all_to_all | solution.py:25
  105.3 1.0 finish.1
  (3 shorter events, 0.0 us)
Async XLA Ops:
  0.6 19.6 %copy-start = (bf16[8192,128]{1,0:T(8,128)(2,1)S(1)}, bf16[8192,128]{1,0:T(8,128)(2,1)}, u32[]{:S(2)}) copy-start(bf16[8192,128]{1,0:T(8,128)(2,1)} %c_ref.5) | copy-start | bytes 6291460
  0.6 19.5 %copy-start.2 = (s32[1,16,32]{2,1,0:T(8,128)S(1)}, s32[1,16,32]{2,1,0:T(8,128)}, u32[]{:S(2)}) copy-start(s32[1,16,32]{2,1,0:T(8,128)} %param.7) | copy-start | bytes 6148
  0.7 19.5 %copy-start.3 = (s32[1,16,32]{2,1,0:T(8,128)S(1)}, s32[1,16,32]{2,1,0:T(8,128)}, u32[]{:S(2)}) copy-start(s32[1,16,32]{2,1,0:T(8,128)} %param.8) | copy-start | bytes 6148
  46.7 30.4 %copy-start.1 = (bf16[48,128]{1,0:T(8,128)(2,1)S(1)}, bf16[48,128]{1,0:T(8,128)(2,1)}, u32[]{:S(2)}) copy-start(bf16[48,128]{1,0:T(8,128)(2,1)} %t_ref.3) | copy-start | bytes 36868
  46.7 30.4 %copy-start.4 = (s32[1,16]{1,0:T(1,128)S(1)}, s32[1,16]{1,0:T(1,128)}, u32[]{:S(2)}) copy-start(s32[1,16]{1,0:T(1,128)} %n_ref.1) | copy-start | bytes 196
  65.4 24.2 %all-to-all-start.2 = ((f32[16,32,128]{2,1,0:T(8,128)}), f32[16,32,128]{2,1,0:T(8,128)S(1)}, u32[]{:S(2)}, u32[]{:S(2)}) async-start(f32[16,32,128]{2,1,0:T(8,128)} %spread.1), calls=%async_computation.2 | async-start | bytes 524288 | tf_op jit(solution)/shard_map/all_to_all | solution.py:25

commit v9 on v7

--- a/solution.py
+++ b/solution.py
@@ -124,14 +124,15 @@
         line = jnp.concatenate(
             [ids >> 7, ids & 127, r_ref[...], jnp.zeros((n_blk, 128 - 3 * capacity), jnp.int32)], axis=1
         ).astype(jnp.float32)
-        for i in range(n_blk):
-            out_ref[i, :, :rows] = lse
-            out_ref[i, :, rows:] = line[i : i + 1, :]
+        groups = [lse[:, g : g + 128] for g in range(0, rows, 128)]
+        blank = jnp.zeros((8 - len(groups) - 1, 128), jnp.float32)
+        for i in range(n_blk):
+            out_ref[i] = jnp.concatenate(groups + [line[i : i + 1, :], blank], axis=0)
 
     return pl.pallas_call(
         kernel,
         out_shape=(
-            jax.ShapeDtypeStruct((n_blk, 1, rows + 128), jnp.float32),
+            jax.ShapeDtypeStruct((n_blk, 8, 128), jnp.float32),
             pltpu.VMEM((rows, slab), jnp.float32),
             pltpu.VMEM((rows, 128), jnp.float32),
         ),
@@ -154,7 +155,7 @@
 
     def kernel(p_ref, ids_ref):
         for i in range(n_blk):
-            line = p_ref[i, :, rows:].astype(jnp.int32)
+            line = p_ref[i, rows // 128 : rows // 128 + 1, :].astype(jnp.int32)
             part = slice(i * capacity, (i + 1) * capacity)
             ids_ref[0:1, part] = line[:, :capacity]
             ids_ref[1:2, part] = line[:, capacity : 2 * capacity]
@@ -181,11 +182,13 @@
     stride = math.gcd(rows, 256)
 
     def kernel(x_ref, c_ref, l_ref, e_ref, b_ref, own_ref, dual_ref, mass_ref, t_ref, d_ref, w_ref):
-        lse = l_ref[:, 0, :rows]
-        top = jnp.max(lse, axis=0, keepdims=True)
-        total = jnp.sum(jnp.exp(lse - top), axis=0, keepdims=True)
-        dual = math.log(all_cols) - (top + jnp.log(total))
-        dual_ref[...] = dual
+        lse = l_ref[...]
+        top = jnp.max(lse, axis=0)
+        total = jnp.sum(jnp.exp(lse - top[None]), axis=0)
+        parts_of = math.log(all_cols) - (top + jnp.log(total))
+        for g in range(rows // 128):
+            dual_ref[:, g * 128 : (g + 1) * 128] = parts_of[g : g + 1, :]
+        dual = dual_ref[...]
         position = lax.axis_index("blk")
         own = jnp.zeros((1, tok), jnp.float32)
         for i in range(n_blk):
@@ -303,7 +306,7 @@
 
     def kernel(x_ref, c_ref, p_ref, d_ref, out_ref, w_ref):
         for i in range(n_blk):
-            w_ref[i : i + 1, :] = p_ref[i, :, rows:]
+            w_ref[i : i + 1, :] = p_ref[i, rows // 128 : rows // 128 + 1, :]
         turned = jnp.transpose(w_ref[...])[2 * capacity : 3 * capacity, :]
         row = lax.broadcasted_iota(jnp.int32, (capacity, tok), 1).astype(jnp.float32)
         lane = lax.broadcasted_iota(jnp.int32, (capacity, 128), 1)

time: 107 us -> 107 us (level)
  no operation moved by 1% of the time
where the time goes in v9:
time: 107 us
  blocking collectives  49.4 us (46%)
  Pallas kernels  36.1 us (34%)
  starting transfers between devices  11.7 us (11%)
  waiting for transfers between devices  7.22 us (7%)
  local copies, waits for them, and re-layouts  1.36 us (1%)
    all_to_all x3, blocking collectives, exchange(): lax.all_to_all(x, axis, split_axis=0, concat_axis=0, axis_index_groups=gr...  41.5 us
    pallas_call x1, Pallas kernels, row_pass(): pl.pallas_call(kernel, out_shape=(jax.ShapeDtypeStruct((n_blk, 8, 128), j...  15.7 us
    pallas_call x1, Pallas kernels, column_pass(): pl.pallas_call(kernel, out_shape=(jax.ShapeDtypeStruct((1, tok), jnp.floa...  13.2 us
    all_to_all x1, starting transfers between devices, exchange(): lax.all_to_all(x, axis, split_axis=0, concat_axis=0, axis_index_groups=gr...  11.7 us
    all_gather x2, blocking collectives, local(): lax.all_gather(mass, 'wide', axis=0, axis_index_groups=pairs, tiled=True)  7.93 us
    all_to_all x1, waiting for transfers between devices, exchange(): lax.all_to_all(x, axis, split_axis=0, concat_axis=0, axis_index_groups=gr...  7.22 us
    pallas_call x1, Pallas kernels, ask_scores(): pl.pallas_call(kernel, out_shape=jax.ShapeDtypeStruct((1, n_blk * capacit...  2.79 us
  transfers between devices with their start and end apart: 1, of which 1 were waited for; matrix products, arithmetic and copies ran while one was open for 1% of the time, Pallas kernels for 4%

profile of v9, /device:TPU:1, one launch (start us, length us, event | category | flops | bytes accessed | tf_op | source)
XLA Modules:
  0.0 106.5 jit_solution(9165768434978413416)
XLA Ops:
  0.6 0.0 copy-start
  0.6 0.0 copy-start.2
  0.7 0.0 copy-start.3
  0.7 0.9 stage.1
  1.6 18.6 %all_to_all.20.x_ref = bf16[16,48,128]{2,1,0:T(8,128)(2,1)S(1)} all-to-all(bf16[16,48,128]{2,1,0:T(8,128)(2,1)S(1)} %stage.1), channel_id=1, replica_groups=mesh['blk'=16,'wide'=32] {'blk'}, dimensions={0} | all-to-all | bytes 393216 | tf_op jit(solution)/shard_map/all_to_all | solution.py:25
  20.2 0.0 copy-done
  20.2 0.0 copy-done.2
  20.2 0.0 copy-done.3
  20.2 15.7 %row_pass.1 = (f32[16,8,128]{2,1,0:T(8,128)S(1)}, f32[768,8192]{1,0:T(8,128)S(1)}, f32[768,128]{1,0:T(8,128)S(1)}) custom-call(bf16[16,48,128]{2,1,0:T(8,128)(2,1)S(1)} %all_to_all.20.x_ref, bf16[8192,128]{1,0:T(8,128)(2,1)S(1)} %copy-done, s32[16,32]{1,0:T(8,128)S(1)} %bitcast.11, s32[16,32]{1,0:T(8,128)S(1)} %bitcast.9), custom_call_target="tpu_custom_call" | custom-call | tf_op jit(solution)/shard_map/row_pass/pallas_call | solution.py:132
  35.9 10.9 %all_to_all.21.l_ref.p_ref = f32[16,8,128]{2,1,0:T(8,128)S(1)} all-to-all(f32[16,8,128]{2,1,0:T(8,128)S(1)} %get-tuple-element.17), channel_id=1, replica_groups=mesh['blk'=16,'wide'=32] {'blk'}, dimensions={0} | all-to-all | bytes 131072 | tf_op jit(solution)/shard_map/all_to_all | solution.py:25
  46.8 0.0 copy-start.1
  46.8 0.0 copy-start.4
  46.8 13.2 %column_pass.1 = (f32[1,48]{1,0:T(1,128)}, f32[1,768]{1,0:T(1,128)S(1)}, f32[64,128]{1,0:T(8,128)S(1)}) custom-call(bf16[16,48,128]{2,1,0:T(8,128)(2,1)S(1)} %all_to_all.20.x_ref, bf16[8192,128]{1,0:T(8,128)(2,1)S(1)} %copy-done, f32[16,8,128]{2,1,0:T(8,128)S(1)} %all_to_all.21.l_ref.p_ref, f32[768,8192]{1,0:T(8,128)S(1)} %get-tuple-element.18.e_ref, ...), custom_call_target="tpu_custom_call" | custom-call | tf_op jit(solution)/shard_map/column_pass/pallas_call | solution.py:239
  60.0 4.8 %all_gather.6.p_ref = f32[128,128]{1,0:T(8,128)S(1)} all-gather(f32[64,128]{1,0:T(8,128)S(1)} %get-tuple-element.21), channel_id=1, replica_groups={{0,1},{2,3},{4,5},{6,7},{8,9},{10,11},{12,13},{14,15},{16,17},{18,19},{..., dimensions={0}, use_global_device_ids=true | all-gather | bytes 98304 | tf_op jit(solution)/shard_map/all_gather | solution.py:454
  64.9 0.7 spread.1
  65.6 11.7 %all-to-all-start.2 = ((f32[16,32,128]{2,1,0:T(8,128)}), f32[16,32,128]{2,1,0:T(8,128)S(1)}, u32[]{:S(2)}, u32[]{:S(2)}) async-start(f32[16,32,128]{2,1,0:T(8,128)} %spread.1), calls=%async_computation.2 | async-start | bytes 524288 | tf_op jit(solution)/shard_map/all_to_all | solution.py:25
  77.3 0.0 copy-done.1
  77.3 0.0 copy-done.4
  77.3 0.9 prepare.1
  78.2 0.2 unpack.1.i_ref
  78.4 1.3 %gather_fusion = bf16[512,128]{1,0:T(8,128)(2,1)S(1)} fusion(bf16[8192,128]{1,0:T(8,128)(2,1)S(1)} %copy-done, s32[1024]{0:T(1024)S(1)} %pad_clamp_fusion), kind=kCustom, calls=%fused_computation | custom fusion | bytes 264192 | tf_op jit(solution)/shard_map/gather | solution.py:457
  79.8 2.8 %ask_scores.1.s_ref = f32[1,512]{1,0:T(1,128)S(1)} custom-call(bf16[16,48,128]{2,1,0:T(8,128)(2,1)S(1)} %all_to_all.20.x_ref, bf16[512,128]{1,0:T(8,128)(2,1)S(1)} %gather_fusion, f32[16,8,128]{2,1,0:T(8,128)S(1)} %all_to_all.21.l_ref.p_ref, f32[1,768]{1,0:T(1,128)S(1)} %get-tuple-element.22.d_ref), custom_call_target="tpu_custom_call" | custom-call | tf_op jit(solution)/shard_map/ask_scores/pallas_call | solution.py:328
  82.6 7.2 %all-to-all-done.2.p_ref = f32[16,32,128]{2,1,0:T(8,128)S(1)} async-done(((f32[16,32,128]{2,1,0:T(8,128)}), f32[16,32,128]{2,1,0:T(8,128)S(1)}, u32[]{:S(2)}, u32[]{:S(2)}) %all-to-all-start.2) | async-done | bytes 262176 | tf_op jit(solution)/shard_map/all_to_all | solution.py:25
  89.8 3.1 %all_gather.7.m_ref = f32[64,128]{1,0:T(8,128)S(1)} all-gather(f32[32,128]{1,0:T(8,128)S(1)} %add_up.1), channel_id=1, replica_groups={{0,1},{2,3},{4,5},{6,7},{8,9},{10,11},{12,13},{14,15},{16,17},{18,19},{..., dimensions={0}, use_global_device_ids=true | all-gather | bytes 49152 | tf_op jit(solution)/shard_map/all_gather | solution.py:461
  92.9 0.6 look_up.1
  93.5 12.0 %all_to_all.22.g_ref = bf16[16,33,128]{2,1,0:T(8,128)(2,1)S(1)} all-to-all(bf16[16,33,128]{2,1,0:T(8,128)(2,1)S(1)} %get-tuple-element.28), channel_id=1, replica_groups=mesh['blk'=16,'wide'=32] {'blk'}, dimensions={0} | all-to-all | bytes 270336 | tf_op jit(solution)/shard_map/all_to_all | solution.py:25
  105.5 1.0 finish.1
  (3 shorter events, 0.0 us)
Async XLA Ops:
  0.6 19.6 %copy-start = (bf16[8192,128]{1,0:T(8,128)(2,1)S(1)}, bf16[8192,128]{1,0:T(8,128)(2,1)}, u32[]{:S(2)}) copy-start(bf16[8192,128]{1,0:T(8,128)(2,1)} %c_ref.5) | copy-start | bytes 6291460
  0.6 19.5 %copy-start.2 = (s32[1,16,32]{2,1,0:T(8,128)S(1)}, s32[1,16,32]{2,1,0:T(8,128)}, u32[]{:S(2)}) copy-start(s32[1,16,32]{2,1,0:T(8,128)} %param.7) | copy-start | bytes 6148
  0.7 19.5 %copy-start.3 = (s32[1,16,32]{2,1,0:T(8,128)S(1)}, s32[1,16,32]{2,1,0:T(8,128)}, u32[]{:S(2)}) copy-start(s32[1,16,32]{2,1,0:T(8,128)} %param.8) | copy-start | bytes 6148
  46.8 30.4 %copy-start.1 = (bf16[48,128]{1,0:T(8,128)(2,1)S(1)}, bf16[48,128]{1,0:T(8,128)(2,1)}, u32[]{:S(2)}) copy-start(bf16[48,128]{1,0:T(8,128)(2,1)} %t_ref.3) | copy-start | bytes 36868
  46.8 30.5 %copy-start.4 = (s32[1,16]{1,0:T(1,128)S(1)}, s32[1,16]{1,0:T(1,128)}, u32[]{:S(2)}) copy-start(s32[1,16]{1,0:T(1,128)} %n_ref.1) | copy-start | bytes 196
  65.6 24.2 %all-to-all-start.2 = ((f32[16,32,128]{2,1,0:T(8,128)}), f32[16,32,128]{2,1,0:T(8,128)S(1)}, u32[]{:S(2)}, u32[]{:S(2)}) async-start(f32[16,32,128]{2,1,0:T(8,128)} %spread.1), calls=%async_computation.2 | async-start | bytes 524288 | tf_op jit(solution)/shard_map/all_to_all | solution.py:25
